TPU v7x, 512 devices: a whole 4x4x16 slice. The times are simulated.
512 devices in a mesh: dp: 64 (over z, y), section: 2 (over core), mp: 4 (over x).
Axes of the slice: x: 4, y: 4, z: 16, core: 2. Of those that a mesh axis runs over, the one named last changes fastest.
Arguments:
- frames: bfloat16 [64, 128, 512], P('dp'), may hold values from -6 to 6
- lengths: int32 [64], P('dp'), may hold values from 32 to 128
- feature_proj: bfloat16 [512, 1920], P(None, 'mp'), may hold values from -0.25 to 0.25
- norm_gain: float32 [2, 1920], P('section'), may hold values from 0.25 to 1.75
- qkv_weight: bfloat16 [2, 1920, 5760], P('section', 'dp', 'mp'), may hold values from -0.125 to 0.125
- out_weight: bfloat16 [2, 1920, 1920], P('section', 'mp', 'dp'), may hold values from -0.125 to 0.125
- center: float32 [1920], replicated, may hold values from -4 to 4
- whitening: float32 [1920, 1024], P(None, 'dp'), may hold values from -0.125 to 0.125
Outputs:
- embeddings: float32 [64, 1024], P(None, 'dp')
All inputs are finite; a program needn't handle non-finite values.
Results may differ from a plain program's by a relative error of at most 0.0095.
Values may be sent and summed in bfloat16 or wider, within the bound.
No kernel may reach another device: no remote copies, remote signals or barrier semaphores. Data moves between devices by JAX's collectives and lax.ppermute only.
A program may use at most 64 MiB of HBM per device.

v0:
```python
import jax
import jax.numpy as jnp
from jax import lax
from jax.sharding import PartitionSpec as P

HD = 120


def passed_along(x, axis, by):
    count = lax.axis_size(axis)
    pairs = [(i, i + by) for i in range(count) if 0 <= i + by < count]
    return lax.ppermute(x, axis, pairs)


def broadcast(value, axis, source):
    kept = jnp.where(lax.axis_index(axis) == source, value, 0).astype(value.dtype)
    return lax.psum(kept, axis)


def layer_norm(values, gain):
    mean = jnp.mean(values, axis=-1, keepdims=True)
    centered = values - mean
    var = jnp.mean(centered * centered, axis=-1, keepdims=True)
    return centered * lax.rsqrt(var + 1e-05) * gain


def body(frames, lengths, feature_proj, norm_gain, qkv_weight, out_weight, center, whitening):
    section_index = lax.axis_index("section")
    gain = norm_gain[0]
    qkv_local = qkv_weight[0]
    out_local = out_weight[0]
    count_utt = frames.shape[0]
    frames_count = frames.shape[1]
    width = gain.shape[0]
    qkv_cols = qkv_local.shape[1]
    heads_local = qkv_cols // (3 * HD)
    full_qkv, full_out = (
        lax.all_gather(qkv_local, "dp", axis=0, tiled=True),
        lax.all_gather(out_local, "dp", axis=1, tiled=True),
    )
    received = jnp.zeros((frames_count, width), jnp.bfloat16)
    pooled_rows = []
    frame_ids = jnp.arange(frames_count, dtype=jnp.int32)
    for step in range(count_utt + 1):
        first_mb = min(step, count_utt - 1)
        second_mb = max(step - 1, 0)
        projected_part = jnp.dot(
            frames[first_mb], feature_proj, preferred_element_type=jnp.float32
        ).astype(jnp.bfloat16)
        projected = lax.all_gather(projected_part, "mp", axis=1, tiled=True)
        first_section = section_index == 0
        layer_input = jnp.where(first_section, projected, received)
        length = jnp.where(first_section, lengths[first_mb], lengths[second_mb])
        normed = layer_norm(layer_input.astype(jnp.float32), gain).astype(jnp.bfloat16)
        qkv_sum = jnp.dot(normed, full_qkv, preferred_element_type=jnp.float32)
        qkv = qkv_sum.astype(jnp.bfloat16).reshape(frames_count, 3, heads_local, HD)
        query = qkv[:, 0]
        keys = qkv[:, 1]
        values = qkv[:, 2]
        scores = jnp.einsum(
            "qhd,khd->hqk", query, keys, preferred_element_type=jnp.float32
        ) / jnp.sqrt(jnp.float32(HD))
        attention_valid = jnp.arange(frames_count, dtype=jnp.int32) < length
        scores = jnp.where(attention_valid[None, None, :], scores, jnp.float32(-1e30))
        probs = jax.nn.softmax(scores, axis=-1).astype(jnp.bfloat16)
        context = jnp.einsum(
            "hqk,khd->qhd", probs, values, preferred_element_type=jnp.float32
        ).astype(jnp.bfloat16)
        context = context.reshape(frames_count, heads_local * HD)
        partial_out = jnp.dot(context, full_out, preferred_element_type=jnp.float32)
        attended = lax.psum(partial_out.astype(jnp.bfloat16), "mp").astype(jnp.float32)
        result = (layer_input.astype(jnp.float32) + attended).astype(jnp.bfloat16)
        if step >= 1:
            valid = frame_ids < lengths[step - 1]
            summed = jnp.sum(
                jnp.where(valid[:, None], result.astype(jnp.float32), jnp.float32(0.0)), axis=0
            )
            pooled_rows.append(summed / lengths[step - 1].astype(jnp.float32))
        if step < count_utt:
            received = passed_along(result, "section", 1)
    pooled = jnp.stack(pooled_rows, axis=0)
    pooled = broadcast(pooled, "section", 1)
    return jnp.dot(
        lax.all_gather(pooled, "dp", axis=0, tiled=True) - center,
        whitening,
        precision=lax.Precision.HIGHEST,
        preferred_element_type=jnp.float32,
    )


def solution(mesh):
    in_specs = (
        P("dp", None, None),
        P("dp"),
        P(None, "mp"),
        P("section", None),
        P("section", "dp", "mp"),
        P("section", "mp", "dp"),
        P(),
        P(None, "dp"),
    )
    out_specs = P(None, "dp")
    return jax.shard_map(body, mesh=mesh, in_specs=in_specs, out_specs=out_specs, check_vma=False)
```

profile of v0, /device:TPU:6, one launch (start us, length us, event | category | flops | bytes accessed | tf_op | source)
XLA Modules:
  0.0 595.7 jit_solution(13150222934486986474)
XLA Ops:
  6.5 1.5 copy.22
  8.1 1.7 copy.19
  10.5 0.7 reduce
  11.3 1.2 convolution_convert_fusion.2
  12.5 15.4 %all_gather.13 = bf16[128,1920]{0,1:T(8,128)(2,1)S(1)} all-gather(bf16[128,480]{0,1:T(8,128)(2,1)S(1)} %convolution_convert_fusion.2), channel_id=1, replica_groups=mesh['dp'=64,'section'=2,'mp'=4] {'mp'}, dimensions={1}, use_global_device_ids=true | all-gather | bytes 614400 | tf_op jit(solution)/shard_map/all_gather | solution.py:50
  27.8 0.3 convert_reduce_fusion.1
  28.1 0.3 fusion.27
  28.4 132.7 %all-gather.8.cloned.1.call-done = bf16[1,480,1920]{1,0,2:T(2,128)(2,1)} async-done(((bf16[1,480,30]{1,0,2:T(2,128)(2,1)}), bf16[1,480,1920]{1,0,2:T(2,128)(2,1)}) %all-gather.8.cloned.1.call-update) | async-done | bytes 1843216 | tf_op jit(solution)/shard_map/all_gather | solution.py:39
  161.1 7.6 %copy.23 = bf16[1,480,1920]{2,1,0:T(8,128)(2,1)S(1)} copy(bf16[1,480,1920]{1,0,2:T(2,128)(2,1)} %all-gather.8.cloned.1.call-done) | data formatting | bytes 3686400 | tf_op jit(solution)/shard_map/all_gather | solution.py:39
  168.7 157.5 %all-gather.6.cloned.1.call-done = bf16[1,1920,1440]{2,0,1:T(2,128)(2,1)} async-done(((bf16[1,30,1440]{2,0,1:T(2,128)(2,1)}), bf16[1,1920,1440]{2,0,1:T(2,128)(2,1)}) %all-gather.6.cloned.1.call-update) | async-done | bytes 5529616 | tf_op jit(solution)/shard_map/all_gather | solution.py:38
  326.1 23.4 %copy.20 = bf16[1,1920,1440]{1,2,0:T(8,128)(2,1)} copy(bf16[1,1920,1440]{2,0,1:T(2,128)(2,1)} %all-gather.6.cloned.1.call-done) | data formatting | bytes 11059200 | tf_op jit(solution)/shard_map/all_gather | solution.py:38
  349.5 4.3 fusion.9
  353.8 0.3 fusion.54
  354.4 0.9 convolution_convert_fusion.4
  355.3 2.6 convolution_convert_fusion.1
  357.9 51.6 %all-reduce.3.cloned.1.call-done = bf16[128,1920]{0,1:T(8,128)(2,1)} async-done(((bf16[128,1920]{0,1:T(8,128)(2,1)}), bf16[128,1920]{0,1:T(8,128)(2,1)}) %all-reduce.3.cloned.1.call-update) | async-done | bytes 491536 | tf_op jit(solution)/shard_map/psum | solution.py:71
  409.5 1.2 fusion.30
  410.7 1.3 collective-permute-start
  412.1 1.4 collective-permute-done
  413.5 0.3 convert_reduce_fusion
  413.8 0.3 fusion.24
  414.1 4.3 fusion.6
  418.4 0.7 copy-done.1
  419.1 0.3 fusion.55
  419.4 1.2 fusion.16
  420.6 1.1 convolution_convert_fusion.3
  421.8 1.7 convolution_convert_fusion
  423.5 59.0 %all-reduce.5.cloned.1.call-done = bf16[128,1920]{0,1:T(8,128)(2,1)} async-done(((bf16[128,1920]{0,1:T(8,128)(2,1)}), bf16[128,1920]{0,1:T(8,128)(2,1)}) %all-reduce.5.cloned.1.call-update) | async-done | bytes 491536 | tf_op jit(solution)/shard_map/psum | solution.py:71
  482.5 1.4 select_reduce_fusion
  484.0 2.5 psum.23
  486.4 101.5 %all-gather.2 = f32[64,1,1920]{2,1,0:T(1,128)S(1)} all-gather(f32[1,1,1920]{2,1,0:T(1,128)S(1)} %bitcast.80), channel_id=1, replica_groups=mesh['dp'=64,'section'=2,'mp'=4] {'dp'}, dimensions={0}, use_global_device_ids=true | all-gather | bytes 499200 | tf_op jit(solution)/shard_map/all_gather | solution.py:84
  588.0 1.1 fusion.34
  (23 shorter events, 0.5 us)
Async XLA Ops:
  6.5 4.7 copy-start
  6.5 154.5 %all-gather.8.cloned.1.call-start = ((), (), s32[]{:S(2)}) async-start(), calls=%async_computation.3 | async-start | bytes 3993600 | tf_op jit(solution)/shard_map/all_gather | solution.py:39
  8.0 318.1 %all-gather.6.cloned.1.call-start = ((), (), s32[]{:S(2)}) async-start(), calls=%async_computation.2 | async-start | bytes 11980800 | tf_op jit(solution)/shard_map/all_gather | solution.py:38
  9.8 399.7 %all-reduce.3.cloned.1.call-start = ((), (), s32[]{:S(2)}) async-start(), calls=%async_computation | async-start | bytes 983040 | tf_op jit(solution)/shard_map/psum | solution.py:71
  357.9 124.7 %all-reduce.5.cloned.1.call-start = ((), (), s32[]{:S(2)}) async-start(), calls=%async_computation.1 | async-start | bytes 983040 | tf_op jit(solution)/shard_map/psum | solution.py:71
  410.7 2.8 collective-permute-start
  414.1 173.9 %copy-start.2 = (f32[1920,16]{0,1:T(8,128)S(1)}, f32[1920,16]{0,1:T(8,128)}, u32[]{:S(2)}) copy-start(f32[1920,16]{0,1:T(8,128)} %param.15) | copy-start | bytes 368644
  414.1 173.9 %copy-start.3 = (f32[1920]{0:T(1024)S(1)}, f32[1920]{0:T(1024)}, u32[]{:S(2)}) copy-start(f32[1920]{0:T(1024)} %param.14) | copy-start | bytes 23044
  418.4 0.7 copy-start.1
Sparse Core Ops, SparseCore 0:
  10.3 150.7 all-gather.7
  164.0 162.0 all-gather.5
  358.0 51.4 all-reduce.2
  423.6 58.8 all-reduce.4
where the time goes:
time: 597 us; the launch traced here: 596 us
  waiting for transfers between devices  402 us (67%)
  blocking collectives  119 us (20%)
  local copies, waits for them, and re-layouts  34.9 us (6%)
  matrix products  19.3 us (3%)
  between operations  13.9 us (2%)
    all_gather x1, waiting for transfers between devices, body(): lax.all_gather(qkv_local, 'dp', axis=0, tiled=True)  157 us
    all_gather x1, waiting for transfers between devices, body(): lax.all_gather(out_local, 'dp', axis=1, tiled=True)  133 us
    psum x2, waiting for transfers between devices, body(): lax.psum(partial_out.astype(jnp.bfloat16), 'mp').astype(jnp.float32)  111 us
    all_gather x1, blocking collectives, body(): lax.all_gather(pooled, 'dp', axis=0, tiled=True) - center  102 us
    all_gather x1, local copies, waits for them, and re-layouts, body(): lax.all_gather(qkv_local, 'dp', axis=0, tiled=True)  23.4 us
    all_gather x1, blocking collectives, body(): projected = lax.all_gather(projected_part, 'mp', axis=1, tiled=True)  15.4 us
  transfers between devices with their start and end apart: 5, of which 5 were waited for; matrix products, arithmetic and copies ran while one was open for 2% of the time, Pallas kernels for 0%

commit v1 on v0

v1 whole, which is shorter than its diff:
```python
import jax
import jax.numpy as jnp
from jax import lax
from jax.sharding import Mesh, PartitionSpec as P

HD = 120
NY = 4
BF = jnp.bfloat16
F32 = jnp.float32


def plane_gather(block):
    count = lax.axis_size("x") * lax.axis_size("y")
    spread = jnp.broadcast_to(block[None], (count,) + block.shape)
    return lax.all_to_all(spread, ("x", "y"), 0, 0)


def swap_cores(value):
    return lax.ppermute(value, "c", [(0, 1), (1, 0)])


def normalized(chunks, gain):
    values = chunks.astype(F32)
    width = values.shape[0] * values.shape[2]
    mean = jnp.sum(values, axis=(0, 2), keepdims=True) / width
    centered = values - mean
    var = jnp.sum(centered * centered, axis=(0, 2), keepdims=True) / width
    return (centered * lax.rsqrt(var + 1e-05) * gain[:, None, :]).astype(BF)


def head_probs(normed, q_weight, k_weight, v_weight, valid):
    def project(weight):
        return jnp.einsum(
            "btk,bkn->tn", normed, weight, preferred_element_type=F32
        ).astype(BF).reshape(2, 128, HD)

    query, keys, values = project(q_weight), project(k_weight), project(v_weight)
    scores = jnp.einsum("uqd,ukd->uqk", query, keys, preferred_element_type=F32)
    scores = scores / jnp.sqrt(F32(HD))
    scores = jnp.where(valid[:, None, :], scores, F32(-1e30))
    return jax.nn.softmax(scores, axis=-1).astype(BF), values


def body(frames, lengths, feature_proj, norm_gain, qkv_weight, out_weight, center, whitening):
    core = lax.axis_index("c")
    chunk = lax.axis_index("x") * NY + lax.axis_index("y")
    half = frames.shape[1] // 2

    qkv = qkv_weight[0].reshape(30, 3, NY, HD).transpose(2, 1, 0, 3)
    out = out_weight[0].T.reshape(30, NY, HD).transpose(1, 0, 2)[:, None]
    mats = jnp.concatenate([qkv, out], axis=1)
    tail = jnp.broadcast_to(lengths[0].astype(BF), (NY, 4, 2, HD))
    mats = jnp.concatenate([mats, tail], axis=2).reshape(2 * NY, 2, 32, HD)
    regrouped = lax.all_to_all(mats, ("y", "c"), 0, 0).reshape(NY, 2, 2, 32, HD)
    plane_lengths = regrouped[:, 0, 0, 30, 0].astype(jnp.int32)

    def layer_weights(layer):
        shard = regrouped[:, layer, :, :30].transpose(1, 0, 2, 3).reshape(2, HD, HD)
        shard = jnp.pad(shard, ((0, 0), (0, 8), (0, 8)))
        return lax.all_gather(shard, "z", axis=0)

    halves = [layer_weights(0), layer_weights(1)]

    def both_halves(own):
        own = own[:, :, :HD, :HD]
        other = swap_cores(own)
        first = jnp.where(core == 0, own, other)
        second = jnp.where(core == 0, other, own)
        return first[:, 0], first[:, 1], second[:, 0], second[:, 1]

    own_half = lax.dynamic_slice_in_dim(frames[0], core * half, half, 0)
    projected = jnp.dot(own_half, feature_proj, preferred_element_type=F32).astype(BF)
    projected = projected.reshape(half, NY, HD).transpose(1, 0, 2)
    plane = plane_gather(projected).reshape(4, NY, NY, half, HD)
    plane = plane.transpose(1, 0, 2, 3, 4).reshape(NY, 16, half, HD)
    mine = lax.dynamic_slice_in_dim(plane, 2 * core, 2, 0)
    theirs = lax.dynamic_slice_in_dim(plane, 2 * (1 - core), 2, 0)
    theirs = swap_cores(theirs)
    x0 = jnp.stack([mine, theirs], axis=1).transpose(2, 0, 1, 3, 4).reshape(16, 256, HD)

    gains = lax.all_gather(norm_gain[0], "c", axis=0).reshape(2, 16, HD)
    frame_ids = jnp.concatenate(
        [core * half + jnp.arange(half), (1 - core) * half + jnp.arange(half)]
    )
    my_lengths = lax.dynamic_slice_in_dim(plane_lengths, 2 * core, 2, 0)
    valid = frame_ids[None, :] < my_lengths[:, None]
    share = valid.astype(F32) / my_lengths.astype(F32)[:, None]

    white_cols = lax.all_gather(whitening.T, "y", axis=0, tiled=True).reshape(64, 16, HD)

    q_w, k_w, v_w, o_w = both_halves(halves[0])
    probs, values = head_probs(normalized(x0, gains[0]), q_w, k_w, v_w, valid)
    context = jnp.einsum("uqk,ukd->uqd", probs, values, preferred_element_type=F32)
    context = context.astype(BF).reshape(256, HD)
    partial = jnp.einsum("tr,bcr->btc", context, o_w, preferred_element_type=F32).astype(BF)
    partial = lax.all_to_all(partial, ("x", "y"), 0, 0)
    attended = jnp.sum(partial.astype(F32), axis=0)
    x0_own = lax.dynamic_index_in_dim(x0, chunk, 0, keepdims=False)
    x1_own = (x0_own.astype(F32) + attended).astype(BF)
    x1 = plane_gather(x1_own)

    q_w, k_w, v_w, o_w = both_halves(halves[1])
    probs, values = head_probs(normalized(x1, gains[1]), q_w, k_w, v_w, valid)
    context = jnp.einsum("uqk,ukd->uqd", probs, values, preferred_element_type=F32).astype(BF)
    pooled_context = jnp.sum(context.astype(F32) * share[:, :, None], axis=1)
    pooled_x1 = jnp.sum(x1_own.reshape(2, 128, HD).astype(F32) * share[:, :, None], axis=1)
    out_white = jnp.einsum(
        "nbc,bcr->nr", white_cols, o_w.astype(F32), precision=lax.Precision.HIGHEST
    )
    white_own = lax.dynamic_index_in_dim(white_cols, chunk, 1, keepdims=False)
    center_own = lax.dynamic_index_in_dim(center.reshape(16, HD), chunk, 0, keepdims=False)
    packed = jnp.concatenate([pooled_context, pooled_x1 - center_own], axis=1)
    packed = jnp.broadcast_to(packed[None], (16,) + packed.shape)
    packed = lax.all_to_all(packed, "z", 0, 0).reshape(32, 2 * HD)
    mixed = jnp.concatenate([out_white, white_own], axis=1)
    part = jnp.einsum("tk,nk->nt", packed, mixed, precision=lax.Precision.HIGHEST)
    part = jnp.broadcast_to(part.reshape(NY, 1, 16, 32), (NY, 8, 16, 32)).reshape(32, 16, 32)
    part = lax.all_to_all(part, ("y", "c", "x"), 0, 0).reshape(NY, 2, 4, 16, 32)
    total = jnp.sum(part, axis=(0, 2))
    return total.reshape(2, 16, 16, 2).transpose(2, 0, 3, 1).reshape(64, 16)


def solution(mesh):
    devices = mesh.devices.reshape(-1, NY, 2, 4)
    split = Mesh(devices, ("z", "y", "c", "x"))
    dp = ("z", "y")
    in_specs = (
        P(dp, None, None),
        P(dp),
        P(None, "x"),
        P("c", None),
        P("c", dp, "x"),
        P("c", "x", dp),
        P(),
        P(None, dp),
    )
    return jax.shard_map(
        body, mesh=split, in_specs=in_specs, out_specs=P(None, dp), check_vma=False
    )
```

time: 597 us -> 259 us (0.43)
  waiting for transfers between devices: 402 us -> 122 us
  blocking collectives: 119 us -> 46.3 us
  starting transfers between devices: 1.45 us -> 36.1 us
  local copies, waits for them, and re-layouts: 34.9 us -> 17.9 us
  matrix products: 19.3 us -> 8.49 us
    all_gather x2, waiting for transfers between devices: 290 us -> 95.3 us  [layer_weights(): return lax.all_gather(shard, 'z', axis=0)]
    psum x2 -> x0, waiting for transfers between devices: 111 us -> none  [body(): lax.psum(partial_out.astype(jnp.bfloat16), 'mp').astype(jnp.float32)]
    all_gather x2, blocking collectives: 117 us -> 24.3 us  [the longest x1 22.5 us: body(): lax.all_gather(whitening.T, 'y', axis=0, tiled=True).reshape(64, 16, HD)]
    all_gather x2 -> x0, local copies, waits for them, and re-layouts: 31 us -> none  [the longest x1 23.4 us: body(): lax.all_gather(qkv_local, 'dp', axis=0, tiled=True)]
    all_to_all x0 -> x4, starting transfers between devices: none -> 30.3 us  [the longest x2 15.1 us: plane_gather(): return lax.all_to_all(spread, ('x', 'y'), 0, 0)]
    all_to_all x0 -> x4, waiting for transfers between devices: none -> 25.4 us  [the longest x2 13.4 us: plane_gather(): return lax.all_to_all(spread, ('x', 'y'), 0, 0)]
    all_to_all x0 -> x2, blocking collectives: none -> 22 us  [the longest x1 11.6 us: body(): part = lax.all_to_all(part, ('y', 'c', 'x'), 0, 0).reshape(NY, 2, 4, 16, 32)]
    dot_general x10 -> x14, matrix products: 18.7 us -> 7.94 us  [the longest x6 4.46 us: project(): jnp.einsum('btk,bkn->tn', normed, weight, preferred_element_type=F32)]
  transfers between devices with their start and end apart: 5 -> 9, of which waited for: 5 -> 5; matrix products, arithmetic and copies ran while one was open for 2% -> 9% of each run, Pallas kernels for 0% -> 0%
where the time goes in v1:
time: 259 us; the launch traced here: 255 us
  waiting for transfers between devices  122 us (47%)
  blocking collectives  46.3 us (18%)
  starting transfers between devices  36.1 us (14%)
  local copies, waits for them, and re-layouts  17.9 us (7%)
  between operations  14.7 us (6%)
  other arithmetic  9.94 us (4%)
  matrix products  8.49 us (3%)
    all_gather x2, waiting for transfers between devices, layer_weights(): return lax.all_gather(shard, 'z', axis=0)  95.3 us
    all_gather x1, blocking collectives, body(): lax.all_gather(whitening.T, 'y', axis=0, tiled=True).reshape(64, 16, HD)  22.5 us
    all_to_all x2, starting transfers between devices, plane_gather(): return lax.all_to_all(spread, ('x', 'y'), 0, 0)  15.1 us
    all_to_all x2, waiting for transfers between devices, plane_gather(): return lax.all_to_all(spread, ('x', 'y'), 0, 0)  13.4 us
    all_to_all x1, waiting for transfers between devices, body(): packed = lax.all_to_all(packed, 'z', 0, 0).reshape(32, 2 * HD)  12 us
    all_to_all x1, blocking collectives, body(): part = lax.all_to_all(part, ('y', 'c', 'x'), 0, 0).reshape(NY, 2, 4, 16, 32)  11.6 us
    all_to_all x1, blocking collectives, body(): regrouped = lax.all_to_all(mats, ('y', 'c'), 0, 0).reshape(NY, 2, 2, 32, HD)  10.4 us
    all_to_all x1, starting transfers between devices, body(): packed = lax.all_to_all(packed, 'z', 0, 0).reshape(32, 2 * HD)  7.95 us
  transfers between devices with their start and end apart: 9, of which 5 were waited for; matrix products, arithmetic and copies ran while one was open for 9% of the time, Pallas kernels for 0%

profile of v1, /device:TPU:6, one launch (start us, length us, event | category | flops | bytes accessed | tf_op | source)
XLA Modules:
  0.0 254.9 jit_solution(10375177286044964732)
XLA Ops:
  6.5 0.9 reshape.212
  7.5 1.1 reshape_squeeze.3
  9.4 10.4 %all_to_all.30 = bf16[8,2,32,120]{3,2,1,0:T(8,128)(2,1)S(1)} all-to-all(bf16[8,2,32,120]{3,2,1,0:T(8,128)(2,1)S(1)} %bitcast.217), channel_id=1, replica_groups=mesh['z'=16,'y'=4,'c'=2,'x'=4] {'y','c'}, dimensions={0} | all-to-all | bytes 245760 | tf_op jit(solution)/shard_map/all_to_all | solution.py:54
  21.0 1.2 broadcast_in_dim.30
  22.2 7.6 %all-to-all-start.1 = ((bf16[16,4,64,120]{3,2,1,0:T(8,128)(2,1)}), bf16[16,4,64,120]{3,2,1,0:T(8,128)(2,1)S(1)}, u32[]{:S(2)}, u32[]{:S(2)}) async-start(bf16[16,4,64,120]{3,2,1,0:T(8,128)(2,1)} %broadcast_in_dim.30), calls=%async_computation.1 | async-start | bytes 2097152 | tf_op jit(solution)/shard_map/all_to_all | solution.py:15
  29.9 1.8 all-gather.2
  31.7 13.4 %all-to-all-done.1 = bf16[16,4,64,120]{3,2,1,0:T(8,128)(2,1)S(1)} async-done(((bf16[16,4,64,120]{3,2,1,0:T(8,128)(2,1)}), bf16[16,4,64,120]{3,2,1,0:T(8,128)(2,1)S(1)}, u32[]{:S(2)}, u32[]{:S(2)}) %all-to-all-start.1) | async-done | bytes 983072 | tf_op jit(solution)/shard_map/all_to_all | solution.py:15
  45.3 1.9 collective-permute-start.1
  49.0 45.1 %all-gather.8.cloned.1.call-done = bf16[32,128,128]{2,1,0:T(8,128)(2,1)} async-done(((bf16[2,128,128]{2,1,0:T(8,128)(2,1)}), bf16[32,128,128]{2,1,0:T(8,128)(2,1)}) %all-gather.8.cloned.1.call-update) | async-done | bytes 1048592 | tf_op jit(solution)/shard_map/all_gather | solution.py:60
  94.1 1.3 slice.69
  95.4 1.9 collective-permute-start.2
  98.9 1.0 collective-permute-done.2
  100.1 1.4 broadcast_select_fusion.2
  102.7 1.5 fusion.31
  105.4 1.4 fusion.12
  106.8 7.2 %all-to-all-start.2 = ((bf16[16,256,120]{1,2,0:T(8,128)(2,1)}), bf16[16,256,120]{1,2,0:T(8,128)(2,1)}, u32[]{:S(2)}, u32[]{:S(2)}) async-start(bf16[16,256,120]{1,2,0:T(8,128)(2,1)} %fusion.12), calls=%async_computation.2 | async-start | bytes 1966080 | tf_op jit(solution)/shard_map/all_to_all | solution.py:96
  114.0 50.2 %all-gather.6.cloned.1.call-done = bf16[32,128,128]{2,1,0:T(8,128)(2,1)} async-done(((bf16[2,128,128]{2,1,0:T(8,128)(2,1)}), bf16[32,128,128]{2,1,0:T(8,128)(2,1)}) %all-gather.6.cloned.1.call-update) | async-done | bytes 1048592 | tf_op jit(solution)/shard_map/all_gather | solution.py:60
  164.2 1.3 slice.65
  165.5 1.0 copy.179
  166.5 1.9 collective-permute-start
  168.9 1.4 convert_reduce_fusion.2
  170.9 1.0 broadcast_in_dim.33
  172.0 7.5 %all-to-all-start.3 = ((bf16[16,256,120]{1,2,0:T(8,128)(2,1)}), bf16[16,256,120]{1,2,0:T(8,128)(2,1)S(1)}, u32[]{:S(2)}, u32[]{:S(2)}) async-start(bf16[16,256,120]{1,2,0:T(8,128)(2,1)} %broadcast_in_dim.33), calls=%async_computation.3 | async-start | bytes 1966080 | tf_op jit(solution)/shard_map/all_to_all | solution.py:15
  179.4 22.5 %all_gather.20 = f32[64,1920]{1,0:T(8,128)S(1)} all-gather(f32[16,1920]{1,0:T(8,128)S(1)} %bitcast.226), channel_id=1, replica_groups=mesh['z'=16,'y'=4,'c'=2,'x'=4] {'y'}, dimensions={0}, use_global_device_ids=true | all-gather | bytes 614400 | tf_op jit(solution)/shard_map/all_gather | solution.py:89
  201.9 0.7 reshape.230
  203.2 0.7 fusion.71
  204.0 0.9 reshape.236
  204.9 2.9 %broadcast_select_fusion.3 = (bf16[16,2,120,120]{3,2,0,1:T(8,128)(2,1)}, bf16[16,2,120,120]{3,2,0,1:T(8,128)(2,1)}) fusion(bf16[16,2,120,120]{3,2,0,1:T(8,128)(2,1)} %collective-permute-done, pred[]{:T(512)S(6)} %eq.2, bf16[16,2,128,128]{3,2,1,0:T(8,128)(2,1)S(1)} %bitcast.209), kind=kLoop, calls=%fused_computation.55 | loop fusion | flops 921600 | bytes 3747841 | tf_op jit(solution)/shard_map/jit(_where)/select_n | solution.py:68
  213.2 8.0 %all-to-all-start.4 = ((f32[16,2,240]{2,1,0:T(2,128)}), f32[16,2,240]{2,1,0:T(2,128)S(1)}, u32[]{:S(2)}, u32[]{:S(2)}) async-start(f32[16,2,240]{2,1,0:T(2,128)} %broadcast_in_dim.34), calls=%async_computation.4 | async-start | bytes 65536 | tf_op jit(solution)/shard_map/all_to_all | solution.py:114
  221.8 12.0 %all-to-all-done.4 = f32[16,2,240]{2,1,0:T(2,128)S(1)} async-done(((f32[16,2,240]{2,1,0:T(2,128)}), f32[16,2,240]{2,1,0:T(2,128)S(1)}, u32[]{:S(2)}, u32[]{:S(2)}) %all-to-all-start.4) | async-done | bytes 30752 | tf_op jit(solution)/shard_map/all_to_all | solution.py:114
  234.3 11.6 %all_to_all.31 = f32[32,1,512]{2,1,0:T(1,128)S(1)} all-to-all(f32[32,1,512]{2,1,0:T(1,128)S(1)} %reshape.259), channel_id=1, replica_groups=mesh['z'=16,'y'=4,'c'=2,'x'=4] {'y','c','x'}, dimensions={0} | all-to-all | bytes 131072 | tf_op jit(solution)/shard_map/all_to_all | solution.py:118
  246.4 0.8 reduce.8
  (112 shorter events, 17.0 us)
Async XLA Ops:
  6.5 14.0 %copy-start = (bf16[512,480]{0,1:T(8,128)(2,1)S(1)}, bf16[512,480]{0,1:T(8,128)(2,1)}, u32[]{:S(2)}) copy-start(bf16[512,480]{0,1:T(8,128)(2,1)} %param.10) | copy-start | bytes 1474564
  6.5 14.0 %copy-start.11 = (bf16[1,128,512]{2,1,0:T(8,128)(2,1)S(1)}, bf16[1,128,512]{2,1,0:T(8,128)(2,1)}, u32[]{:S(2)}) copy-start(bf16[1,128,512]{2,1,0:T(8,128)(2,1)} %param.8) | copy-start | bytes 393220
  6.5 87.6 %all-gather.8.cloned.1.call-start = ((), (), s32[]{:S(2)}) async-start(), calls=%async_computation.7 | async-start | bytes 1114112 | tf_op jit(solution)/shard_map/all_gather | solution.py:60
  22.2 7.7 %copy-start.13 = (f32[1,1920]{1,0:T(1,128)S(1)}, f32[1,1920]{1,0:T(1,128)}, u32[]{:S(2)}) copy-start(f32[1,1920]{1,0:T(1,128)} %param.11) | copy-start | bytes 23044
  22.2 22.9 %all-to-all-start.1 = ((bf16[16,4,64,120]{3,2,1,0:T(8,128)(2,1)}), bf16[16,4,64,120]{3,2,1,0:T(8,128)(2,1)S(1)}, u32[]{:S(2)}, u32[]{:S(2)}) async-start(bf16[16,4,64,120]{3,2,1,0:T(8,128)(2,1)} %broadcast_in_dim.30), calls=%async_computation.1 | async-start | bytes 2097152 | tf_op jit(solution)/shard_map/all_to_all | solution.py:15
  29.8 134.4 %all-gather.6.cloned.1.call-start = ((), (), s32[]{:S(2)}) async-start(), calls=%async_computation.6 | async-start | bytes 1114112 | tf_op jit(solution)/shard_map/all_gather | solution.py:60
  45.3 52.1 %collective-permute-start.1 = (bf16[2,16,64,120]{3,2,1,0:T(8,128)(2,1)S(1)}, bf16[2,16,64,120]{3,2,1,0:T(8,128)(2,1)S(1)}, u32[]{:S(2)}, u32[]{:S(2)}) collective-permute-start(bf16[2,16,64,120]{3,2,1,0:T(8,128)(2,1)S(1)} %get-tuple-element.14), channel_id=1, source_target_pairs={{0,4},{4,0},{1,5},{5,1},{2,6},{6,2},{3,7},{7,3},{8,12},{12,8},{9,1... | collective-permute-start | bytes 1474568 | tf_op jit(solution)/shard_map/ppermute | solution.py:19
  49.0 55.3 %copy-start.14 = (pred[2,128]{1,0:T(4,128)(4,1)}, pred[2,128]{1,0:T(4,128)(4,1)S(1)}, u32[]{:S(2)}) copy-start(pred[2,128]{1,0:T(4,128)(4,1)S(1)} %get-tuple-element.8) | copy-start | bytes 772
  95.4 4.5 %collective-permute-start.2 = (bf16[16,2,120,120]{3,2,0,1:T(8,128)(2,1)S(1)}, bf16[16,2,120,120]{3,2,0,1:T(8,128)(2,1)S(1)}, u32[]{:S(2)}, u32[]{:S(2)}) collective-permute-start(bf16[16,2,120,120]{3,2,0,1:T(8,128)(2,1)S(1)} %copy.181), channel_id=1, source_target_pairs={{0,4},{4,0},{1,5},{5,1},{2,6},{6,2},{3,7},{7,3},{8,12},{12,8},{9,1... | collective-permute-start | bytes 2764808 | tf_op jit(solution)/shard_map/ppermute | solution.py:19
  98.8 1.2 copy-start.3
  104.2 1.2 copy-start.1
  106.8 62.1 %all-to-all-start.2 = ((bf16[16,256,120]{1,2,0:T(8,128)(2,1)}), bf16[16,256,120]{1,2,0:T(8,128)(2,1)}, u32[]{:S(2)}, u32[]{:S(2)}) async-start(bf16[16,256,120]{1,2,0:T(8,128)(2,1)} %fusion.12), calls=%async_computation.2 | async-start | bytes 1966080 | tf_op jit(solution)/shard_map/all_to_all | solution.py:96
  166.5 38.4 %collective-permute-start = (bf16[16,2,120,120]{3,2,0,1:T(8,128)(2,1)}, bf16[16,2,120,120]{3,2,0,1:T(8,128)(2,1)}, u32[]{:S(2)}, u32[]{:S(2)}) collective-permute-start(bf16[16,2,120,120]{3,2,0,1:T(8,128)(2,1)} %copy.179), channel_id=1, source_target_pairs={{0,4},{4,0},{1,5},{5,1},{2,6},{6,2},{3,7},{7,3},{8,12},{12,8},{9,1... | collective-permute-start | bytes 2764808 | tf_op jit(solution)/shard_map/ppermute | solution.py:19
  168.9 3.1 %copy-start.9 = (bf16[1,256,120]{1,2,0:T(8,128)(2,1)}, bf16[1,256,120]{1,2,0:T(8,128)(2,1)S(1)}, u32[]{:S(2)}) copy-start(bf16[1,256,120]{1,2,0:T(8,128)(2,1)S(1)} %copy.180) | copy-start | bytes 184324
  170.3 0.7 copy-start.5
  171.9 7.5 %copy-start.10 = (f32[1920,16]{0,1:T(8,128)S(1)}, f32[1920,16]{0,1:T(8,128)}, u32[]{:S(2)}) copy-start(f32[1920,16]{0,1:T(8,128)} %param.15) | copy-start | bytes 368644
  172.0 30.0 %copy-start.12 = (f32[1920]{0:T(1024)S(1)}, f32[1920]{0:T(1024)}, u32[]{:S(2)}) copy-start(f32[1920]{0:T(1024)} %param.14) | copy-start | bytes 23044
  172.0 36.0 %all-to-all-start.3 = ((bf16[16,256,120]{1,2,0:T(8,128)(2,1)}), bf16[16,256,120]{1,2,0:T(8,128)(2,1)S(1)}, u32[]{:S(2)}, u32[]{:S(2)}) async-start(bf16[16,256,120]{1,2,0:T(8,128)(2,1)} %broadcast_in_dim.33), calls=%async_computation.3 | async-start | bytes 1966080 | tf_op jit(solution)/shard_map/all_to_all | solution.py:15
  179.4 25.5 %copy-start.2 = (bf16[32,128,128]{2,1,0:T(8,128)(2,1)S(1)}, bf16[32,128,128]{2,1,0:T(8,128)(2,1)}, u32[]{:S(2)}) copy-start(bf16[32,128,128]{2,1,0:T(8,128)(2,1)} %all-gather.6.cloned.1.call-done) | copy-start | bytes 3145732
  204.9 2.9 %copy-start.6 = (f32[256,120]{0,1:T(8,128)S(1)}, f32[256,120]{0,1:T(8,128)}, u32[]{:S(2)}) copy-start(f32[256,120]{0,1:T(8,128)} %copy-done.5) | copy-start | bytes 368644
  204.9 2.9 %copy-start.16 = (f32[2,128]{1,0:T(2,128)S(1)}, f32[2,128]{1,0:T(2,128)}, u32[]{:S(2)}) copy-start(f32[2,128]{1,0:T(2,128)} %get-tuple-element.7) | copy-start | bytes 3076
  207.9 1.2 copy-start.7
  209.1 1.2 copy-start.8
  210.3 0.7 copy-start.15
  210.3 1.2 copy-start.4
  213.2 20.6 %all-to-all-start.4 = ((f32[16,2,240]{2,1,0:T(2,128)}), f32[16,2,240]{2,1,0:T(2,128)S(1)}, u32[]{:S(2)}, u32[]{:S(2)}) async-start(f32[16,2,240]{2,1,0:T(2,128)} %broadcast_in_dim.34), calls=%async_computation.4 | async-start | bytes 65536 | tf_op jit(solution)/shard_map/all_to_all | solution.py:114
Sparse Core Ops, SparseCore 0:
  20.6 73.3 all-gather.7
  96.2 67.9 all-gather.5

commit v2 on v1

--- a/solution.py
+++ b/solution.py
@@ -50,19 +50,21 @@
     out = out_weight[0].T.reshape(30, NY, HD).transpose(1, 0, 2)[:, None]
     mats = jnp.concatenate([qkv, out], axis=1)
     tail = jnp.broadcast_to(lengths[0].astype(BF), (NY, 4, 2, HD))
-    mats = jnp.concatenate([mats, tail], axis=2).reshape(2 * NY, 2, 32, HD)
-    regrouped = lax.all_to_all(mats, ("y", "c"), 0, 0).reshape(NY, 2, 2, 32, HD)
+    mats = jnp.concatenate([mats, tail], axis=2)
+    mats = jnp.broadcast_to(mats[:, None], (NY, 2, 4, 32, HD)).reshape(2 * NY, 4, 32, HD)
+    regrouped = lax.all_to_all(mats, ("y", "c"), 0, 0).reshape(NY, 2, 4, 32, HD)
     plane_lengths = regrouped[:, 0, 0, 30, 0].astype(jnp.int32)
 
-    def layer_weights(layer):
-        shard = regrouped[:, layer, :, :30].transpose(1, 0, 2, 3).reshape(2, HD, HD)
-        shard = jnp.pad(shard, ((0, 0), (0, 8), (0, 8)))
-        return lax.all_gather(shard, "z", axis=0)
+    def shard(layer):
+        rows = regrouped[:, layer, :, :30].transpose(1, 0, 2, 3)
+        return rows.reshape(4, HD, HD)
 
-    halves = [layer_weights(0), layer_weights(1)]
+    first_shard = lax.dynamic_slice_in_dim(shard(0), 2 * core, 2, 0)
+    first_shard, second_shard = lax.optimization_barrier((first_shard, shard(1)))
+    second_weights = lax.all_gather(second_shard, "z", axis=0)
+    own = lax.all_gather(first_shard, "z", axis=0)
 
     def both_halves(own):
-        own = own[:, :, :HD, :HD]
         other = swap_cores(own)
         first = jnp.where(core == 0, own, other)
         second = jnp.where(core == 0, other, own)
@@ -86,9 +88,13 @@
     valid = frame_ids[None, :] < my_lengths[:, None]
     share = valid.astype(F32) / my_lengths.astype(F32)[:, None]
 
-    white_cols = lax.all_gather(whitening.T, "y", axis=0, tiled=True).reshape(64, 16, HD)
+    white_cols = whitening.T.reshape(16, 16, HD).transpose(1, 0, 2)
+    white_cols = jnp.broadcast_to(white_cols[None], (NY, 16, 16, HD))
+    white_cols = lax.all_to_all(white_cols, "y", 0, 0)
 
-    q_w, k_w, v_w, o_w = both_halves(halves[0])
+    x0, white_cols, gains = lax.optimization_barrier((x0, white_cols, gains))
+
+    q_w, k_w, v_w, o_w = both_halves(own)
     probs, values = head_probs(normalized(x0, gains[0]), q_w, k_w, v_w, valid)
     context = jnp.einsum("uqk,ukd->uqd", probs, values, preferred_element_type=F32)
     context = context.astype(BF).reshape(256, HD)
@@ -99,20 +105,20 @@
     x1_own = (x0_own.astype(F32) + attended).astype(BF)
     x1 = plane_gather(x1_own)
 
-    q_w, k_w, v_w, o_w = both_halves(halves[1])
+    q_w, k_w, v_w, o_w = (second_weights[:, i] for i in range(4))
     probs, values = head_probs(normalized(x1, gains[1]), q_w, k_w, v_w, valid)
     context = jnp.einsum("uqk,ukd->uqd", probs, values, preferred_element_type=F32).astype(BF)
     pooled_context = jnp.sum(context.astype(F32) * share[:, :, None], axis=1)
     pooled_x1 = jnp.sum(x1_own.reshape(2, 128, HD).astype(F32) * share[:, :, None], axis=1)
     out_white = jnp.einsum(
-        "nbc,bcr->nr", white_cols, o_w.astype(F32), precision=lax.Precision.HIGHEST
+        "ybnc,bcr->ynr", white_cols, o_w.astype(F32), precision=lax.Precision.HIGHEST
     )
     white_own = lax.dynamic_index_in_dim(white_cols, chunk, 1, keepdims=False)
     center_own = lax.dynamic_index_in_dim(center.reshape(16, HD), chunk, 0, keepdims=False)
     packed = jnp.concatenate([pooled_context, pooled_x1 - center_own], axis=1)
     packed = jnp.broadcast_to(packed[None], (16,) + packed.shape)
     packed = lax.all_to_all(packed, "z", 0, 0).reshape(32, 2 * HD)
-    mixed = jnp.concatenate([out_white, white_own], axis=1)
+    mixed = jnp.concatenate([out_white, white_own], axis=2).reshape(64, 2 * HD)
     part = jnp.einsum("tk,nk->nt", packed, mixed, precision=lax.Precision.HIGHEST)
     part = jnp.broadcast_to(part.reshape(NY, 1, 16, 32), (NY, 8, 16, 32)).reshape(32, 16, 32)
     part = lax.all_to_all(part, ("y", "c", "x"), 0, 0).reshape(NY, 2, 4, 16, 32)

time: 259 us -> 201 us (0.78)
  waiting for transfers between devices: 122 us -> 54.7 us
  blocking collectives: 46.3 us -> 54 us
  matrix products: 8.49 us -> 12.7 us
  starting transfers between devices: 36.1 us -> 39.6 us
  local copies, waits for them, and re-layouts: 17.9 us -> 14.7 us
  other arithmetic: 9.94 us -> 7.29 us
    all_gather x2 -> x1, waiting for transfers between devices: 95.3 us -> 6.83 us  [body(): second_weights = lax.all_gather(second_shard, 'z', axis=0)]
    all_gather x1, blocking collectives: 22.5 us -> 38.9 us  [body(): own = lax.all_gather(first_shard, 'z', axis=0)]
    all_to_all x1, waiting for transfers between devices: 0.01 us -> 13.3 us  [body(): partial = lax.all_to_all(partial, ('x', 'y'), 0, 0)]
    all_to_all x0 -> x2, waiting for transfers between devices: none -> 11.9 us  [the longest x1 7.12 us: body(): regrouped = lax.all_to_all(mats, ('y', 'c'), 0, 0).reshape(NY, 2, 4, 32, HD)]
    all_to_all x1 -> x0, blocking collectives: 10.4 us -> none  [body(): regrouped = lax.all_to_all(mats, ('y', 'c'), 0, 0).reshape(NY, 2, 2, 32, HD)]
    all_to_all x0 -> x2, starting transfers between devices: none -> 8.84 us  [the longest x1 4.47 us: body(): regrouped = lax.all_to_all(mats, ('y', 'c'), 0, 0).reshape(NY, 2, 4, 32, HD)]
    unnamed x42 -> x25, local copies, waits for them, and re-layouts: 4.15 us -> 0.82 us
    dot_general x6, matrix products: 4.46 us -> 7.71 us  [project(): jnp.einsum('btk,bkn->tn', normed, weight, preferred_element_type=F32)]
  transfers between devices with their start and end apart: 9 -> 9, of which waited for: 5 -> 6; matrix products, arithmetic and copies ran while one was open for 9% -> 11% of each run, Pallas kernels for 0% -> 0%
where the time goes in v2:
time: 201 us; the launch traced here: 198 us
  waiting for transfers between devices  54.7 us (27%)
  blocking collectives  54 us (27%)
  starting transfers between devices  39.6 us (20%)
  local copies, waits for them, and re-layouts  14.7 us (7%)
  between operations  14.6 us (7%)
  matrix products  12.7 us (6%)
  other arithmetic  7.29 us (4%)
    all_gather x1, blocking collectives, body(): own = lax.all_gather(first_shard, 'z', axis=0)  38.9 us
    all_to_all x2, starting transfers between devices, plane_gather(): return lax.all_to_all(spread, ('x', 'y'), 0, 0)  13.8 us
    all_to_all x1, waiting for transfers between devices, body(): partial = lax.all_to_all(partial, ('x', 'y'), 0, 0)  13.3 us
    all_to_all x1, blocking collectives, body(): part = lax.all_to_all(part, ('y', 'c', 'x'), 0, 0).reshape(NY, 2, 4, 16, 32)  13.1 us
    all_to_all x2, waiting for transfers between devices, plane_gather(): return lax.all_to_all(spread, ('x', 'y'), 0, 0)  11.6 us
    all_to_all x1, waiting for transfers between devices, body(): packed = lax.all_to_all(packed, 'z', 0, 0).reshape(32, 2 * HD)  11.1 us
    dot_general x6, matrix products, project(): jnp.einsum('btk,bkn->tn', normed, weight, preferred_element_type=F32)  7.71 us
    all_to_all x1, starting transfers between devices, body(): packed = lax.all_to_all(packed, 'z', 0, 0).reshape(32, 2 * HD)  7.68 us
  transfers between devices with their start and end apart: 9, of which 6 were waited for; matrix products, arithmetic and copies ran while one was open for 11% of the time, Pallas kernels for 0%

profile of v2, /device:TPU:6, one launch (start us, length us, event | category | flops | bytes accessed | tf_op | source)
XLA Modules:
  0.0 197.6 jit_solution(12907532395513297033)
XLA Ops:
  6.5 0.9 reshape.200
  7.5 1.1 reshape_squeeze.3
  10.1 4.5 %all-to-all-start.2 = ((bf16[8,4,32,120]{3,2,1,0:T(8,128)(2,1)}), bf16[8,4,32,120]{3,2,1,0:T(8,128)(2,1)S(1)}, u32[]{:S(2)}, u32[]{:S(2)}) async-start(bf16[8,4,32,120]{3,2,1,0:T(8,128)(2,1)} %bitcast.19), calls=%async_computation.2 | async-start | bytes 524288 | tf_op jit(solution)/shard_map/all_to_all | solution.py:55
  15.0 7.1 %all-to-all-done.2 = bf16[8,4,32,120]{3,2,1,0:T(8,128)(2,1)S(1)} async-done(((bf16[8,4,32,120]{3,2,1,0:T(8,128)(2,1)}), bf16[8,4,32,120]{3,2,1,0:T(8,128)(2,1)S(1)}, u32[]{:S(2)}, u32[]{:S(2)}) %all-to-all-start.2) | async-done | bytes 245792 | tf_op jit(solution)/shard_map/all_to_all | solution.py:55
  22.1 1.2 broadcast_in_dim.32
  23.3 8.2 %all-to-all-start = ((bf16[16,4,64,120]{3,2,1,0:T(8,128)(2,1)}), bf16[16,4,64,120]{3,2,1,0:T(8,128)(2,1)S(1)}, u32[]{:S(2)}, u32[]{:S(2)}) async-start(bf16[16,4,64,120]{3,2,1,0:T(8,128)(2,1)} %broadcast_in_dim.32), calls=%async_computation | async-start | bytes 2097152 | tf_op jit(solution)/shard_map/all_to_all | solution.py:15
  32.6 38.9 %all-gather.1 = bf16[32,120,120]{2,1,0:T(8,128)(2,1)S(1)} all-gather(bf16[2,120,120]{2,1,0:T(8,128)(2,1)S(1)} %copy.149), channel_id=3, replica_groups=mesh['z'=16,'y'=4,'c'=2,'x'=4] {'z'}, dimensions={0}, use_global_device_ids=true | all-gather | bytes 979200 | tf_op jit(solution)/shard_map/all_gather | solution.py:65
  72.1 1.9 collective-permute-start.1
  74.0 1.1 reshape.198
  75.2 2.0 %all-gather.2 = f32[2,1,1920]{2,1,0:T(1,128)S(1)} all-gather(f32[1,1,1920]{2,1,0:T(1,128)S(1)} %bitcast.232), channel_id=1, replica_groups=mesh['z'=16,'y'=4,'c'=2,'x'=4] {'c'}, dimensions={0}, use_global_device_ids=true | all-gather | bytes 23040 | tf_op jit(solution)/shard_map/all_gather | solution.py:83
  78.2 1.6 copy.145
  79.8 0.8 broadcast_in_dim.33
  80.7 4.4 %all-to-all-start.1 = ((f32[4,16,16,120]{3,2,1,0:T(8,128)}), f32[4,16,16,120]{3,2,1,0:T(8,128)S(1)}, u32[]{:S(2)}, u32[]{:S(2)}) async-start(f32[4,16,16,120]{3,2,1,0:T(8,128)} %broadcast_in_dim.33), calls=%async_computation.1 | async-start | bytes 1048576 | tf_op jit(solution)/shard_map/all_to_all | solution.py:93
  85.2 1.9 collective-permute-start
  87.3 2.6 %broadcast_select_fusion.1 = (bf16[16,2,120,120]{2,3,0,1:T(8,128)(2,1)}, bf16[16,2,120,120]{2,3,0,1:T(8,128)(2,1)}) fusion(bf16[16,2,120,120]{2,3,0,1:T(8,128)(2,1)} %collective-permute-done.1, bf16[16,2,120,120]{2,3,0,1:T(8,128)(2,1)S(1)} %copy.150, pred[]{:T(512)S(6)} %eq.4), kind=kLoop, calls=%fused_computation.54 | loop fusion | flops 921600 | bytes 3686401 | tf_op jit(solution)/shard_map/jit(_where)/select_n | solution.py:70
  90.2 4.8 %all-to-all-done.1 = f32[4,16,16,120]{3,2,1,0:T(8,128)S(1)} async-done(((f32[4,16,16,120]{3,2,1,0:T(8,128)}), f32[4,16,16,120]{3,2,1,0:T(8,128)S(1)}, u32[]{:S(2)}, u32[]{:S(2)}) %all-to-all-start.1) | async-done | bytes 491552 | tf_op jit(solution)/shard_map/all_to_all | solution.py:93
  98.3 1.7 fusion.31
  100.3 1.4 fusion.12
  101.8 5.4 %all-to-all-start.3 = ((bf16[16,256,120]{1,2,0:T(8,128)(2,1)}), bf16[16,256,120]{1,2,0:T(8,128)(2,1)S(1)}, u32[]{:S(2)}, u32[]{:S(2)}) async-start(bf16[16,256,120]{1,2,0:T(8,128)(2,1)} %fusion.12), calls=%async_computation.3 | async-start | bytes 1966080 | tf_op jit(solution)/shard_map/all_to_all | solution.py:102
  107.7 13.3 %all-to-all-done.3 = bf16[16,256,120]{1,2,0:T(8,128)(2,1)S(1)} async-done(((bf16[16,256,120]{1,2,0:T(8,128)(2,1)}), bf16[16,256,120]{1,2,0:T(8,128)(2,1)S(1)}, u32[]{:S(2)}, u32[]{:S(2)}) %all-to-all-start.3) | async-done | bytes 983072 | tf_op jit(solution)/shard_map/all_to_all | solution.py:102
  121.1 1.0 broadcast_in_dim.39
  122.2 5.6 %all-to-all-start.4 = ((bf16[16,256,120]{1,2,0:T(8,128)(2,1)}), bf16[16,256,120]{1,2,0:T(8,128)(2,1)S(1)}, u32[]{:S(2)}, u32[]{:S(2)}) async-start(bf16[16,256,120]{1,2,0:T(8,128)(2,1)} %broadcast_in_dim.39), calls=%async_computation.4 | async-start | bytes 1966080 | tf_op jit(solution)/shard_map/all_to_all | solution.py:15
  128.0 1.0 multiply_reduce_fusion
  129.0 11.6 %all-to-all-done.4 = bf16[16,256,120]{1,2,0:T(8,128)(2,1)S(1)} async-done(((bf16[16,256,120]{1,2,0:T(8,128)(2,1)}), bf16[16,256,120]{1,2,0:T(8,128)(2,1)S(1)}, u32[]{:S(2)}, u32[]{:S(2)}) %all-to-all-start.4) | async-done | bytes 983072 | tf_op jit(solution)/shard_map/all_to_all | solution.py:15
  141.2 6.8 %all-gather.5.cloned.1.call-done = bf16[64,120,120]{2,1,0:T(8,128)(2,1)} async-done(((bf16[4,120,120]{2,1,0:T(8,128)(2,1)}), bf16[64,120,120]{2,1,0:T(8,128)(2,1)}) %all-gather.5.cloned.1.call-update) | async-done | bytes 1843216 | tf_op jit(solution)/shard_map/all_gather | solution.py:64
  148.1 1.7 fusion.29
  149.8 1.7 fusion.30
  152.0 1.7 fusion.28
  154.7 7.7 %all-to-all-start.5 = ((f32[16,2,240]{2,1,0:T(2,128)}), f32[16,2,240]{2,1,0:T(2,128)S(1)}, u32[]{:S(2)}, u32[]{:S(2)}) async-start(f32[16,2,240]{2,1,0:T(2,128)} %broadcast_in_dim.40), calls=%async_computation.5 | async-start | bytes 65536 | tf_op jit(solution)/shard_map/all_to_all | solution.py:120
  162.4 1.6 convolution_bitcast_fusion.6
  163.9 11.1 %all-to-all-done.5 = f32[16,2,240]{2,1,0:T(2,128)S(1)} async-done(((f32[16,2,240]{2,1,0:T(2,128)}), f32[16,2,240]{2,1,0:T(2,128)S(1)}, u32[]{:S(2)}, u32[]{:S(2)}) %all-to-all-start.5) | async-done | bytes 30752 | tf_op jit(solution)/shard_map/all_to_all | solution.py:120
  175.5 13.1 %all_to_all.35 = f32[32,1,512]{2,1,0:T(1,128)S(1)} all-to-all(f32[32,1,512]{2,1,0:T(1,128)S(1)} %reshape.239), channel_id=1, replica_groups=mesh['z'=16,'y'=4,'c'=2,'x'=4] {'y','c','x'}, dimensions={0} | all-to-all | bytes 131072 | tf_op jit(solution)/shard_map/all_to_all | solution.py:124
  (95 shorter events, 13.7 us)
Async XLA Ops:
  6.5 8.0 %copy-start = (bf16[512,480]{0,1:T(8,128)(2,1)S(1)}, bf16[512,480]{0,1:T(8,128)(2,1)}, u32[]{:S(2)}) copy-start(bf16[512,480]{0,1:T(8,128)(2,1)} %param.10) | copy-start | bytes 1474564
  6.5 8.0 %copy-start.8 = (bf16[1,128,512]{2,1,0:T(8,128)(2,1)S(1)}, bf16[1,128,512]{2,1,0:T(8,128)(2,1)}, u32[]{:S(2)}) copy-start(bf16[1,128,512]{2,1,0:T(8,128)(2,1)} %param.8) | copy-start | bytes 393220
  10.1 12.0 %all-to-all-start.2 = ((bf16[8,4,32,120]{3,2,1,0:T(8,128)(2,1)}), bf16[8,4,32,120]{3,2,1,0:T(8,128)(2,1)S(1)}, u32[]{:S(2)}, u32[]{:S(2)}) async-start(bf16[8,4,32,120]{3,2,1,0:T(8,128)(2,1)} %bitcast.19), calls=%async_computation.2 | async-start | bytes 524288 | tf_op jit(solution)/shard_map/all_to_all | solution.py:55
  22.1 9.6 %copy-start.5 = (bf16[8,4,32,120]{3,2,1,0:T(8,128)(2,1)}, bf16[8,4,32,120]{3,2,1,0:T(8,128)(2,1)S(1)}, u32[]{:S(2)}) copy-start(bf16[8,4,32,120]{3,2,1,0:T(8,128)(2,1)S(1)} %all-to-all-done.2) | copy-start | bytes 737284
  23.3 56.5 %all-to-all-start = ((bf16[16,4,64,120]{3,2,1,0:T(8,128)(2,1)}), bf16[16,4,64,120]{3,2,1,0:T(8,128)(2,1)S(1)}, u32[]{:S(2)}, u32[]{:S(2)}) async-start(bf16[16,4,64,120]{3,2,1,0:T(8,128)(2,1)} %broadcast_in_dim.32), calls=%async_computation | async-start | bytes 2097152 | tf_op jit(solution)/shard_map/all_to_all | solution.py:15
  31.6 116.5 %all-gather.5.cloned.1.call-start = ((), (), s32[]{:S(2)}) async-start(), calls=%async_computation.7 | async-start | bytes 2088960 | tf_op jit(solution)/shard_map/all_gather | solution.py:64
  31.7 43.4 %copy-start.10 = (f32[1,1920]{1,0:T(1,128)S(1)}, f32[1,1920]{1,0:T(1,128)}, u32[]{:S(2)}) copy-start(f32[1,1920]{1,0:T(1,128)} %param.11) | copy-start | bytes 23044
  72.1 15.2 %collective-permute-start.1 = (bf16[16,2,120,120]{2,3,0,1:T(8,128)(2,1)S(1)}, bf16[16,2,120,120]{2,3,0,1:T(8,128)(2,1)}, u32[]{:S(2)}, u32[]{:S(2)}) collective-permute-start(bf16[16,2,120,120]{2,3,0,1:T(8,128)(2,1)S(1)} %copy.150), channel_id=1, source_target_pairs={{0,4},{4,0},{1,5},{5,1},{2,6},{6,2},{3,7},{7,3},{8,12},{12,8},{9,1... | collective-permute-start | bytes 2764808 | tf_op jit(solution)/shard_map/ppermute | solution.py:19
  80.7 14.3 %all-to-all-start.1 = ((f32[4,16,16,120]{3,2,1,0:T(8,128)}), f32[4,16,16,120]{3,2,1,0:T(8,128)S(1)}, u32[]{:S(2)}, u32[]{:S(2)}) async-start(f32[4,16,16,120]{3,2,1,0:T(8,128)} %broadcast_in_dim.33), calls=%async_computation.1 | async-start | bytes 1048576 | tf_op jit(solution)/shard_map/all_to_all | solution.py:93
  85.2 4.7 %collective-permute-start = (bf16[2,16,64,120]{3,2,1,0:T(8,128)(2,1)S(1)}, bf16[2,16,64,120]{3,2,1,0:T(8,128)(2,1)S(1)}, u32[]{:S(2)}, u32[]{:S(2)}) collective-permute-start(bf16[2,16,64,120]{3,2,1,0:T(8,128)(2,1)S(1)} %get-tuple-element.20), channel_id=1, source_target_pairs={{0,4},{4,0},{1,5},{5,1},{2,6},{6,2},{3,7},{7,3},{8,12},{12,8},{9,1... | collective-permute-start | bytes 1474568 | tf_op jit(solution)/shard_map/ppermute | solution.py:19
  95.0 1.3 copy-start.1
  95.0 1.4 copy-start.7
  96.4 1.0 copy-start.6
  96.4 1.9 copy-start.3
  101.8 19.2 %all-to-all-start.3 = ((bf16[16,256,120]{1,2,0:T(8,128)(2,1)}), bf16[16,256,120]{1,2,0:T(8,128)(2,1)S(1)}, u32[]{:S(2)}, u32[]{:S(2)}) async-start(bf16[16,256,120]{1,2,0:T(8,128)(2,1)} %fusion.12), calls=%async_computation.3 | async-start | bytes 1966080 | tf_op jit(solution)/shard_map/all_to_all | solution.py:102
  107.6 20.1 %copy-start.9 = (f32[1920]{0:T(1024)S(1)}, f32[1920]{0:T(1024)}, u32[]{:S(2)}) copy-start(f32[1920]{0:T(1024)} %param.14) | copy-start | bytes 23044
  121.1 1.1 copy-start.4
  121.1 6.9 %copy-start.2 = (f32[4,16,16,120]{3,2,1,0:T(8,128)S(1)}, f32[4,16,16,120]{3,2,1,0:T(8,128)}, u32[]{:S(2)}) copy-start(f32[4,16,16,120]{3,2,1,0:T(8,128)} %copy-done.1) | copy-start | bytes 1474564
  122.2 18.5 %all-to-all-start.4 = ((bf16[16,256,120]{1,2,0:T(8,128)(2,1)}), bf16[16,256,120]{1,2,0:T(8,128)(2,1)S(1)}, u32[]{:S(2)}, u32[]{:S(2)}) async-start(bf16[16,256,120]{1,2,0:T(8,128)(2,1)} %broadcast_in_dim.39), calls=%async_computation.4 | async-start | bytes 1966080 | tf_op jit(solution)/shard_map/all_to_all | solution.py:15
  154.7 20.3 %all-to-all-start.5 = ((f32[16,2,240]{2,1,0:T(2,128)}), f32[16,2,240]{2,1,0:T(2,128)S(1)}, u32[]{:S(2)}, u32[]{:S(2)}) async-start(f32[16,2,240]{2,1,0:T(2,128)} %broadcast_in_dim.40), calls=%async_computation.5 | async-start | bytes 65536 | tf_op jit(solution)/shard_map/all_to_all | solution.py:120
Sparse Core Ops, SparseCore 0:
  79.9 68.0 all-gather.4

commit v3 on v2

v3 whole, which is shorter than its diff:
```python
import jax
import jax.numpy as jnp
from jax import lax
from jax.experimental import pallas as pl
from jax.experimental.pallas import tpu as pltpu
from jax.sharding import Mesh, PartitionSpec as P

HD = 120
NY = 4
CHUNKS = 16
BF = jnp.bfloat16
F32 = jnp.float32
VMEM = pl.BlockSpec(memory_space=pltpu.VMEM)
SMEM = pl.BlockSpec(memory_space=pltpu.SMEM)


def plane_gather(block):
    count = lax.axis_size("x") * lax.axis_size("y")
    spread = jnp.broadcast_to(block[None], (count,) + block.shape)
    return lax.all_to_all(spread, ("x", "y"), 0, 0)


def swap_cores(value):
    return lax.ppermute(value, "c", [(0, 1), (1, 0)])


def matmul(left, right, contract_right=0):
    return lax.dot_general(
        left, right, (((1,), (contract_right,)), ((), ())), preferred_element_type=F32
    )


def normalize(values, gain, along):
    values = values.astype(F32)
    width = CHUNKS * HD
    mean = jnp.sum(jnp.sum(values, axis=0, keepdims=True), axis=along, keepdims=True) / width
    centered = values - mean
    var = jnp.sum(jnp.sum(centered * centered, axis=0, keepdims=True), axis=along, keepdims=True)
    return (centered * lax.rsqrt(var / width + 1e-05) * gain).astype(BF)


def project(normed_ref, weight_ref, index, out_ref, slot, contract):
    total = jnp.zeros((HD, 256), F32)
    for b in range(CHUNKS):
        total += matmul(weight_ref[b, index], normed_ref[b], contract)
    out_ref[slot] = total.astype(BF)


def frame_of(place, core):
    return jnp.where(place < 64, place + core * 64, place - core * 64)


def attend(qkv_ref, u, core, length):
    columns = slice(u * 128, u * 128 + 128)
    keys = qkv_ref[1, :, columns].astype(F32).T.astype(BF)
    scores = matmul(keys, qkv_ref[0, :, columns]) / jnp.sqrt(F32(HD))
    place = lax.broadcasted_iota(jnp.int32, (128, 128), 0)
    scores = jnp.where(frame_of(place, core) < length, scores, F32(-1e30))
    top = jnp.max(scores, axis=0, keepdims=True)
    grown = jnp.exp(scores - top)
    probs = (grown / jnp.sum(grown, axis=0, keepdims=True)).astype(BF)
    return matmul(qkv_ref[2, :, columns], probs).astype(BF)


def first_kernel(scalars, raw, swapped, own, other, gain, partial, kept, normed, qkv, context):
    core = scalars[0]
    xi, yi = scalars[1], scalars[2]
    for u in range(2):
        for h in range(2):
            rows = slice(u * 128 + h * 64, u * 128 + h * 64 + 64)
            picks = [raw[x, 2 * core + u] if h == 0 else swapped[x, u] for x in range(4)]
            values = jnp.concatenate(picks, axis=0)
            normed[:, rows, :] = normalize(values, gain[...], 2)
        low = raw[xi, 2 * core + u, yi].astype(F32)
        high = swapped[xi, u, yi].astype(F32)
        both = jnp.concatenate([low, high], axis=0)
        kept[:, u * 128 : u * 128 + 128] = both.T.astype(BF)

    def qkv_from(low, high):
        project(normed, low, 0, qkv, 0, 1)
        project(normed, low, 1, qkv, 1, 1)
        project(normed, high, 0, qkv, 2, 1)

    def out_from(high):
        for b in range(CHUNKS):
            partial[b] = matmul(high[b, 1], context[...]).astype(BF)

    pl.when(core == 0)(lambda: qkv_from(own, other))
    pl.when(core == 1)(lambda: qkv_from(other, own))
    for u in range(2):
        context[:, u * 128 : u * 128 + 128] = attend(qkv, u, core, scalars[3 + u])
    pl.when(core == 0)(lambda: out_from(other))
    pl.when(core == 1)(lambda: out_from(own))


def second_kernel(scalars, x1, weights, gain, pooled, normed, qkv):
    core = scalars[0]
    for part in range(2):
        columns = slice(part * 128, part * 128 + 128)
        normed[:, :, columns] = normalize(x1[:, :, columns], gain[...], 1)
    for index in range(3):
        project(normed, weights, index, qkv, index, 0)
    for u in range(2):
        length = scalars[3 + u]
        context = attend(qkv, u, core, length).astype(F32)
        place = lax.broadcasted_iota(jnp.int32, (HD, 128), 1)
        valid = frame_of(place, core) < length
        total = jnp.sum(jnp.where(valid, context, F32(0.0)), axis=1, keepdims=True)
        pooled[:, u : u + 1] = total / length.astype(F32)


def run_first(scalars, raw, swapped, own, other, gain):
    return pl.pallas_call(
        first_kernel,
        out_shape=(
            jax.ShapeDtypeStruct((CHUNKS, HD, 256), BF),
            jax.ShapeDtypeStruct((HD, 256), BF),
        ),
        in_specs=[SMEM] + [VMEM] * 5,
        out_specs=(VMEM, VMEM),
        scratch_shapes=[
            pltpu.VMEM((CHUNKS, 256, HD), BF),
            pltpu.VMEM((3, HD, 256), BF),
            pltpu.VMEM((HD, 256), BF),
        ],
        compiler_params=pltpu.CompilerParams(vmem_limit_bytes=20 << 20),
        cost_estimate=pl.CostEstimate(
            flops=1_000_000_000, bytes_accessed=6_000_000, transcendentals=32768
        ),
        name="first_layer",
    )(scalars, raw, swapped, own, other, gain)


def run_second(scalars, x1, weights, gain):
    return pl.pallas_call(
        second_kernel,
        out_shape=jax.ShapeDtypeStruct((HD, 2), F32),
        in_specs=[SMEM] + [VMEM] * 3,
        out_specs=VMEM,
        scratch_shapes=[
            pltpu.VMEM((CHUNKS, HD, 256), BF),
            pltpu.VMEM((3, HD, 256), BF),
        ],
        compiler_params=pltpu.CompilerParams(vmem_limit_bytes=20 << 20),
        cost_estimate=pl.CostEstimate(
            flops=1_000_000_000, bytes_accessed=6_000_000, transcendentals=32768
        ),
        name="second_layer",
    )(scalars, x1, weights, gain)


def body(frames, lengths, feature_proj, norm_gain, qkv_weight, out_weight, center, whitening):
    core = lax.axis_index("c")
    xi, yi = lax.axis_index("x"), lax.axis_index("y")
    chunk = xi * NY + yi
    half = frames.shape[1] // 2

    qkv = qkv_weight[0].reshape(30, 3, NY, HD).transpose(2, 1, 0, 3)
    out = out_weight[0].T.reshape(30, NY, HD).transpose(1, 0, 2)[:, None]
    mats = jnp.concatenate([qkv, out], axis=1)
    tail = jnp.broadcast_to(lengths[0].astype(BF), (NY, 4, 2, HD))
    mats = jnp.concatenate([mats, tail], axis=2)
    mats = jnp.broadcast_to(mats[:, None], (NY, 2, 4, 32, HD)).reshape(2 * NY, 4, 32, HD)
    regrouped = lax.all_to_all(mats, ("y", "c"), 0, 0).reshape(NY, 2, 4, 32, HD)
    plane_lengths = regrouped[:, 0, 0, 30, 0].astype(jnp.int32)
    my_lengths = lax.dynamic_slice_in_dim(plane_lengths, 2 * core, 2, 0)
    gains = lax.all_gather(norm_gain[0], "c", axis=0)

    def shard(layer):
        rows = regrouped[:, layer, :, :30].transpose(1, 0, 2, 3).reshape(4, HD, HD)
        return jnp.concatenate([rows[:3].transpose(0, 2, 1), rows[3:]], axis=0)

    first_shard = lax.dynamic_slice_in_dim(shard(0), 2 * core, 2, 0)
    first_shard, second_shard, gains, my_lengths = lax.optimization_barrier(
        (first_shard, shard(1), gains, my_lengths)
    )
    second_weights = lax.all_gather(second_shard, "z", axis=0)
    own = lax.all_gather(first_shard, "z", axis=0)
    other = swap_cores(own)

    own_half = lax.dynamic_slice_in_dim(frames[0], core * half, half, 0)
    projected = jnp.dot(own_half, feature_proj, preferred_element_type=F32).astype(BF)
    projected = projected.reshape(half, NY, HD).transpose(1, 0, 2)
    raw = plane_gather(projected).reshape(4, NY, NY, half, HD)
    theirs = lax.dynamic_slice_in_dim(raw, 2 * (1 - core), 2, 1)
    swapped = swap_cores(theirs)

    scalars = jnp.concatenate([jnp.stack([core, xi, yi]).astype(jnp.int32), my_lengths])
    first_gain = gains[0].reshape(CHUNKS, 1, HD)
    second_gain = gains[1].reshape(CHUNKS, HD, 1)
    partial, x0_own = run_first(scalars, raw, swapped, own, other, first_gain)

    white = whitening.T.reshape(16, CHUNKS, HD).transpose(1, 0, 2)
    partial, white = lax.optimization_barrier((partial, white))
    whites = [white]
    for step in range(1, NY):
        pairs = [((i + step) % NY, i) for i in range(NY)]
        whites.append(lax.ppermute(white, "y", pairs))

    partial = lax.all_to_all(partial, ("x", "y"), 0, 0)
    attended = jnp.sum(partial.astype(F32), axis=0)
    x1_own = (x0_own.astype(F32) + attended).astype(BF)
    x1 = plane_gather(x1_own)

    frame_ids = jnp.concatenate(
        [core * half + jnp.arange(half), (1 - core) * half + jnp.arange(half)]
    )
    valid = frame_ids[None, :] < my_lengths[:, None]
    share = valid.astype(F32) / my_lengths.astype(F32)[:, None]
    pooled_x1 = jnp.sum(x1_own.reshape(HD, 2, 128).astype(F32) * share, axis=2).T
    white_cols = jnp.concatenate([w[None] for w in whites], axis=0)
    out_white = jnp.einsum(
        "ybnc,bcr->ynr",
        white_cols,
        second_weights[:, 3].astype(F32),
        precision=lax.Precision.HIGHEST,
    )
    white_own = lax.dynamic_index_in_dim(white_cols, chunk, 1, keepdims=False)
    mixed = jnp.concatenate([out_white, white_own], axis=2)
    mixed = jnp.concatenate([mixed, mixed], axis=0)
    mixed = lax.dynamic_slice_in_dim(mixed, (NY - yi) % NY, NY, 0).reshape(64, 2 * HD)

    pooled_context = run_second(scalars, x1, second_weights, second_gain).T
    center_own = lax.dynamic_index_in_dim(center.reshape(CHUNKS, HD), chunk, 0, keepdims=False)
    packed = jnp.concatenate([pooled_context, pooled_x1 - center_own], axis=1)
    packed = jnp.broadcast_to(packed[None], (16,) + packed.shape)
    packed = lax.all_to_all(packed, "z", 0, 0).reshape(32, 2 * HD)
    part = jnp.einsum("tk,nk->nt", packed, mixed, precision=lax.Precision.HIGHEST)
    part = jnp.broadcast_to(part.reshape(NY, 1, 16, 32), (NY, 8, 16, 32)).reshape(32, 16, 32)
    part = lax.all_to_all(part, ("y", "c", "x"), 0, 0).reshape(NY, 2, 4, 16, 32)
    total = jnp.sum(part, axis=(0, 2))
    return total.reshape(2, 16, 16, 2).transpose(2, 0, 3, 1).reshape(64, 16)


def solution(mesh):
    devices = mesh.devices.reshape(-1, NY, 2, 4)
    split = Mesh(devices, ("z", "y", "c", "x"))
    dp = ("z", "y")
    in_specs = (
        P(dp, None, None),
        P(dp),
        P(None, "x"),
        P("c", None),
        P("c", dp, "x"),
        P("c", "x", dp),
        P(),
        P(None, dp),
    )
    return jax.shard_map(
        body, mesh=split, in_specs=in_specs, out_specs=P(None, dp), check_vma=False
    )
```

time: 201 us -> 184 us (0.915)
  waiting for transfers between devices: 54.7 us -> 39.6 us
  matrix products: 12.7 us -> 2.12 us
  starting transfers between devices: 39.6 us -> 47.7 us
  Pallas kernels: 0 us -> 7.85 us
  other arithmetic: 7.29 us -> 1.93 us
  local copies, waits for them, and re-layouts: 14.7 us -> 12.6 us
    all_to_all x2, waiting for transfers between devices: 11.6 us -> 0.01 us  [plane_gather(): return lax.all_to_all(spread, ('x', 'y'), 0, 0)]
    ppermute x0 -> x3, starting transfers between devices: none -> 10.1 us  [body(): whites.append(lax.ppermute(white, 'y', pairs))]
    dot_general x12 -> x1, matrix products: 11.6 us -> 1.57 us  [body(): jnp.einsum('ybnc,bcr->ynr', white_cols, second_weights[:, 3].astype(F32),...]
    pallas_call x0 -> x2, Pallas kernels: none -> 7.85 us  [the longest x1 4.95 us: run_first(): pl.pallas_call(first_kernel, out_shape=(jax.ShapeDtypeStruct((CHUNKS, HD,...]
    ppermute x0 -> x3, waiting for transfers between devices: none -> 7.15 us  [body(): whites.append(lax.ppermute(white, 'y', pairs))]
    all_gather x1, waiting for transfers between devices: 6.83 us -> 0.01 us  [body(): second_weights = lax.all_gather(second_shard, 'z', axis=0)]
    all_to_all x1 -> x0, waiting for transfers between devices: 4.78 us -> none  [body(): white_cols = lax.all_to_all(white_cols, 'y', 0, 0)]
    all_to_all x1 -> x0, starting transfers between devices: 4.37 us -> none  [body(): white_cols = lax.all_to_all(white_cols, 'y', 0, 0)]
  transfers between devices with their start and end apart: 9 -> 11, of which waited for: 6 -> 7; matrix products, arithmetic and copies ran while one was open for 11% -> 4% of each run, Pallas kernels for 0% -> 3%
where the time goes in v3:
time: 184 us; the launch traced here: 180 us
  blocking collectives  53.9 us (29%)
  starting transfers between devices  47.7 us (26%)
  waiting for transfers between devices  39.6 us (22%)
  between operations  14.5 us (8%)
  local copies, waits for them, and re-layouts  12.6 us (7%)
  Pallas kernels  7.85 us (4%)
  matrix products  2.12 us (1%)
  other arithmetic  1.93 us (1%)
    all_gather x1, blocking collectives, body(): own = lax.all_gather(first_shard, 'z', axis=0)  40.3 us
    all_to_all x1, waiting for transfers between devices, body(): partial = lax.all_to_all(partial, ('x', 'y'), 0, 0)  15 us
    all_to_all x2, starting transfers between devices, plane_gather(): return lax.all_to_all(spread, ('x', 'y'), 0, 0)  14.1 us
    all_to_all x1, blocking collectives, body(): part = lax.all_to_all(part, ('y', 'c', 'x'), 0, 0).reshape(NY, 2, 4, 16, 32)  11.6 us
    all_to_all x1, waiting for transfers between devices, body(): packed = lax.all_to_all(packed, 'z', 0, 0).reshape(32, 2 * HD)  11.1 us
    ppermute x3, starting transfers between devices, body(): whites.append(lax.ppermute(white, 'y', pairs))  10.1 us
    all_to_all x1, starting transfers between devices, body(): partial = lax.all_to_all(partial, ('x', 'y'), 0, 0)  8.21 us
    ppermute x3, waiting for transfers between devices, body(): whites.append(lax.ppermute(white, 'y', pairs))  7.15 us
  transfers between devices with their start and end apart: 11, of which 7 were waited for; matrix products, arithmetic and copies ran while one was open for 4% of the time, Pallas kernels for 3%

profile of v3, /device:TPU:6, one launch (start us, length us, event | category | flops | bytes accessed | tf_op | source)
XLA Modules:
  0.0 180.2 jit_solution(7932692215295318218)
XLA Ops:
  6.5 1.1 reshape_squeeze.9
  7.7 0.9 reshape.101
  10.1 4.5 %all-to-all-start = ((bf16[8,4,32,120]{3,2,1,0:T(8,128)(2,1)}), bf16[8,4,32,120]{3,2,1,0:T(8,128)(2,1)S(1)}, u32[]{:S(2)}, u32[]{:S(2)}) async-start(bf16[8,4,32,120]{3,2,1,0:T(8,128)(2,1)} %bitcast.10), calls=%async_computation | async-start | bytes 524288 | tf_op jit(solution)/shard_map/all_to_all | solution.py:164
  14.6 2.0 %all-gather.2 = f32[2,1,1920]{2,1,0:T(1,128)S(1)} all-gather(f32[1,1,1920]{2,1,0:T(1,128)S(1)} %bitcast.109), channel_id=1, replica_groups=mesh['z'=16,'y'=4,'c'=2,'x'=4] {'c'}, dimensions={0}, use_global_device_ids=true | all-gather | bytes 23040 | tf_op jit(solution)/shard_map/all_gather | solution.py:167
  17.0 5.1 %all-to-all-done = bf16[8,4,32,120]{3,2,1,0:T(8,128)(2,1)S(1)} async-done(((bf16[8,4,32,120]{3,2,1,0:T(8,128)(2,1)}), bf16[8,4,32,120]{3,2,1,0:T(8,128)(2,1)S(1)}, u32[]{:S(2)}, u32[]{:S(2)}) %all-to-all-start) | async-done | bytes 245792 | tf_op jit(solution)/shard_map/all_to_all | solution.py:164
  22.1 1.2 broadcast_in_dim.22
  23.4 8.2 %all-to-all-start.1 = ((bf16[16,4,64,120]{3,2,1,0:T(8,128)(2,1)}), bf16[16,4,64,120]{3,2,1,0:T(8,128)(2,1)S(1)}, u32[]{:S(2)}, u32[]{:S(2)}) async-start(bf16[16,4,64,120]{3,2,1,0:T(8,128)(2,1)} %broadcast_in_dim.22), calls=%async_computation.1 | async-start | bytes 2097152 | tf_op jit(solution)/shard_map/all_to_all | solution.py:20
  32.5 0.8 copy.114
  33.3 40.3 %all-gather = bf16[32,120,120]{2,1,0:T(8,128)(2,1)S(1)} all-gather(bf16[2,120,120]{2,1,0:T(8,128)(2,1)S(1)} %copy.109), channel_id=2, replica_groups=mesh['z'=16,'y'=4,'c'=2,'x'=4] {'z'}, dimensions={0}, use_global_device_ids=true | all-gather | bytes 979200 | tf_op jit(solution)/shard_map/all_gather | solution.py:178
  73.5 1.9 %collective-permute-start.1 = (bf16[16,2,120,120]{3,2,1,0:T(8,128)(2,1)S(1)}, bf16[16,2,120,120]{3,2,1,0:T(8,128)(2,1)}, u32[]{:S(2)}, u32[]{:S(2)}) collective-permute-start(bf16[16,2,120,120]{3,2,1,0:T(8,128)(2,1)S(1)} %bitcast.81), channel_id=1, source_target_pairs={{0,4},{4,0},{1,5},{5,1},{2,6},{6,2},{3,7},{7,3},{8,12},{12,8},{9,1... | collective-permute-start | bytes 2764808 | tf_op jit(solution)/shard_map/ppermute | solution.py:24
  75.5 0.9 constant_dynamic-slice_fusion.1
  76.3 2.4 %collective-permute-start = (bf16[4,2,4,64,120]{4,3,2,1,0:T(8,128)(2,1)}, bf16[4,2,4,64,120]{4,3,2,1,0:T(8,128)(2,1)S(1)}, u32[]{:S(2)}, u32[]{:S(2)}) collective-permute-start(bf16[4,2,4,64,120]{4,3,2,1,0:T(8,128)(2,1)} %constant_dynamic-slice_fusion.1), channel_id=1, source_target_pairs={{0,4},{4,0},{1,5},{5,1},{2,6},{6,2},{3,7},{7,3},{8,12},{12,8},{9,1... | collective-permute-start | bytes 1474568 | tf_op jit(solution)/shard_map/ppermute | solution.py:24
  79.2 1.3 collective-permute-done.swapped
  80.5 4.9 %first_layer.1 = (bf16[16,120,256]{2,1,0:T(8,128)(2,1)}, bf16[120,256]{1,0:T(8,128)(2,1)S(1)}) custom-call(s32[5]{0:T(128)S(1)} %pad_add_fusion.scalars, bf16[4,4,4,64,120]{4,3,2,1,0:T(8,128)(2,1)S(1)} %bitcast.78, bf16[4,2,4,64,120]{4,3,2,1,0:T(8,128)(2,1)S(1)} %collective-permute-done.swapped, bf16[16,2,120,120]{3,2,1,0:T(8,128)(2,1)S(1)} %bitcast.82, ...), custom_call_target="tpu_custom_call" | custom-call | flops 1000000000 | bytes 6000000 | tf_op jit(solution)/shard_map/first_layer/pallas_call | solution.py:113
  85.4 8.2 %all-to-all-start.2 = ((bf16[16,120,256]{2,1,0:T(8,128)(2,1)}), bf16[16,120,256]{2,1,0:T(8,128)(2,1)S(1)}, u32[]{:S(2)}, u32[]{:S(2)}) async-start(bf16[16,120,256]{2,1,0:T(8,128)(2,1)} %get-tuple-element.20), calls=%async_computation.2 | async-start | bytes 1966080 | tf_op jit(solution)/shard_map/all_to_all | solution.py:200
  93.8 15.0 %all-to-all-done.2 = bf16[16,120,256]{2,1,0:T(8,128)(2,1)S(1)} async-done(((bf16[16,120,256]{2,1,0:T(8,128)(2,1)}), bf16[16,120,256]{2,1,0:T(8,128)(2,1)S(1)}, u32[]{:S(2)}, u32[]{:S(2)}) %all-to-all-start.2) | async-done | bytes 983072 | tf_op jit(solution)/shard_map/all_to_all | solution.py:200
  109.0 1.0 broadcast_in_dim.27
  110.0 5.9 %all-to-all-start.3 = ((bf16[16,120,256]{2,1,0:T(8,128)(2,1)}), bf16[16,120,256]{2,1,0:T(8,128)(2,1)S(1)}, u32[]{:S(2)}, u32[]{:S(2)}) async-start(bf16[16,120,256]{2,1,0:T(8,128)(2,1)} %broadcast_in_dim.27), calls=%async_computation.3 | async-start | bytes 1966080 | tf_op jit(solution)/shard_map/all_to_all | solution.py:20
  115.9 0.8 reshape_squeeze.12.gain
  116.8 4.6 %collective-permute-start.2 = (f32[16,16,120]{2,1,0:T(8,128)S(1)}, f32[16,16,120]{2,1,0:T(8,128)S(1)}, u32[]{:S(2)}, u32[]{:S(2)}) collective-permute-start(f32[16,16,120]{2,1,0:T(8,128)S(1)} %bitcast.88), channel_id=1, source_target_pairs={{8,0},{16,8},{24,16},{0,24},{9,1},{17,9},{25,17},{1,25},{10,2},{18... | collective-permute-start | bytes 368648 | tf_op jit(solution)/shard_map/ppermute | solution.py:198
  121.4 2.8 %collective-permute-start.3 = (f32[16,16,120]{2,1,0:T(8,128)S(1)}, f32[16,16,120]{2,1,0:T(8,128)S(1)}, u32[]{:S(2)}, u32[]{:S(2)}) collective-permute-start(f32[16,16,120]{2,1,0:T(8,128)S(1)} %bitcast.89), channel_id=1, source_target_pairs={{16,0},{24,8},{0,16},{8,24},{17,1},{25,9},{1,17},{9,25},{18,2},{26... | collective-permute-start | bytes 368648 | tf_op jit(solution)/shard_map/ppermute | solution.py:198
  124.1 2.8 %collective-permute-start.4 = (f32[16,16,120]{2,1,0:T(8,128)S(1)}, f32[16,16,120]{2,1,0:T(8,128)S(1)}, u32[]{:S(2)}, u32[]{:S(2)}) collective-permute-start(f32[16,16,120]{2,1,0:T(8,128)S(1)} %bitcast.90), channel_id=1, source_target_pairs={{24,0},{0,8},{8,16},{16,24},{25,1},{1,9},{9,17},{17,25},{26,2},{2,... | collective-permute-start | bytes 368648 | tf_op jit(solution)/shard_map/ppermute | solution.py:198
  127.0 3.9 %collective-permute-done.2 = f32[16,16,120]{2,1,0:T(8,128)S(1)} collective-permute-done((f32[16,16,120]{2,1,0:T(8,128)S(1)}, f32[16,16,120]{2,1,0:T(8,128)S(1)}, u32[]{:S(2)}, u32[]{:S(2)}) %collective-permute-start.2) | collective-permute-done | bytes 122912 | tf_op jit(solution)/shard_map/ppermute | solution.py:198
  130.9 1.3 collective-permute-done.3
  132.3 1.9 %collective-permute-done.4 = f32[16,16,120]{2,1,0:T(8,128)S(1)} collective-permute-done((f32[16,16,120]{2,1,0:T(8,128)S(1)}, f32[16,16,120]{2,1,0:T(8,128)S(1)}, u32[]{:S(2)}, u32[]{:S(2)}) %collective-permute-start.4) | collective-permute-done | bytes 122912 | tf_op jit(solution)/shard_map/ppermute | solution.py:198
  134.7 1.5 copy-done.1
  136.2 2.9 %second_layer.1 = f32[120,2]{1,0:T(8,128)S(1)} custom-call(s32[5]{0:T(128)S(1)} %pad_add_fusion.scalars, bf16[16,120,256]{2,1,0:T(8,128)(2,1)S(1)} %all-to-all-done.3.x1, bf16[16,4,120,120]{3,2,1,0:T(8,128)(2,1)S(1)} %bitcast.80, f32[16,120,1]{2,1,0:T(8,128)S(1)} %reshape_squeeze.12.gain), custom_call_target="tpu_custom_call" | custom-call | flops 1000000000 | bytes 6000000 | tf_op jit(solution)/shard_map/second_layer/pallas_call | solution.py:135
  139.9 6.4 %all-to-all-start.4 = ((f32[16,2,240]{2,1,0:T(2,128)}), f32[16,2,240]{2,1,0:T(2,128)S(1)}, u32[]{:S(2)}, u32[]{:S(2)}) async-start(f32[16,2,240]{2,1,0:T(2,128)} %broadcast_in_dim.28), calls=%async_computation.4 | async-start | bytes 65536 | tf_op jit(solution)/shard_map/all_to_all | solution.py:227
  146.3 1.6 convolution_bitcast_fusion
  147.9 11.1 %all-to-all-done.4 = f32[16,2,240]{2,1,0:T(2,128)S(1)} async-done(((f32[16,2,240]{2,1,0:T(2,128)}), f32[16,2,240]{2,1,0:T(2,128)S(1)}, u32[]{:S(2)}, u32[]{:S(2)}) %all-to-all-start.4) | async-done | bytes 30752 | tf_op jit(solution)/shard_map/all_to_all | solution.py:227
  159.5 11.6 %all_to_all.30 = f32[32,1,512]{2,1,0:T(1,128)S(1)} all-to-all(f32[32,1,512]{2,1,0:T(1,128)S(1)} %reshape.125), channel_id=1, replica_groups=mesh['z'=16,'y'=4,'c'=2,'x'=4] {'y','c','x'}, dimensions={0} | all-to-all | bytes 131072 | tf_op jit(solution)/shard_map/all_to_all | solution.py:230
  171.6 0.8 reduce.6
  (76 shorter events, 6.1 us)
Async XLA Ops:
  6.5 10.1 %copy-start = (bf16[512,480]{0,1:T(8,128)(2,1)S(1)}, bf16[512,480]{0,1:T(8,128)(2,1)}, u32[]{:S(2)}) copy-start(bf16[512,480]{0,1:T(8,128)(2,1)} %param.10) | copy-start | bytes 1474564
  6.5 8.1 %copy-start.5 = (f32[1,1920]{1,0:T(1,128)S(1)}, f32[1,1920]{1,0:T(1,128)}, u32[]{:S(2)}) copy-start(f32[1,1920]{1,0:T(1,128)} %param.11) | copy-start | bytes 23044
  6.5 10.1 %copy-start.3 = (bf16[1,128,512]{2,1,0:T(8,128)(2,1)S(1)}, bf16[1,128,512]{2,1,0:T(8,128)(2,1)}, u32[]{:S(2)}) copy-start(bf16[1,128,512]{2,1,0:T(8,128)(2,1)} %param.8) | copy-start | bytes 393220
  10.1 12.0 %all-to-all-start = ((bf16[8,4,32,120]{3,2,1,0:T(8,128)(2,1)}), bf16[8,4,32,120]{3,2,1,0:T(8,128)(2,1)S(1)}, u32[]{:S(2)}, u32[]{:S(2)}) async-start(bf16[8,4,32,120]{3,2,1,0:T(8,128)(2,1)} %bitcast.10), calls=%async_computation | async-start | bytes 524288 | tf_op jit(solution)/shard_map/all_to_all | solution.py:164
  23.4 52.1 %all-to-all-start.1 = ((bf16[16,4,64,120]{3,2,1,0:T(8,128)(2,1)}), bf16[16,4,64,120]{3,2,1,0:T(8,128)(2,1)S(1)}, u32[]{:S(2)}, u32[]{:S(2)}) async-start(bf16[16,4,64,120]{3,2,1,0:T(8,128)(2,1)} %broadcast_in_dim.22), calls=%async_computation.1 | async-start | bytes 2097152 | tf_op jit(solution)/shard_map/all_to_all | solution.py:20
  31.6 103.0 %all-gather.5.cloned.1.call-start = ((), (), s32[]{:S(2)}) async-start(), calls=%async_computation.6 | async-start | bytes 2088960 | tf_op jit(solution)/shard_map/all_gather | solution.py:177
  31.8 47.0 %copy-start.2 = (f32[1920,16]{0,1:T(8,128)S(1)}, f32[1920,16]{0,1:T(8,128)}, u32[]{:S(2)}) copy-start(f32[1920,16]{0,1:T(8,128)} %param.15) | copy-start | bytes 368644
  73.5 5.7 %collective-permute-start.1 = (bf16[16,2,120,120]{3,2,1,0:T(8,128)(2,1)S(1)}, bf16[16,2,120,120]{3,2,1,0:T(8,128)(2,1)}, u32[]{:S(2)}, u32[]{:S(2)}) collective-permute-start(bf16[16,2,120,120]{3,2,1,0:T(8,128)(2,1)S(1)} %bitcast.81), channel_id=1, source_target_pairs={{0,4},{4,0},{1,5},{5,1},{2,6},{6,2},{3,7},{7,3},{8,12},{12,8},{9,1... | collective-permute-start | bytes 2764808 | tf_op jit(solution)/shard_map/ppermute | solution.py:24
  76.3 4.1 %collective-permute-start = (bf16[4,2,4,64,120]{4,3,2,1,0:T(8,128)(2,1)}, bf16[4,2,4,64,120]{4,3,2,1,0:T(8,128)(2,1)S(1)}, u32[]{:S(2)}, u32[]{:S(2)}) collective-permute-start(bf16[4,2,4,64,120]{4,3,2,1,0:T(8,128)(2,1)} %constant_dynamic-slice_fusion.1), channel_id=1, source_target_pairs={{0,4},{4,0},{1,5},{5,1},{2,6},{6,2},{3,7},{7,3},{8,12},{12,8},{9,1... | collective-permute-start | bytes 1474568 | tf_op jit(solution)/shard_map/ppermute | solution.py:24
  79.2 14.4 %copy-start.4 = (f32[1920]{0:T(1024)S(1)}, f32[1920]{0:T(1024)}, u32[]{:S(2)}) copy-start(f32[1920]{0:T(1024)} %param.14) | copy-start | bytes 23044
  85.4 23.4 %all-to-all-start.2 = ((bf16[16,120,256]{2,1,0:T(8,128)(2,1)}), bf16[16,120,256]{2,1,0:T(8,128)(2,1)S(1)}, u32[]{:S(2)}, u32[]{:S(2)}) async-start(bf16[16,120,256]{2,1,0:T(8,128)(2,1)} %get-tuple-element.20), calls=%async_computation.2 | async-start | bytes 1966080 | tf_op jit(solution)/shard_map/all_to_all | solution.py:200
  110.0 24.6 %all-to-all-start.3 = ((bf16[16,120,256]{2,1,0:T(8,128)(2,1)}), bf16[16,120,256]{2,1,0:T(8,128)(2,1)S(1)}, u32[]{:S(2)}, u32[]{:S(2)}) async-start(bf16[16,120,256]{2,1,0:T(8,128)(2,1)} %broadcast_in_dim.27), calls=%async_computation.3 | async-start | bytes 1966080 | tf_op jit(solution)/shard_map/all_to_all | solution.py:20
  116.8 14.2 %collective-permute-start.2 = (f32[16,16,120]{2,1,0:T(8,128)S(1)}, f32[16,16,120]{2,1,0:T(8,128)S(1)}, u32[]{:S(2)}, u32[]{:S(2)}) collective-permute-start(f32[16,16,120]{2,1,0:T(8,128)S(1)} %bitcast.88), channel_id=1, source_target_pairs={{8,0},{16,8},{24,16},{0,24},{9,1},{17,9},{25,17},{1,25},{10,2},{18... | collective-permute-start | bytes 368648 | tf_op jit(solution)/shard_map/ppermute | solution.py:198
  121.4 10.9 %collective-permute-start.3 = (f32[16,16,120]{2,1,0:T(8,128)S(1)}, f32[16,16,120]{2,1,0:T(8,128)S(1)}, u32[]{:S(2)}, u32[]{:S(2)}) collective-permute-start(f32[16,16,120]{2,1,0:T(8,128)S(1)} %bitcast.89), channel_id=1, source_target_pairs={{16,0},{24,8},{0,16},{8,24},{17,1},{25,9},{1,17},{9,25},{18,2},{26... | collective-permute-start | bytes 368648 | tf_op jit(solution)/shard_map/ppermute | solution.py:198
  124.1 10.0 %collective-permute-start.4 = (f32[16,16,120]{2,1,0:T(8,128)S(1)}, f32[16,16,120]{2,1,0:T(8,128)S(1)}, u32[]{:S(2)}, u32[]{:S(2)}) collective-permute-start(f32[16,16,120]{2,1,0:T(8,128)S(1)} %bitcast.90), channel_id=1, source_target_pairs={{24,0},{0,8},{8,16},{16,24},{25,1},{1,9},{9,17},{17,25},{26,2},{2,... | collective-permute-start | bytes 368648 | tf_op jit(solution)/shard_map/ppermute | solution.py:198
  134.7 1.6 copy-start.1
  139.9 19.0 %all-to-all-start.4 = ((f32[16,2,240]{2,1,0:T(2,128)}), f32[16,2,240]{2,1,0:T(2,128)S(1)}, u32[]{:S(2)}, u32[]{:S(2)}) async-start(f32[16,2,240]{2,1,0:T(2,128)} %broadcast_in_dim.28), calls=%async_computation.4 | async-start | bytes 65536 | tf_op jit(solution)/shard_map/all_to_all | solution.py:227
Sparse Core Ops, SparseCore 0:
  34.5 75.1 all-gather.4

commit v4 on v3

v4 whole, which is shorter than its diff:
```python
import jax
import jax.numpy as jnp
from jax import lax
from jax.experimental import pallas as pl
from jax.experimental.pallas import tpu as pltpu
from jax.sharding import Mesh, PartitionSpec as P

HD = 120
NY = 4
CHUNKS = 16
BF = jnp.bfloat16
F32 = jnp.float32
VMEM = pl.BlockSpec(memory_space=pltpu.VMEM)
SMEM = pl.BlockSpec(memory_space=pltpu.SMEM)


def plane_gather(block):
    count = lax.axis_size("x") * lax.axis_size("y")
    spread = jnp.broadcast_to(block[None], (count,) + block.shape)
    return lax.all_to_all(spread, ("x", "y"), 0, 0)


def swap_cores(value):
    return lax.ppermute(value, "c", [(0, 1), (1, 0)])


def matmul(left, right):
    return jnp.dot(left, right, preferred_element_type=F32)


def normalize(values, gain_rows, out_ref, columns):
    values = values.astype(F32)
    width = CHUNKS * HD
    mean = jnp.sum(jnp.sum(values, axis=0), axis=0, keepdims=True) / width
    centered = values - mean[None]
    var = jnp.sum(jnp.sum(centered * centered, axis=0), axis=0, keepdims=True) / width
    scale = lax.rsqrt(var + 1e-05)
    for b in range(CHUNKS):
        out_ref[b, :, columns] = (centered[b] * scale * gain_rows[:, b : b + 1]).astype(BF)


def project(normed_ref, weight_ref, index, out_ref, slot):
    total = jnp.zeros((HD, 256), F32)
    for b in range(CHUNKS):
        total += matmul(weight_ref[b, index], normed_ref[b])
    out_ref[slot] = total.astype(BF)


def attend(query, keys, values, length):
    keys = keys.astype(F32).T.astype(BF)
    scores = matmul(keys, query) / jnp.sqrt(F32(HD))
    place = lax.broadcasted_iota(jnp.int32, (128, 128), 0)
    scores = jnp.where(place < length, scores, F32(-1e30))
    top = jnp.max(scores, axis=0, keepdims=True)
    grown = jnp.exp(scores - top)
    probs = (grown / jnp.sum(grown, axis=0, keepdims=True)).astype(BF)
    return matmul(values, probs).astype(BF)


def utterance(u):
    return slice(u * 128, u * 128 + 128)


def norm_kernel(scalars, raw, own, gain, normed, mine):
    core = scalars[0]
    gain_rows = gain[...].T
    for u in range(2):
        picks = [raw[x, 2 * core + u] for x in range(4)]
        values = jnp.concatenate(picks, axis=0)
        normalize(values, gain_rows, normed, utterance(u))
    project(normed, own, 0, mine, 0)
    pl.when(core == 0)(lambda: project(normed, own, 1, mine, 1))


def attend_kernel(scalars, raw, normed, mine, own, other, partial, kept, rest, context):
    core = scalars[0]
    xi, yi = scalars[1], scalars[2]
    for u in range(2):
        kept[:, utterance(u)] = raw[xi, 2 * core + u, yi]

    def attend_all(query, keys, values):
        for u in range(2):
            columns = utterance(u)
            context[:, columns] = attend(
                query[:, columns], keys[:, columns], values[:, columns], scalars[3 + u]
            )

    def out_from(high):
        for b in range(CHUNKS):
            partial[b] = matmul(high[b, 1], context[...]).astype(BF)

    def on_first():
        project(normed, other, 0, rest, 0)
        attend_all(mine.at[0], mine.at[1], rest.at[0])
        out_from(other)

    def on_second():
        project(normed, other, 0, rest, 0)
        project(normed, other, 1, rest, 1)
        attend_all(rest.at[0], rest.at[1], mine.at[0])
        out_from(own)

    pl.when(core == 0)(on_first)
    pl.when(core == 1)(on_second)


def second_kernel(scalars, x1, weights_hbm, gain, pooled, weights, normed, qkv, arrived):
    copy = pltpu.make_async_copy(weights_hbm.at[:, pl.ds(0, 3)], weights, arrived)
    copy.start()
    gain_rows = gain[...].T
    for u in range(2):
        normalize(x1[:, :, utterance(u)], gain_rows, normed, utterance(u))
    copy.wait()
    for index in range(3):
        project(normed, weights, index, qkv, index)
    for u in range(2):
        length = scalars[3 + u]
        columns = utterance(u)
        context = attend(qkv[0, :, columns], qkv[1, :, columns], qkv[2, :, columns], length)
        valid = lax.broadcasted_iota(jnp.int32, (HD, 128), 1) < length
        total = jnp.where(valid, context.astype(F32), F32(0.0))
        pooled[:, u : u + 1] = jnp.sum(total, axis=1, keepdims=True) / length.astype(F32)


def cost(flops, moved):
    return pl.CostEstimate(flops=flops, bytes_accessed=moved, transcendentals=32768)


def run_norm(scalars, raw, own, gain):
    return pl.pallas_call(
        norm_kernel,
        out_shape=(
            jax.ShapeDtypeStruct((CHUNKS, HD, 256), BF),
            jax.ShapeDtypeStruct((2, HD, 256), BF),
        ),
        in_specs=[SMEM] + [VMEM] * 3,
        out_specs=(VMEM, VMEM),
        compiler_params=pltpu.CompilerParams(vmem_limit_bytes=20 << 20),
        cost_estimate=cost(400_000_000, 4_000_000),
        name="first_norm",
    )(scalars, raw, own, gain)


def run_attend(scalars, raw, normed, mine, own, other):
    return pl.pallas_call(
        attend_kernel,
        out_shape=(
            jax.ShapeDtypeStruct((CHUNKS, HD, 256), BF),
            jax.ShapeDtypeStruct((HD, 256), BF),
        ),
        in_specs=[SMEM] + [VMEM] * 5,
        out_specs=(VMEM, VMEM),
        scratch_shapes=[
            pltpu.VMEM((2, HD, 256), BF),
            pltpu.VMEM((HD, 256), BF),
        ],
        compiler_params=pltpu.CompilerParams(vmem_limit_bytes=20 << 20),
        cost_estimate=cost(600_000_000, 5_000_000),
        name="first_attend",
    )(scalars, raw, normed, mine, own, other)


def run_second(scalars, x1, weights, gain):
    return pl.pallas_call(
        second_kernel,
        out_shape=jax.ShapeDtypeStruct((HD, 2), F32),
        in_specs=[SMEM, VMEM, pl.BlockSpec(memory_space=pltpu.HBM), VMEM],
        out_specs=VMEM,
        scratch_shapes=[
            pltpu.VMEM((CHUNKS, 3, HD, HD), BF),
            pltpu.VMEM((CHUNKS, HD, 256), BF),
            pltpu.VMEM((3, HD, 256), BF),
            pltpu.SemaphoreType.DMA,
        ],
        compiler_params=pltpu.CompilerParams(vmem_limit_bytes=58 << 20),
        cost_estimate=cost(1_000_000_000, 6_000_000),
        name="second_layer",
    )(scalars, x1, weights, gain)


def body(frames, lengths, feature_proj, norm_gain, qkv_weight, out_weight, center, whitening):
    core = lax.axis_index("c")
    xi, yi = lax.axis_index("x"), lax.axis_index("y")
    chunk = xi * NY + yi

    white_cols = jnp.pad(whitening.T, ((0, 24), (0, 0)))
    white_cols = lax.all_gather(white_cols, "y", axis=0)[:, :16].reshape(NY, 16, CHUNKS, HD)

    projected = lax.dot_general(
        feature_proj, frames[0], (((0,), (1,)), ((), ())), preferred_element_type=F32
    )
    projected = projected.astype(BF).reshape(1, NY, HD, 128)
    projected = jnp.broadcast_to(projected, (16, NY, HD, 128))

    qkv = qkv_weight[0].reshape(30, 3, NY, HD).transpose(2, 1, 0, 3)
    out = out_weight[0].T.reshape(30, NY, HD).transpose(1, 0, 2)[:, None]
    mats = jnp.concatenate([qkv, out], axis=1)
    tail = jnp.broadcast_to(lengths[0].astype(BF), (NY, 4, 2, HD))
    mats = jnp.concatenate([mats, tail], axis=2)
    mats = jnp.broadcast_to(mats[:, None], (NY, 2, 4, 32, HD)).reshape(2 * NY, 4, 32, HD)
    regrouped = lax.all_to_all(mats, ("y", "c"), 0, 0).reshape(NY, 2, 4, 32, HD)
    gains = lax.all_gather(norm_gain[0], "c", axis=0)
    regrouped, gains, projected = lax.optimization_barrier((regrouped, gains, projected))
    plane_lengths = regrouped[:, 0, 0, 30, 0].astype(jnp.int32)
    my_lengths = lax.dynamic_slice_in_dim(plane_lengths, 2 * core, 2, 0)

    def shard(layer):
        rows = regrouped[:, layer, :, :30].transpose(1, 0, 2, 3).reshape(4, HD, HD)
        return jnp.concatenate([rows[:3].transpose(0, 2, 1), rows[3:]], axis=0)

    first_shard = lax.dynamic_slice_in_dim(shard(0), 2 * core, 2, 0)
    first_shard, second_shard, my_lengths = lax.optimization_barrier(
        (first_shard, shard(1), my_lengths)
    )
    second_weights = lax.all_gather(second_shard, "z", axis=0)
    own = lax.all_gather(first_shard, "z", axis=0)
    other = swap_cores(own)

    raw = lax.all_to_all(projected, ("x", "y"), 0, 0).reshape(4, NY, NY, HD, 128)

    scalars = jnp.concatenate([jnp.stack([core, xi, yi]).astype(jnp.int32), my_lengths])
    gains = gains.reshape(2, CHUNKS, HD)
    normed, mine = run_norm(scalars, raw, own, gains[0])
    partial, x0_own = run_attend(scalars, raw, normed, mine, own, other)
    partial = lax.all_to_all(partial, ("x", "y"), 0, 0)
    attended = jnp.sum(partial.astype(F32), axis=0)
    x1_own = (x0_own.astype(F32) + attended).astype(BF)
    x1 = plane_gather(x1_own)

    valid = jnp.arange(128)[None, :] < my_lengths[:, None]
    share = valid.astype(F32) / my_lengths.astype(F32)[:, None]
    pooled_x1 = jnp.sum(x1_own.reshape(HD, 2, 128).astype(F32) * share, axis=2).T
    out_white = jnp.einsum(
        "ynbc,bcr->ynr",
        white_cols,
        second_weights[:, 3].astype(F32),
        precision=lax.Precision.HIGHEST,
    )
    white_own = lax.dynamic_index_in_dim(white_cols, chunk, 2, keepdims=False)
    mixed = jnp.concatenate([out_white, white_own], axis=2).reshape(64, 2 * HD)

    pooled_context = run_second(scalars, x1, second_weights, gains[1]).T
    center_own = lax.dynamic_index_in_dim(center.reshape(CHUNKS, HD), chunk, 0, keepdims=False)
    packed = jnp.concatenate([pooled_context, pooled_x1 - center_own], axis=1)
    packed = jnp.broadcast_to(packed[None], (16,) + packed.shape)
    packed = lax.all_to_all(packed, "z", 0, 0).reshape(32, 2 * HD)
    part = jnp.einsum("tk,nk->nt", packed, mixed, precision=lax.Precision.HIGHEST)
    part = jnp.broadcast_to(part.reshape(NY, 1, 16, 32), (NY, 8, 16, 32)).reshape(32, 16, 32)
    part = lax.all_to_all(part, ("y", "c", "x"), 0, 0).reshape(NY, 2, 4, 16, 32)
    total = jnp.sum(part, axis=(0, 2))
    return total.reshape(2, 16, 16, 2).transpose(2, 0, 3, 1).reshape(64, 16)


def solution(mesh):
    devices = mesh.devices.reshape(-1, NY, 2, 4)
    split = Mesh(devices, ("z", "y", "c", "x"))
    dp = ("z", "y")
    in_specs = (
        P(dp, None, None),
        P(dp),
        P(None, "x"),
        P("c", None),
        P("c", dp, "x"),
        P("c", "x", dp),
        P(),
        P(None, dp),
    )
    return jax.shard_map(
        body, mesh=split, in_specs=in_specs, out_specs=P(None, dp), check_vma=False
    )
```

time: 184 us -> 197 us (1.071)
  blocking collectives: 53.9 us -> 75.8 us
  starting transfers between devices: 47.7 us -> 27.5 us
  waiting for transfers between devices: 39.6 us -> 46.4 us
  local copies, waits for them, and re-layouts: 12.6 us -> 15 us
  Pallas kernels: 7.85 us -> 9.92 us
    all_gather x1, waiting for transfers between devices: 0.01 us -> 30 us  [body(): second_weights = lax.all_gather(second_shard, 'z', axis=0)]
    all_to_all x0 -> x1, blocking collectives: none -> 21.6 us  [body(): partial = lax.all_to_all(partial, ('x', 'y'), 0, 0)]
    all_to_all x1, waiting for transfers between devices: 15 us -> 0.01 us  [body(): lax.all_to_all(projected, ('x', 'y'), 0, 0).reshape(4, NY, NY, HD, 128)]
    ppermute x3 -> x0, starting transfers between devices: 10.1 us -> none  [body(): whites.append(lax.ppermute(white, 'y', pairs))]
    all_to_all x2 -> x1, starting transfers between devices: 14.1 us -> 5.49 us  [plane_gather(): return lax.all_to_all(spread, ('x', 'y'), 0, 0)]
    ppermute x3 -> x0, waiting for transfers between devices: 7.15 us -> none  [body(): whites.append(lax.ppermute(white, 'y', pairs))]
    ppermute x2 -> x1, starting transfers between devices: 4.3 us -> 1.91 us  [swap_cores(): return lax.ppermute(value, 'c', [(0, 1), (1, 0)])]
    all_to_all x1, blocking collectives: 11.6 us -> 13.6 us  [body(): part = lax.all_to_all(part, ('y', 'c', 'x'), 0, 0).reshape(NY, 2, 4, 16, 32)]
  transfers between devices with their start and end apart: 11 -> 7, of which waited for: 7 -> 4; matrix products, arithmetic and copies ran while one was open for 4% -> 6% of each run, Pallas kernels for 3% -> 3%
where the time goes in v4:
time: 197 us; the launch traced here: 193 us
  blocking collectives  75.8 us (38%)
  waiting for transfers between devices  46.4 us (24%)
  starting transfers between devices  27.5 us (14%)
  local copies, waits for them, and re-layouts  15 us (8%)
  between operations  14.5 us (7%)
  Pallas kernels  9.92 us (5%)
  matrix products  2.25 us (1%)
    all_gather x1, blocking collectives, body(): own = lax.all_gather(first_shard, 'z', axis=0)  38.6 us
    all_gather x1, waiting for transfers between devices, body(): second_weights = lax.all_gather(second_shard, 'z', axis=0)  30 us
    all_to_all x1, blocking collectives, body(): partial = lax.all_to_all(partial, ('x', 'y'), 0, 0)  21.6 us
    all_to_all x1, blocking collectives, body(): part = lax.all_to_all(part, ('y', 'c', 'x'), 0, 0).reshape(NY, 2, 4, 16, 32)  13.6 us
    all_to_all x1, waiting for transfers between devices, body(): packed = lax.all_to_all(packed, 'z', 0, 0).reshape(32, 2 * HD)  10.9 us
    all_to_all x1, starting transfers between devices, body(): lax.all_to_all(projected, ('x', 'y'), 0, 0).reshape(4, NY, NY, HD, 128)  8.3 us
    all_to_all x1, starting transfers between devices, body(): packed = lax.all_to_all(packed, 'z', 0, 0).reshape(32, 2 * HD)  7.28 us
    all_to_all x1, starting transfers between devices, plane_gather(): return lax.all_to_all(spread, ('x', 'y'), 0, 0)  5.49 us
  transfers between devices with their start and end apart: 7, of which 4 were waited for; matrix products, arithmetic and copies ran while one was open for 6% of the time, Pallas kernels for 3%

profile of v4, /device:TPU:6, one launch (start us, length us, event | category | flops | bytes accessed | tf_op | source)
XLA Modules:
  0.0 193.2 jit_solution(14347667393264281739)
XLA Ops:
  6.5 1.7 pad.5
  8.3 1.1 reshape_squeeze.3
  9.3 0.9 reshape.102
  11.1 0.8 broadcast_in_dim.15
  11.8 4.5 %all-to-all-start = ((bf16[8,4,32,120]{3,2,1,0:T(8,128)(2,1)}), bf16[8,4,32,120]{3,2,1,0:T(8,128)(2,1)S(1)}, u32[]{:S(2)}, u32[]{:S(2)}) async-start(bf16[8,4,32,120]{3,2,1,0:T(8,128)(2,1)} %bitcast.9), calls=%async_computation | async-start | bytes 524288 | tf_op jit(solution)/shard_map/all_to_all | solution.py:201
  16.3 2.0 %all-gather.3 = f32[2,1,1920]{2,1,0:T(1,128)S(1)} all-gather(f32[1,1,1920]{2,1,0:T(1,128)S(1)} %bitcast.91), channel_id=1, replica_groups=mesh['z'=16,'y'=4,'c'=2,'x'=4] {'c'}, dimensions={0}, use_global_device_ids=true | all-gather | bytes 23040 | tf_op jit(solution)/shard_map/all_gather | solution.py:202
  18.6 5.2 %all-to-all-done = bf16[8,4,32,120]{3,2,1,0:T(8,128)(2,1)S(1)} async-done(((bf16[8,4,32,120]{3,2,1,0:T(8,128)(2,1)}), bf16[8,4,32,120]{3,2,1,0:T(8,128)(2,1)S(1)}, u32[]{:S(2)}, u32[]{:S(2)}) %all-to-all-start) | async-done | bytes 245792 | tf_op jit(solution)/shard_map/all_to_all | solution.py:201
  23.8 1.5 broadcast_in_dim.17
  25.3 8.3 %all-to-all-start.1 = ((bf16[16,4,120,128]{3,2,1,0:T(8,128)(2,1)}), bf16[16,4,120,128]{3,2,1,0:T(8,128)(2,1)S(1)}, u32[]{:S(2)}, u32[]{:S(2)}) async-start(bf16[16,4,120,128]{3,2,1,0:T(8,128)(2,1)} %broadcast_in_dim.17), calls=%async_computation.1 | async-start | bytes 3932160 | tf_op jit(solution)/shard_map/all_to_all | solution.py:219
  34.5 0.8 copy.67
  35.3 38.6 %all-gather.2 = bf16[32,120,120]{2,1,0:T(8,128)(2,1)S(1)} all-gather(bf16[2,120,120]{2,1,0:T(8,128)(2,1)S(1)} %copy.69), channel_id=4, replica_groups=mesh['z'=16,'y'=4,'c'=2,'x'=4] {'z'}, dimensions={0}, use_global_device_ids=true | all-gather | bytes 979200 | tf_op jit(solution)/shard_map/all_gather | solution.py:216
  73.9 1.9 collective-permute-start
  76.0 2.2 %first_norm.1 = (bf16[16,120,256]{2,1,0:T(8,128)(2,1)S(1)}, bf16[2,120,256]{2,1,0:T(8,128)(2,1)S(1)}) custom-call(s32[5]{0:T(128)S(1)} %pad_add_fusion.scalars, bf16[4,4,4,120,128]{4,3,2,1,0:T(8,128)(2,1)S(1)} %bitcast.67, bf16[16,2,120,120]{3,2,1,0:T(8,128)(2,1)S(1)} %bitcast.70, f32[16,120]{1,0:T(8,128)S(1)} %squeeze.32.gain), custom_call_target="tpu_custom_call" | custom-call | flops 400000000 | bytes 4000000 | tf_op jit(solution)/shard_map/first_norm/pallas_call | solution.py:130
  78.5 2.9 %first_attend.1 = (bf16[16,120,256]{2,1,0:T(8,128)(2,1)S(1)}, bf16[120,256]{1,0:T(8,128)(2,1)S(1)}) custom-call(s32[5]{0:T(128)S(1)} %pad_add_fusion.scalars, bf16[4,4,4,120,128]{4,3,2,1,0:T(8,128)(2,1)S(1)} %bitcast.68, bf16[16,120,256]{2,1,0:T(8,128)(2,1)S(1)} %get-tuple-element.21.normed, bf16[2,120,256]{2,1,0:T(8,128)(2,1)S(1)} %get-tuple-element.22.mine, ...), custom_call_target="tpu_custom_call" | custom-call | flops 600000000 | bytes 5000000 | tf_op jit(solution)/shard_map/first_attend/pallas_call | solution.py:145
  81.4 21.6 %all_to_all.30 = bf16[16,120,256]{2,1,0:T(8,128)(2,1)S(1)} all-to-all(bf16[16,120,256]{2,1,0:T(8,128)(2,1)S(1)} %get-tuple-element.24), channel_id=1, replica_groups=mesh['z'=16,'y'=4,'c'=2,'x'=4] {'x','y'}, dimensions={0} | all-to-all | bytes 1966080 | tf_op jit(solution)/shard_map/all_to_all | solution.py:225
  103.1 1.0 broadcast_in_dim.18
  104.2 5.5 %all-to-all-start.3 = ((bf16[16,120,256]{2,1,0:T(8,128)(2,1)}), bf16[16,120,256]{2,1,0:T(8,128)(2,1)S(1)}, u32[]{:S(2)}, u32[]{:S(2)}) async-start(bf16[16,120,256]{2,1,0:T(8,128)(2,1)} %broadcast_in_dim.18), calls=%async_computation.3 | async-start | bytes 1966080 | tf_op jit(solution)/shard_map/all_to_all | solution.py:20
  109.8 0.7 squeeze.33.gain
  110.5 1.1 slice.62
  111.6 0.5 reshape.101
  112.6 30.0 %all-gather.9.cloned.1.call-done = bf16[64,120,120]{2,1,0:T(8,128)(2,1)} async-done(((bf16[4,120,120]{2,1,0:T(8,128)(2,1)}), bf16[64,120,120]{2,1,0:T(8,128)(2,1)}) %all-gather.9.cloned.1.call-update) | async-done | bytes 1843216 | tf_op jit(solution)/shard_map/all_gather | solution.py:215
  142.6 1.0 copy-done.2
  143.6 4.8 %second_layer.1 = f32[120,2]{1,0:T(8,128)} custom-call(s32[5]{0:T(128)} %copy-done.1, bf16[16,120,256]{2,1,0:T(8,128)(2,1)} %copy-done.2, bf16[16,4,120,120]{3,2,1,0:T(8,128)(2,1)} %bitcast.84, f32[16,120]{1,0:T(8,128)} %squeeze.33.gain), custom_call_target="tpu_custom_call" | custom-call | flops 1000000000 | bytes 6000000 | tf_op jit(solution)/shard_map/second_layer/pallas_call | solution.py:164
  148.5 0.9 copy.70
  149.4 0.6 broadcast_in_dim.19
  150.1 7.3 %all-to-all-start.4 = ((f32[16,2,240]{2,1,0:T(2,128)}), f32[16,2,240]{2,1,0:T(2,128)S(1)}, u32[]{:S(2)}, u32[]{:S(2)}) async-start(f32[16,2,240]{2,1,0:T(2,128)} %broadcast_in_dim.19), calls=%async_computation.4 | async-start | bytes 65536 | tf_op jit(solution)/shard_map/all_to_all | solution.py:246
  157.4 1.7 convolution_bitcast_fusion
  159.1 10.9 %all-to-all-done.4 = f32[16,2,240]{2,1,0:T(2,128)S(1)} async-done(((f32[16,2,240]{2,1,0:T(2,128)}), f32[16,2,240]{2,1,0:T(2,128)S(1)}, u32[]{:S(2)}, u32[]{:S(2)}) %all-to-all-start.4) | async-done | bytes 30752 | tf_op jit(solution)/shard_map/all_to_all | solution.py:246
  170.5 13.6 %all_to_all.31 = f32[32,1,512]{2,1,0:T(1,128)S(1)} all-to-all(f32[32,1,512]{2,1,0:T(1,128)S(1)} %reshape.126), channel_id=1, replica_groups=mesh['z'=16,'y'=4,'c'=2,'x'=4] {'y','c','x'}, dimensions={0} | all-to-all | bytes 131072 | tf_op jit(solution)/shard_map/all_to_all | solution.py:249
  184.1 0.5 broadcast.29
  184.6 0.8 reduce.6
  185.7 0.7 copy.74
  (65 shorter events, 3.2 us)
Async XLA Ops:
  6.5 11.7 %copy-start = (bf16[512,480]{0,1:T(8,128)(2,1)S(1)}, bf16[512,480]{0,1:T(8,128)(2,1)}, u32[]{:S(2)}) copy-start(bf16[512,480]{0,1:T(8,128)(2,1)} %param.10) | copy-start | bytes 1474564
  6.5 9.7 %copy-start.5 = (f32[1,1920]{1,0:T(1,128)S(1)}, f32[1,1920]{1,0:T(1,128)}, u32[]{:S(2)}) copy-start(f32[1,1920]{1,0:T(1,128)} %param.11) | copy-start | bytes 23044
  6.5 11.7 %copy-start.3 = (bf16[1,128,512]{2,1,0:T(8,128)(2,1)S(1)}, bf16[1,128,512]{2,1,0:T(8,128)(2,1)}, u32[]{:S(2)}) copy-start(bf16[1,128,512]{2,1,0:T(8,128)(2,1)} %param.8) | copy-start | bytes 393220
  6.5 104.0 %all-gather.7.cloned.1.call-start = ((), (), s32[]{:S(2)}) async-start(), calls=%async_computation.6 | async-start | bytes 1536000 | tf_op jit(solution)/shard_map/all_gather | solution.py:187
  11.8 12.0 %all-to-all-start = ((bf16[8,4,32,120]{3,2,1,0:T(8,128)(2,1)}), bf16[8,4,32,120]{3,2,1,0:T(8,128)(2,1)S(1)}, u32[]{:S(2)}, u32[]{:S(2)}) async-start(bf16[8,4,32,120]{3,2,1,0:T(8,128)(2,1)} %bitcast.9), calls=%async_computation | async-start | bytes 524288 | tf_op jit(solution)/shard_map/all_to_all | solution.py:201
  25.3 50.7 %all-to-all-start.1 = ((bf16[16,4,120,128]{3,2,1,0:T(8,128)(2,1)}), bf16[16,4,120,128]{3,2,1,0:T(8,128)(2,1)S(1)}, u32[]{:S(2)}, u32[]{:S(2)}) async-start(bf16[16,4,120,128]{3,2,1,0:T(8,128)(2,1)} %broadcast_in_dim.17), calls=%async_computation.1 | async-start | bytes 3932160 | tf_op jit(solution)/shard_map/all_to_all | solution.py:219
  33.6 109.0 %all-gather.9.cloned.1.call-start = ((), (), s32[]{:S(2)}) async-start(), calls=%async_computation.7 | async-start | bytes 2088960 | tf_op jit(solution)/shard_map/all_gather | solution.py:215
  73.9 4.6 %collective-permute-start = (bf16[16,2,120,120]{3,2,1,0:T(8,128)(2,1)S(1)}, bf16[16,2,120,120]{3,2,1,0:T(8,128)(2,1)}, u32[]{:S(2)}, u32[]{:S(2)}) collective-permute-start(bf16[16,2,120,120]{3,2,1,0:T(8,128)(2,1)S(1)} %bitcast.69), channel_id=1, source_target_pairs={{0,4},{4,0},{1,5},{5,1},{2,6},{6,2},{3,7},{7,3},{8,12},{12,8},{9,1... | collective-permute-start | bytes 2764808 | tf_op jit(solution)/shard_map/ppermute | solution.py:24
  76.0 5.3 %copy-start.1 = (s32[5]{0:T(128)}, s32[5]{0:T(128)S(1)}, u32[]{:S(2)}) copy-start(s32[5]{0:T(128)S(1)} %pad_add_fusion.scalars) | copy-start | bytes 64
  103.0 6.7 %copy-start.4 = (f32[1920]{0:T(1024)S(1)}, f32[1920]{0:T(1024)}, u32[]{:S(2)}) copy-start(f32[1920]{0:T(1024)} %param.14) | copy-start | bytes 23044
  104.2 38.5 %all-to-all-start.3 = ((bf16[16,120,256]{2,1,0:T(8,128)(2,1)}), bf16[16,120,256]{2,1,0:T(8,128)(2,1)S(1)}, u32[]{:S(2)}, u32[]{:S(2)}) async-start(bf16[16,120,256]{2,1,0:T(8,128)(2,1)} %broadcast_in_dim.18), calls=%async_computation.3 | async-start | bytes 1966080 | tf_op jit(solution)/shard_map/all_to_all | solution.py:20
  142.6 1.0 copy-start.2
  150.1 19.9 %all-to-all-start.4 = ((f32[16,2,240]{2,1,0:T(2,128)}), f32[16,2,240]{2,1,0:T(2,128)S(1)}, u32[]{:S(2)}, u32[]{:S(2)}) async-start(f32[16,2,240]{2,1,0:T(2,128)} %broadcast_in_dim.19), calls=%async_computation.4 | async-start | bytes 65536 | tf_op jit(solution)/shard_map/all_to_all | solution.py:246
Sparse Core Ops, SparseCore 0:
  9.5 56.8 all-gather.6
  68.5 74.1 all-gather.8

commit v5 on v4

--- a/solution.py
+++ b/solution.py
@@ -72,7 +72,9 @@
     pl.when(core == 0)(lambda: project(normed, own, 1, mine, 1))
 
 
-def attend_kernel(scalars, raw, normed, mine, own, other, partial, kept, rest, context):
+def attend_kernel(
+    scalars, raw, normed, mine, own, other, partial, kept, rest, context
+):
     core = scalars[0]
     xi, yi = scalars[1], scalars[2]
     for u in range(2):
@@ -86,8 +88,9 @@
             )
 
     def out_from(high):
-        for b in range(CHUNKS):
-            partial[b] = matmul(high[b, 1], context[...]).astype(BF)
+        for group in range(4):
+            for b in range(4 * group, 4 * group + 4):
+                partial[b] = matmul(high[b, 1], context[...]).astype(BF)
 
     def on_first():
         project(normed, other, 0, rest, 0)
@@ -104,22 +107,28 @@
     pl.when(core == 1)(on_second)
 
 
-def second_kernel(scalars, x1, weights_hbm, gain, pooled, weights, normed, qkv, arrived):
-    copy = pltpu.make_async_copy(weights_hbm.at[:, pl.ds(0, 3)], weights, arrived)
+def stage_kernel(weights_hbm, staged, arrived):
+    copy = pltpu.make_async_copy(weights_hbm.at[:, pl.ds(0, 3)], staged, arrived)
     copy.start()
+    copy.wait()
+
+
+def second_kernel(scalars, x1, weights, gain, rest, packed, normed, qkv):
     gain_rows = gain[...].T
     for u in range(2):
         normalize(x1[:, :, utterance(u)], gain_rows, normed, utterance(u))
-    copy.wait()
     for index in range(3):
         project(normed, weights, index, qkv, index)
     for u in range(2):
         length = scalars[3 + u]
         columns = utterance(u)
         context = attend(qkv[0, :, columns], qkv[1, :, columns], qkv[2, :, columns], length)
-        valid = lax.broadcasted_iota(jnp.int32, (HD, 128), 1) < length
-        total = jnp.where(valid, context.astype(F32), F32(0.0))
-        pooled[:, u : u + 1] = jnp.sum(total, axis=1, keepdims=True) / length.astype(F32)
+        valid = lax.broadcasted_iota(jnp.int32, (128, HD), 0) < length
+        total = jnp.where(valid, context.astype(F32).T, F32(0.0))
+        pooled = jnp.sum(total, axis=0, keepdims=True) / length.astype(F32)
+        row = jnp.concatenate([pooled, rest[u : u + 1, :]], axis=1)
+        for z in range(16):
+            packed[z, u : u + 1, :] = row
 
 
 def cost(flops, moved):
@@ -160,31 +169,39 @@
     )(scalars, raw, normed, mine, own, other)
 
 
-def run_second(scalars, x1, weights, gain):
+def run_stage(weights):
+    return pl.pallas_call(
+        stage_kernel,
+        out_shape=jax.ShapeDtypeStruct((CHUNKS, 3, HD, HD), BF),
+        in_specs=[pl.BlockSpec(memory_space=pltpu.HBM)],
+        out_specs=VMEM,
+        scratch_shapes=[pltpu.SemaphoreType.DMA],
+        compiler_params=pltpu.CompilerParams(vmem_limit_bytes=20 << 20),
+        cost_estimate=cost(0, 3_000_000),
+        name="stage",
+    )(weights)
+
+
+def run_second(scalars, x1, weights, gain, rest):
     return pl.pallas_call(
         second_kernel,
-        out_shape=jax.ShapeDtypeStruct((HD, 2), F32),
-        in_specs=[SMEM, VMEM, pl.BlockSpec(memory_space=pltpu.HBM), VMEM],
+        out_shape=jax.ShapeDtypeStruct((16, 2, 2 * HD), F32),
+        in_specs=[SMEM] + [VMEM] * 4,
         out_specs=VMEM,
         scratch_shapes=[
-            pltpu.VMEM((CHUNKS, 3, HD, HD), BF),
             pltpu.VMEM((CHUNKS, HD, 256), BF),
             pltpu.VMEM((3, HD, 256), BF),
-            pltpu.SemaphoreType.DMA,
         ],
-        compiler_params=pltpu.CompilerParams(vmem_limit_bytes=58 << 20),
+        compiler_params=pltpu.CompilerParams(vmem_limit_bytes=20 << 20),
         cost_estimate=cost(1_000_000_000, 6_000_000),
         name="second_layer",
-    )(scalars, x1, weights, gain)
+    )(scalars, x1, weights, gain, rest)
 
 
 def body(frames, lengths, feature_proj, norm_gain, qkv_weight, out_weight, center, whitening):
     core = lax.axis_index("c")
     xi, yi = lax.axis_index("x"), lax.axis_index("y")
     chunk = xi * NY + yi
-
-    white_cols = jnp.pad(whitening.T, ((0, 24), (0, 0)))
-    white_cols = lax.all_gather(white_cols, "y", axis=0)[:, :16].reshape(NY, 16, CHUNKS, HD)
 
     projected = lax.dot_general(
         feature_proj, frames[0], (((0,), (1,)), ((), ())), preferred_element_type=F32
@@ -222,6 +239,13 @@
     gains = gains.reshape(2, CHUNKS, HD)
     normed, mine = run_norm(scalars, raw, own, gains[0])
     partial, x0_own = run_attend(scalars, raw, normed, mine, own, other)
+    white = whitening.T.reshape(16, CHUNKS, HD).transpose(1, 0, 2)
+    x0_own, white = lax.optimization_barrier((x0_own, white))
+    near = [(((y + 1 + c) % NY) * 2 + c, y * 2 + c) for y in range(NY) for c in range(2)]
+    far = [(((y + 3) % NY) * 2 + 1, y * 2 + 1) for y in range(NY)]
+    white_near = lax.ppermute(white, ("y", "c"), near)
+    white_far = lax.ppermute(white, ("y", "c"), far)
+
     partial = lax.all_to_all(partial, ("x", "y"), 0, 0)
     attended = jnp.sum(partial.astype(F32), axis=0)
     x1_own = (x0_own.astype(F32) + attended).astype(BF)
@@ -230,19 +254,27 @@
     valid = jnp.arange(128)[None, :] < my_lengths[:, None]
     share = valid.astype(F32) / my_lengths.astype(F32)[:, None]
     pooled_x1 = jnp.sum(x1_own.reshape(HD, 2, 128).astype(F32) * share, axis=2).T
+    center_own = lax.dynamic_index_in_dim(center.reshape(CHUNKS, HD), chunk, 0, keepdims=False)
+    staged = run_stage(second_weights)
+    packed = run_second(scalars, x1, staged, gains[1], pooled_x1 - center_own)
+
+    white_cols = jnp.stack(
+        [jnp.where(core == 0, white, white_near), jnp.where(core == 0, white_near, white_far)]
+    )
     out_white = jnp.einsum(
-        "ynbc,bcr->ynr",
+        "ybnc,bcr->ynr",
         white_cols,
         second_weights[:, 3].astype(F32),
         precision=lax.Precision.HIGHEST,
     )
-    white_own = lax.dynamic_index_in_dim(white_cols, chunk, 2, keepdims=False)
-    mixed = jnp.concatenate([out_white, white_own], axis=2).reshape(64, 2 * HD)
-
-    pooled_context = run_second(scalars, x1, second_weights, gains[1]).T
-    center_own = lax.dynamic_index_in_dim(center.reshape(CHUNKS, HD), chunk, 0, keepdims=False)
-    packed = jnp.concatenate([pooled_context, pooled_x1 - center_own], axis=1)
-    packed = jnp.broadcast_to(packed[None], (16,) + packed.shape)
+    white_own = lax.dynamic_index_in_dim(white_cols, chunk, 1, keepdims=False)
+    mixed = jnp.concatenate([out_white, white_own], axis=2)
+    swapped = swap_cores(mixed)
+    low = jnp.where(core == 0, mixed, swapped)
+    high = jnp.where(core == 0, swapped, mixed)
+    mixed = jnp.concatenate([low, high, low, high], axis=0)
+    mixed = lax.dynamic_slice_in_dim(mixed, (NY - yi) % NY, NY, 0).reshape(64, 2 * HD)
+
     packed = lax.all_to_all(packed, "z", 0, 0).reshape(32, 2 * HD)
     part = jnp.einsum("tk,nk->nt", packed, mixed, precision=lax.Precision.HIGHEST)
     part = jnp.broadcast_to(part.reshape(NY, 1, 16, 32), (NY, 8, 16, 32)).reshape(32, 16, 32)

time: 197 us -> 172 us (0.87)
  blocking collectives: 75.8 us -> 54.7 us
  starting transfers between devices: 27.5 us -> 40.8 us
  waiting for transfers between devices: 46.4 us -> 35.8 us
  local copies, waits for them, and re-layouts: 15 us -> 11.3 us
    all_gather x1, waiting for transfers between devices: 30 us -> 0.01 us  [body(): second_weights = lax.all_gather(second_shard, 'z', axis=0)]
    all_to_all x1 -> x0, blocking collectives: 21.6 us -> none  [body(): partial = lax.all_to_all(partial, ('x', 'y'), 0, 0)]
    all_to_all x0 -> x1, waiting for transfers between devices: none -> 9.76 us  [body(): partial = lax.all_to_all(partial, ('x', 'y'), 0, 0)]
    all_to_all x1, waiting for transfers between devices: 0.01 us -> 8.36 us  [plane_gather(): return lax.all_to_all(spread, ('x', 'y'), 0, 0)]
    all_to_all x0 -> x1, starting transfers between devices: none -> 6.52 us  [body(): partial = lax.all_to_all(partial, ('x', 'y'), 0, 0)]
    ppermute x0 -> x2, starting transfers between devices: none -> 5.24 us  [the longest x1 4.58 us: body(): white_near = lax.ppermute(white, ('y', 'c'), near)]
    all_gather x1, blocking collectives: 38.6 us -> 41.1 us  [body(): own = lax.all_gather(first_shard, 'z', axis=0)]
    all_to_all x1, blocking collectives: 13.6 us -> 11.4 us  [body(): part = lax.all_to_all(part, ('y', 'c', 'x'), 0, 0).reshape(NY, 2, 4, 16, 32)]
  transfers between devices with their start and end apart: 7 -> 10, of which waited for: 4 -> 5; matrix products, arithmetic and copies ran while one was open for 6% -> 3% of each run, Pallas kernels for 3% -> 5%
where the time goes in v5:
time: 172 us; the launch traced here: 169 us
  blocking collectives  54.7 us (32%)
  starting transfers between devices  40.8 us (24%)
  waiting for transfers between devices  35.8 us (21%)
  between operations  14.5 us (8%)
  local copies, waits for them, and re-layouts  11.3 us (7%)
  Pallas kernels  8.66 us (5%)
  other arithmetic  1.85 us (1%)
    all_gather x1, blocking collectives, body(): own = lax.all_gather(first_shard, 'z', axis=0)  41.1 us
    all_to_all x1, waiting for transfers between devices, body(): packed = lax.all_to_all(packed, 'z', 0, 0).reshape(32, 2 * HD)  12.4 us
    all_to_all x1, blocking collectives, body(): part = lax.all_to_all(part, ('y', 'c', 'x'), 0, 0).reshape(NY, 2, 4, 16, 32)  11.4 us
    all_to_all x1, waiting for transfers between devices, body(): partial = lax.all_to_all(partial, ('x', 'y'), 0, 0)  9.76 us
    all_to_all x1, waiting for transfers between devices, plane_gather(): return lax.all_to_all(spread, ('x', 'y'), 0, 0)  8.36 us
    all_to_all x1, starting transfers between devices, body(): lax.all_to_all(projected, ('x', 'y'), 0, 0).reshape(4, NY, NY, HD, 128)  8.3 us
    all_to_all x1, starting transfers between devices, body(): packed = lax.all_to_all(packed, 'z', 0, 0).reshape(32, 2 * HD)  7.11 us
    all_to_all x1, starting transfers between devices, body(): partial = lax.all_to_all(partial, ('x', 'y'), 0, 0)  6.52 us
  transfers between devices with their start and end apart: 10, of which 5 were waited for; matrix products, arithmetic and copies ran while one was open for 3% of the time, Pallas kernels for 5%

profile of v5, /device:TPU:6, one launch (start us, length us, event | category | flops | bytes accessed | tf_op | source)
XLA Modules:
  0.0 168.7 jit_solution(13881792828348020713)
XLA Ops:
  6.5 1.1 reshape_squeeze.3
  7.7 0.9 reshape.93
  9.4 0.7 broadcast_in_dim.13
  10.1 4.5 %all-to-all-start = ((bf16[8,4,32,120]{3,2,1,0:T(8,128)(2,1)}), bf16[8,4,32,120]{3,2,1,0:T(8,128)(2,1)S(1)}, u32[]{:S(2)}, u32[]{:S(2)}) async-start(bf16[8,4,32,120]{3,2,1,0:T(8,128)(2,1)} %bitcast.10), calls=%async_computation | async-start | bytes 524288 | tf_op jit(solution)/shard_map/all_to_all | solution.py:218
  14.6 2.2 %all-gather.2 = f32[2,1,1920]{2,1,0:T(1,128)S(1)} all-gather(f32[1,1,1920]{2,1,0:T(1,128)} %bitcast.93), channel_id=1, replica_groups=mesh['z'=16,'y'=4,'c'=2,'x'=4] {'c'}, dimensions={0}, use_global_device_ids=true | all-gather | bytes 23040 | tf_op jit(solution)/shard_map/all_gather | solution.py:219
  16.8 0.3 convolution_convert_fusion
  17.1 5.0 %all-to-all-done = bf16[8,4,32,120]{3,2,1,0:T(8,128)(2,1)S(1)} async-done(((bf16[8,4,32,120]{3,2,1,0:T(8,128)(2,1)}), bf16[8,4,32,120]{3,2,1,0:T(8,128)(2,1)S(1)}, u32[]{:S(2)}, u32[]{:S(2)}) %all-to-all-start) | async-done | bytes 245792 | tf_op jit(solution)/shard_map/all_to_all | solution.py:218
  22.1 1.5 broadcast_in_dim.15
  23.6 8.3 %all-to-all-start.1 = ((bf16[16,4,120,128]{3,2,1,0:T(8,128)(2,1)}), bf16[16,4,120,128]{3,2,1,0:T(8,128)(2,1)S(1)}, u32[]{:S(2)}, u32[]{:S(2)}) async-start(bf16[16,4,120,128]{3,2,1,0:T(8,128)(2,1)} %broadcast_in_dim.15), calls=%async_computation.1 | async-start | bytes 3932160 | tf_op jit(solution)/shard_map/all_to_all | solution.py:236
  32.7 0.8 copy.53
  33.6 41.1 %all-gather = bf16[32,120,120]{2,1,0:T(8,128)(2,1)S(1)} all-gather(bf16[2,120,120]{2,1,0:T(8,128)(2,1)S(1)} %copy.51), channel_id=2, replica_groups=mesh['z'=16,'y'=4,'c'=2,'x'=4] {'z'}, dimensions={0}, use_global_device_ids=true | all-gather | bytes 979200 | tf_op jit(solution)/shard_map/all_gather | solution.py:233
  74.8 1.9 %collective-permute-start = (bf16[16,2,120,120]{3,2,1,0:T(8,128)(2,1)S(1)}, bf16[16,2,120,120]{3,2,1,0:T(8,128)(2,1)}, u32[]{:S(2)}, u32[]{:S(2)}) collective-permute-start(bf16[16,2,120,120]{3,2,1,0:T(8,128)(2,1)S(1)} %bitcast.71), channel_id=1, source_target_pairs={{0,4},{4,0},{1,5},{5,1},{2,6},{6,2},{3,7},{7,3},{8,12},{12,8},{9,1... | collective-permute-start | bytes 2764808 | tf_op jit(solution)/shard_map/ppermute | solution.py:24
  76.9 2.2 %first_norm.1 = (bf16[16,120,256]{2,1,0:T(8,128)(2,1)S(1)}, bf16[2,120,256]{2,1,0:T(8,128)(2,1)S(1)}) custom-call(s32[5]{0:T(128)S(1)} %pad_add_fusion.scalars, bf16[4,4,4,120,128]{4,3,2,1,0:T(8,128)(2,1)S(1)} %bitcast.69, bf16[16,2,120,120]{3,2,1,0:T(8,128)(2,1)S(1)} %bitcast.72, f32[16,120]{1,0:T(8,128)S(1)} %squeeze.33.gain), custom_call_target="tpu_custom_call" | custom-call | flops 400000000 | bytes 4000000 | tf_op jit(solution)/shard_map/first_norm/pallas_call | solution.py:139
  79.3 2.9 %first_attend.1 = (bf16[16,120,256]{2,1,0:T(8,128)(2,1)S(1)}, bf16[120,256]{1,0:T(8,128)(2,1)S(1)}) custom-call(s32[5]{0:T(128)S(1)} %pad_add_fusion.scalars, bf16[4,4,4,120,128]{4,3,2,1,0:T(8,128)(2,1)S(1)} %bitcast.70, bf16[16,120,256]{2,1,0:T(8,128)(2,1)S(1)} %get-tuple-element.22.normed, bf16[2,120,256]{2,1,0:T(8,128)(2,1)S(1)} %get-tuple-element.23.mine, ...), custom_call_target="tpu_custom_call" | custom-call | flops 600000000 | bytes 5000000 | tf_op jit(solution)/shard_map/first_attend/pallas_call | solution.py:154
  82.2 1.0 copy-done.2
  83.2 6.5 %all-to-all-start.2 = ((bf16[16,120,256]{2,1,0:T(8,128)(2,1)}), bf16[16,120,256]{2,1,0:T(8,128)(2,1)S(1)}, u32[]{:S(2)}, u32[]{:S(2)}) async-start(bf16[16,120,256]{2,1,0:T(8,128)(2,1)} %copy-done.2), calls=%async_computation.2 | async-start | bytes 1966080 | tf_op jit(solution)/shard_map/all_to_all | solution.py:249
  90.2 4.6 %collective-permute-start.1 = (f32[16,16,120]{2,1,0:T(8,128)S(1)}, f32[16,16,120]{2,1,0:T(8,128)S(1)}, u32[]{:S(2)}, u32[]{:S(2)}) collective-permute-start(f32[16,16,120]{2,1,0:T(8,128)S(1)} %bitcast.80), channel_id=1, source_target_pairs={{8,0},{20,4},{16,8},{28,12},{24,16},{4,20},{0,24},{12,28},{9,1},{2... | collective-permute-start | bytes 368648 | tf_op jit(solution)/shard_map/ppermute | solution.py:246
  94.8 0.7 collective-permute-start.2
  95.5 9.8 %all-to-all-done.2 = bf16[16,120,256]{2,1,0:T(8,128)(2,1)S(1)} async-done(((bf16[16,120,256]{2,1,0:T(8,128)(2,1)}), bf16[16,120,256]{2,1,0:T(8,128)(2,1)S(1)}, u32[]{:S(2)}, u32[]{:S(2)}) %all-to-all-start.2) | async-done | bytes 983072 | tf_op jit(solution)/shard_map/all_to_all | solution.py:249
  105.4 1.0 broadcast_in_dim.16
  106.4 5.3 %all-to-all-start.3 = ((bf16[16,120,256]{2,1,0:T(8,128)(2,1)}), bf16[16,120,256]{2,1,0:T(8,128)(2,1)S(1)}, u32[]{:S(2)}, u32[]{:S(2)}) async-start(bf16[16,120,256]{2,1,0:T(8,128)(2,1)} %broadcast_in_dim.16), calls=%async_computation.3 | async-start | bytes 1966080 | tf_op jit(solution)/shard_map/all_to_all | solution.py:20
  112.1 1.5 copy-done.1
  113.8 0.5 convolution_bitcast_fusion
  114.4 1.9 %collective-permute-start.3 = (f32[2,16,240]{2,1,0:T(8,128)S(1)}, f32[2,16,240]{2,1,0:T(8,128)S(1)}, u32[]{:S(2)}, u32[]{:S(2)}) collective-permute-start(f32[2,16,240]{2,1,0:T(8,128)S(1)} %pad_maximum_fusion.4), channel_id=1, source_target_pairs={{0,4},{4,0},{1,5},{5,1},{2,6},{6,2},{3,7},{7,3},{8,12},{12,8},{9,1... | collective-permute-start | bytes 92168 | tf_op jit(solution)/shard_map/ppermute | solution.py:24
  116.3 8.4 %all-to-all-done.3.x1 = bf16[16,120,256]{2,1,0:T(8,128)(2,1)S(1)} async-done(((bf16[16,120,256]{2,1,0:T(8,128)(2,1)}), bf16[16,120,256]{2,1,0:T(8,128)(2,1)S(1)}, u32[]{:S(2)}, u32[]{:S(2)}) %all-to-all-start.3) | async-done | bytes 983072 | tf_op jit(solution)/shard_map/all_to_all | solution.py:20
  124.7 3.5 %second_layer.1 = f32[16,2,240]{2,1,0:T(2,128)} custom-call(s32[5]{0:T(128)S(1)} %pad_add_fusion.scalars, bf16[16,120,256]{2,1,0:T(8,128)(2,1)S(1)} %all-to-all-done.3.x1, bf16[16,3,120,120]{3,2,1,0:T(8,128)(2,1)S(1)} %stage.1.weights, f32[16,120]{1,0:T(8,128)S(1)} %squeeze.36.gain, f32[2,120]{1,0:T(2,128)S(1)} %subtract_bitcast_fusion.rest), custom_call_target="tpu_custom_call" | custom-call | flops 1000000000 | bytes 6000000 | tf_op jit(solution)/shard_map/second_layer/pallas_call | solution.py:186
  128.1 7.1 %all-to-all-start.4 = ((f32[16,2,240]{2,1,0:T(2,128)}), f32[16,2,240]{2,1,0:T(2,128)S(1)}, u32[]{:S(2)}, u32[]{:S(2)}) async-start(f32[16,2,240]{2,1,0:T(2,128)} %second_layer.1), calls=%async_computation.4 | async-start | bytes 65536 | tf_op jit(solution)/shard_map/all_to_all | solution.py:278
  135.4 12.4 %all-to-all-done.4 = f32[16,2,240]{2,1,0:T(2,128)S(1)} async-done(((f32[16,2,240]{2,1,0:T(2,128)}), f32[16,2,240]{2,1,0:T(2,128)S(1)}, u32[]{:S(2)}, u32[]{:S(2)}) %all-to-all-start.4) | async-done | bytes 30752 | tf_op jit(solution)/shard_map/all_to_all | solution.py:278
  148.2 11.4 %all_to_all.30 = f32[32,1,512]{2,1,0:T(1,128)S(1)} all-to-all(f32[32,1,512]{2,1,0:T(1,128)S(1)} %reshape.116), channel_id=1, replica_groups=mesh['z'=16,'y'=4,'c'=2,'x'=4] {'y','c','x'}, dimensions={0} | all-to-all | bytes 131072 | tf_op jit(solution)/shard_map/all_to_all | solution.py:281
  159.6 0.5 broadcast.27
  160.1 0.8 reduce.6
  161.1 0.7 copy.57
  (69 shorter events, 3.3 us)
Async XLA Ops:
  6.5 10.3 %copy-start = (bf16[512,480]{0,1:T(8,128)(2,1)S(1)}, bf16[512,480]{0,1:T(8,128)(2,1)}, u32[]{:S(2)}) copy-start(bf16[512,480]{0,1:T(8,128)(2,1)} %param.10) | copy-start | bytes 1474564
  6.5 10.3 %copy-start.3 = (bf16[1,128,512]{2,1,0:T(8,128)(2,1)S(1)}, bf16[1,128,512]{2,1,0:T(8,128)(2,1)}, u32[]{:S(2)}) copy-start(bf16[1,128,512]{2,1,0:T(8,128)(2,1)} %param.8) | copy-start | bytes 393220
  10.1 12.0 %all-to-all-start = ((bf16[8,4,32,120]{3,2,1,0:T(8,128)(2,1)}), bf16[8,4,32,120]{3,2,1,0:T(8,128)(2,1)S(1)}, u32[]{:S(2)}, u32[]{:S(2)}) async-start(bf16[8,4,32,120]{3,2,1,0:T(8,128)(2,1)} %bitcast.10), calls=%async_computation | async-start | bytes 524288 | tf_op jit(solution)/shard_map/all_to_all | solution.py:218
  23.6 53.3 %all-to-all-start.1 = ((bf16[16,4,120,128]{3,2,1,0:T(8,128)(2,1)}), bf16[16,4,120,128]{3,2,1,0:T(8,128)(2,1)S(1)}, u32[]{:S(2)}, u32[]{:S(2)}) async-start(bf16[16,4,120,128]{3,2,1,0:T(8,128)(2,1)} %broadcast_in_dim.15), calls=%async_computation.1 | async-start | bytes 3932160 | tf_op jit(solution)/shard_map/all_to_all | solution.py:236
  31.9 80.2 %all-gather.5.cloned.1.call-start = ((), (), s32[]{:S(2)}) async-start(), calls=%async_computation.6 | async-start | bytes 2088960 | tf_op jit(solution)/shard_map/all_gather | solution.py:232
  74.8 4.6 %collective-permute-start = (bf16[16,2,120,120]{3,2,1,0:T(8,128)(2,1)S(1)}, bf16[16,2,120,120]{3,2,1,0:T(8,128)(2,1)}, u32[]{:S(2)}, u32[]{:S(2)}) collective-permute-start(bf16[16,2,120,120]{3,2,1,0:T(8,128)(2,1)S(1)} %bitcast.71), channel_id=1, source_target_pairs={{0,4},{4,0},{1,5},{5,1},{2,6},{6,2},{3,7},{7,3},{8,12},{12,8},{9,1... | collective-permute-start | bytes 2764808 | tf_op jit(solution)/shard_map/ppermute | solution.py:24
  82.2 1.0 copy-start.2
  83.2 6.5 %copy-start.4 = (f32[1920,16]{0,1:T(8,128)S(1)}, f32[1920,16]{0,1:T(8,128)}, u32[]{:S(2)}) copy-start(f32[1920,16]{0,1:T(8,128)} %param.15) | copy-start | bytes 368644
  83.2 6.7 %copy-start.5 = (f32[1920]{0:T(1024)S(1)}, f32[1920]{0:T(1024)}, u32[]{:S(2)}) copy-start(f32[1920]{0:T(1024)} %param.14) | copy-start | bytes 23044
  83.2 22.1 %all-to-all-start.2 = ((bf16[16,120,256]{2,1,0:T(8,128)(2,1)}), bf16[16,120,256]{2,1,0:T(8,128)(2,1)S(1)}, u32[]{:S(2)}, u32[]{:S(2)}) async-start(bf16[16,120,256]{2,1,0:T(8,128)(2,1)} %copy-done.2), calls=%async_computation.2 | async-start | bytes 1966080 | tf_op jit(solution)/shard_map/all_to_all | solution.py:249
  90.2 21.5 %collective-permute-start.1 = (f32[16,16,120]{2,1,0:T(8,128)S(1)}, f32[16,16,120]{2,1,0:T(8,128)S(1)}, u32[]{:S(2)}, u32[]{:S(2)}) collective-permute-start(f32[16,16,120]{2,1,0:T(8,128)S(1)} %bitcast.80), channel_id=1, source_target_pairs={{8,0},{20,4},{16,8},{28,12},{24,16},{4,20},{0,24},{12,28},{9,1},{2... | collective-permute-start | bytes 368648 | tf_op jit(solution)/shard_map/ppermute | solution.py:246
  94.8 16.9 %collective-permute-start.2 = (f32[16,16,120]{2,1,0:T(8,128)S(1)}, f32[16,16,120]{2,1,0:T(8,128)S(1)}, u32[]{:S(2)}, u32[]{:S(2)}) collective-permute-start(f32[16,16,120]{2,1,0:T(8,128)S(1)} %bitcast.81), channel_id=1, source_target_pairs={{28,4},{4,12},{12,20},{20,28},{29,5},{5,13},{13,21},{21,29},{30,6}... | collective-permute-start | bytes 368648 | tf_op jit(solution)/shard_map/ppermute | solution.py:247
  106.4 18.2 %all-to-all-start.3 = ((bf16[16,120,256]{2,1,0:T(8,128)(2,1)}), bf16[16,120,256]{2,1,0:T(8,128)(2,1)S(1)}, u32[]{:S(2)}, u32[]{:S(2)}) async-start(bf16[16,120,256]{2,1,0:T(8,128)(2,1)} %broadcast_in_dim.16), calls=%async_computation.3 | async-start | bytes 1966080 | tf_op jit(solution)/shard_map/all_to_all | solution.py:20
  112.1 1.6 copy-start.1
  114.4 20.9 %collective-permute-start.3 = (f32[2,16,240]{2,1,0:T(8,128)S(1)}, f32[2,16,240]{2,1,0:T(8,128)S(1)}, u32[]{:S(2)}, u32[]{:S(2)}) collective-permute-start(f32[2,16,240]{2,1,0:T(8,128)S(1)} %pad_maximum_fusion.4), channel_id=1, source_target_pairs={{0,4},{4,0},{1,5},{5,1},{2,6},{6,2},{3,7},{7,3},{8,12},{12,8},{9,1... | collective-permute-start | bytes 92168 | tf_op jit(solution)/shard_map/ppermute | solution.py:24
  128.1 19.6 %all-to-all-start.4 = ((f32[16,2,240]{2,1,0:T(2,128)}), f32[16,2,240]{2,1,0:T(2,128)S(1)}, u32[]{:S(2)}, u32[]{:S(2)}) async-start(f32[16,2,240]{2,1,0:T(2,128)} %second_layer.1), calls=%async_computation.4 | async-start | bytes 65536 | tf_op jit(solution)/shard_map/all_to_all | solution.py:278
Sparse Core Ops, SparseCore 0:
  34.9 74.3 all-gather.4

commit v6 on v5

--- a/solution.py
+++ b/solution.py
@@ -61,6 +61,18 @@
     return slice(u * 128, u * 128 + 128)
 
 
+def regroup_kernel(lengths, qkv, out, mats):
+    tail = jnp.full((2, HD), lengths[0].astype(F32)).astype(BF)
+    for y in range(NY):
+        for m in range(4):
+            start = (m * NY + y) * HD if m < 3 else y * HD
+            source = qkv if m < 3 else out
+            block = source[:, start : start + HD]
+            for c in range(2):
+                mats[2 * y + c, m, 0:30, :] = block
+                mats[2 * y + c, m, 30:32, :] = tail
+
+
 def norm_kernel(scalars, raw, own, gain, normed, mine):
     core = scalars[0]
     gain_rows = gain[...].T
@@ -114,6 +126,8 @@
 
 
 def second_kernel(scalars, x1, weights, gain, rest, packed, normed, qkv):
+    core = scalars[0]
+    rows = []
     gain_rows = gain[...].T
     for u in range(2):
         normalize(x1[:, :, utterance(u)], gain_rows, normed, utterance(u))
@@ -126,13 +140,28 @@
         valid = lax.broadcasted_iota(jnp.int32, (128, HD), 0) < length
         total = jnp.where(valid, context.astype(F32).T, F32(0.0))
         pooled = jnp.sum(total, axis=0, keepdims=True) / length.astype(F32)
-        row = jnp.concatenate([pooled, rest[u : u + 1, :]], axis=1)
-        for z in range(16):
-            packed[z, u : u + 1, :] = row
+        rows.append(jnp.concatenate([pooled, rest[u : u + 1, :]], axis=1))
+    mine = jnp.concatenate(rows, axis=0)
+    first = jnp.where(core == 0, mine, F32(0.0))
+    second = jnp.where(core == 1, mine, F32(0.0))
+    block = jnp.concatenate([first, second], axis=0)
+    for z in range(16):
+        packed[z] = block
 
 
 def cost(flops, moved):
     return pl.CostEstimate(flops=flops, bytes_accessed=moved, transcendentals=32768)
+
+
+def run_regroup(lengths, qkv, out):
+    return pl.pallas_call(
+        regroup_kernel,
+        out_shape=jax.ShapeDtypeStruct((2 * NY, 4, 32, HD), BF),
+        in_specs=[SMEM, VMEM, VMEM],
+        out_specs=VMEM,
+        cost_estimate=cost(0, 400_000),
+        name="regroup",
+    )(lengths, qkv, out)
 
 
 def run_norm(scalars, raw, own, gain):
@@ -185,7 +214,7 @@
 def run_second(scalars, x1, weights, gain, rest):
     return pl.pallas_call(
         second_kernel,
-        out_shape=jax.ShapeDtypeStruct((16, 2, 2 * HD), F32),
+        out_shape=jax.ShapeDtypeStruct((16, 4, 2 * HD), F32),
         in_specs=[SMEM] + [VMEM] * 4,
         out_specs=VMEM,
         scratch_shapes=[
@@ -209,12 +238,7 @@
     projected = projected.astype(BF).reshape(1, NY, HD, 128)
     projected = jnp.broadcast_to(projected, (16, NY, HD, 128))
 
-    qkv = qkv_weight[0].reshape(30, 3, NY, HD).transpose(2, 1, 0, 3)
-    out = out_weight[0].T.reshape(30, NY, HD).transpose(1, 0, 2)[:, None]
-    mats = jnp.concatenate([qkv, out], axis=1)
-    tail = jnp.broadcast_to(lengths[0].astype(BF), (NY, 4, 2, HD))
-    mats = jnp.concatenate([mats, tail], axis=2)
-    mats = jnp.broadcast_to(mats[:, None], (NY, 2, 4, 32, HD)).reshape(2 * NY, 4, 32, HD)
+    mats = run_regroup(lengths, qkv_weight[0], out_weight[0].T)
     regrouped = lax.all_to_all(mats, ("y", "c"), 0, 0).reshape(NY, 2, 4, 32, HD)
     gains = lax.all_gather(norm_gain[0], "c", axis=0)
     regrouped, gains, projected = lax.optimization_barrier((regrouped, gains, projected))
@@ -275,12 +299,11 @@
     mixed = jnp.concatenate([low, high, low, high], axis=0)
     mixed = lax.dynamic_slice_in_dim(mixed, (NY - yi) % NY, NY, 0).reshape(64, 2 * HD)
 
-    packed = lax.all_to_all(packed, "z", 0, 0).reshape(32, 2 * HD)
+    packed = lax.all_to_all(packed, "z", 0, 0).reshape(64, 2 * HD)
     part = jnp.einsum("tk,nk->nt", packed, mixed, precision=lax.Precision.HIGHEST)
-    part = jnp.broadcast_to(part.reshape(NY, 1, 16, 32), (NY, 8, 16, 32)).reshape(32, 16, 32)
-    part = lax.all_to_all(part, ("y", "c", "x"), 0, 0).reshape(NY, 2, 4, 16, 32)
-    total = jnp.sum(part, axis=(0, 2))
-    return total.reshape(2, 16, 16, 2).transpose(2, 0, 3, 1).reshape(64, 16)
+    part = jnp.broadcast_to(part.reshape(NY, 1, 16, 64), (NY, 8, 16, 64)).reshape(32, 16, 64)
+    part = lax.all_to_all(part, ("y", "c", "x"), 0, 0)
+    return jnp.sum(part, axis=0).T
 
 
 def solution(mesh):

time: 172 us -> 178 us (1.035)
  local copies, waits for them, and re-layouts: 11.3 us -> 14 us
    optimization_barrier x0 -> x1, local copies, waits for them, and re-layouts: none -> 5.96 us  [body(): lax.optimization_barrier((regrouped, gains, projected))]
    pallas_call x1 -> x2, Pallas kernels: 3.48 us -> 5.23 us  [the longest x1 3.5 us: run_second(): pl.pallas_call(second_kernel, out_shape=jax.ShapeDtypeStruct((16, 4, 2 *...]
where the time goes in v6:
time: 178 us; the launch traced here: 175 us
  blocking collectives  55.1 us (31%)
  starting transfers between devices  40.7 us (23%)
  waiting for transfers between devices  35.3 us (20%)
  between operations  14.5 us (8%)
  local copies, waits for them, and re-layouts  14 us (8%)
  Pallas kernels  10.4 us (6%)
  other arithmetic  3.03 us (2%)
  matrix products  1.89 us (1%)
    all_gather x1, blocking collectives, body(): own = lax.all_gather(first_shard, 'z', axis=0)  41.2 us
    all_to_all x1, waiting for transfers between devices, body(): packed = lax.all_to_all(packed, 'z', 0, 0).reshape(64, 2 * HD)  12.8 us
    all_to_all x1, blocking collectives, body(): part = lax.all_to_all(part, ('y', 'c', 'x'), 0, 0)  11.7 us
    all_to_all x1, waiting for transfers between devices, body(): partial = lax.all_to_all(partial, ('x', 'y'), 0, 0)  9.76 us
    all_to_all x1, waiting for transfers between devices, plane_gather(): return lax.all_to_all(spread, ('x', 'y'), 0, 0)  8.36 us
    all_to_all x1, starting transfers between devices, body(): lax.all_to_all(projected, ('x', 'y'), 0, 0).reshape(4, NY, NY, HD, 128)  8.31 us
    all_to_all x1, starting transfers between devices, body(): packed = lax.all_to_all(packed, 'z', 0, 0).reshape(64, 2 * HD)  6.99 us
    all_to_all x1, starting transfers between devices, body(): partial = lax.all_to_all(partial, ('x', 'y'), 0, 0)  6.57 us
  transfers between devices with their start and end apart: 10, of which 5 were waited for; matrix products, arithmetic and copies ran while one was open for 3% of the time, Pallas kernels for 5%

profile of v6, /device:TPU:6, one launch (start us, length us, event | category | flops | bytes accessed | tf_op | source)
XLA Modules:
  0.0 174.9 jit_solution(7652476913594987715)
XLA Ops:
  7.2 1.7 regroup.1
  9.0 4.5 %all-to-all-start = ((bf16[8,4,32,120]{3,2,1,0:T(8,128)(2,1)}), bf16[8,4,32,120]{3,2,1,0:T(8,128)(2,1)S(1)}, u32[]{:S(2)}, u32[]{:S(2)}) async-start(bf16[8,4,32,120]{3,2,1,0:T(8,128)(2,1)} %regroup.1), calls=%async_computation | async-start | bytes 524288 | tf_op jit(solution)/shard_map/all_to_all | solution.py:242
  13.5 2.2 %all-gather.2 = f32[2,1,1920]{2,1,0:T(1,128)S(1)} all-gather(f32[1,1,1920]{2,1,0:T(1,128)} %bitcast.76), channel_id=1, replica_groups=mesh['z'=16,'y'=4,'c'=2,'x'=4] {'c'}, dimensions={0}, use_global_device_ids=true | all-gather | bytes 23040 | tf_op jit(solution)/shard_map/all_gather | solution.py:243
  15.7 1.2 convolution_convert_fusion
  16.9 4.1 %all-to-all-done = bf16[8,4,32,120]{3,2,1,0:T(8,128)(2,1)S(1)} async-done(((bf16[8,4,32,120]{3,2,1,0:T(8,128)(2,1)}), bf16[8,4,32,120]{3,2,1,0:T(8,128)(2,1)S(1)}, u32[]{:S(2)}, u32[]{:S(2)}) %all-to-all-start) | async-done | bytes 245792 | tf_op jit(solution)/shard_map/all_to_all | solution.py:242
  21.0 1.6 broadcast_in_dim.9
  22.7 6.0 %copy.33 = bf16[4,2,4,32,120]{0,4,3,2,1:T(8,128)(2,1)} copy(bf16[4,2,4,32,120]{4,3,2,1,0:T(8,128)(2,1)S(1)} %bitcast.64) | data formatting | bytes 491520 | tf_op jit(solution)/shard_map/optimization_barrier | solution.py:244
  29.0 8.3 %all-to-all-start.1 = ((bf16[16,4,120,128]{3,2,1,0:T(8,128)(2,1)}), bf16[16,4,120,128]{3,2,1,0:T(8,128)(2,1)S(1)}, u32[]{:S(2)}, u32[]{:S(2)}) async-start(bf16[16,4,120,128]{3,2,1,0:T(8,128)(2,1)} %broadcast_in_dim.9), calls=%async_computation.1 | async-start | bytes 3932160 | tf_op jit(solution)/shard_map/all_to_all | solution.py:260
  37.4 0.7 slice_convert_fusion
  38.2 0.8 copy.36
  39.1 41.2 %all-gather = bf16[32,120,120]{2,1,0:T(8,128)(2,1)S(1)} all-gather(bf16[2,120,120]{2,1,0:T(8,128)(2,1)S(1)} %copy.34), channel_id=2, replica_groups=mesh['z'=16,'y'=4,'c'=2,'x'=4] {'z'}, dimensions={0}, use_global_device_ids=true | all-gather | bytes 979200 | tf_op jit(solution)/shard_map/all_gather | solution.py:257
  80.3 1.9 %collective-permute-start = (bf16[16,2,120,120]{3,2,1,0:T(8,128)(2,1)S(1)}, bf16[16,2,120,120]{3,2,1,0:T(8,128)(2,1)}, u32[]{:S(2)}, u32[]{:S(2)}) collective-permute-start(bf16[16,2,120,120]{3,2,1,0:T(8,128)(2,1)S(1)} %bitcast.58), channel_id=1, source_target_pairs={{0,4},{4,0},{1,5},{5,1},{2,6},{6,2},{3,7},{7,3},{8,12},{12,8},{9,1... | collective-permute-start | bytes 2764808 | tf_op jit(solution)/shard_map/ppermute | solution.py:24
  82.5 2.2 %first_norm.1 = (bf16[16,120,256]{2,1,0:T(8,128)(2,1)S(1)}, bf16[2,120,256]{2,1,0:T(8,128)(2,1)S(1)}) custom-call(s32[5]{0:T(128)S(1)} %pad_add_fusion.scalars, bf16[4,4,4,120,128]{4,3,2,1,0:T(8,128)(2,1)S(1)} %bitcast.56, bf16[16,2,120,120]{3,2,1,0:T(8,128)(2,1)S(1)} %bitcast.59, f32[16,120]{1,0:T(8,128)S(1)} %squeeze.36.gain), custom_call_target="tpu_custom_call" | custom-call | flops 400000000 | bytes 4000000 | tf_op jit(solution)/shard_map/first_norm/pallas_call | solution.py:168
  84.9 2.9 %first_attend.1 = (bf16[16,120,256]{2,1,0:T(8,128)(2,1)S(1)}, bf16[120,256]{1,0:T(8,128)(2,1)S(1)}) custom-call(s32[5]{0:T(128)S(1)} %pad_add_fusion.scalars, bf16[4,4,4,120,128]{4,3,2,1,0:T(8,128)(2,1)S(1)} %bitcast.57, bf16[16,120,256]{2,1,0:T(8,128)(2,1)S(1)} %get-tuple-element.22.normed, bf16[2,120,256]{2,1,0:T(8,128)(2,1)S(1)} %get-tuple-element.23.mine, ...), custom_call_target="tpu_custom_call" | custom-call | flops 600000000 | bytes 5000000 | tf_op jit(solution)/shard_map/first_attend/pallas_call | solution.py:183
  87.8 1.0 copy-done.2
  88.8 6.6 %all-to-all-start.2 = ((bf16[16,120,256]{2,1,0:T(8,128)(2,1)}), bf16[16,120,256]{2,1,0:T(8,128)(2,1)S(1)}, u32[]{:S(2)}, u32[]{:S(2)}) async-start(bf16[16,120,256]{2,1,0:T(8,128)(2,1)} %copy-done.2), calls=%async_computation.2 | async-start | bytes 1966080 | tf_op jit(solution)/shard_map/all_to_all | solution.py:273
  95.8 4.6 %collective-permute-start.1 = (f32[16,16,120]{2,1,0:T(8,128)S(1)}, f32[16,16,120]{2,1,0:T(8,128)S(1)}, u32[]{:S(2)}, u32[]{:S(2)}) collective-permute-start(f32[16,16,120]{2,1,0:T(8,128)S(1)} %bitcast.66), channel_id=1, source_target_pairs={{8,0},{20,4},{16,8},{28,12},{24,16},{4,20},{0,24},{12,28},{9,1},{2... | collective-permute-start | bytes 368648 | tf_op jit(solution)/shard_map/ppermute | solution.py:270
  100.4 0.7 collective-permute-start.2
  101.1 9.8 %all-to-all-done.2 = bf16[16,120,256]{2,1,0:T(8,128)(2,1)S(1)} async-done(((bf16[16,120,256]{2,1,0:T(8,128)(2,1)}), bf16[16,120,256]{2,1,0:T(8,128)(2,1)S(1)}, u32[]{:S(2)}, u32[]{:S(2)}) %all-to-all-start.2) | async-done | bytes 983072 | tf_op jit(solution)/shard_map/all_to_all | solution.py:273
  111.0 1.0 broadcast_in_dim.10
  112.0 5.3 %all-to-all-start.3 = ((bf16[16,120,256]{2,1,0:T(8,128)(2,1)}), bf16[16,120,256]{2,1,0:T(8,128)(2,1)S(1)}, u32[]{:S(2)}, u32[]{:S(2)}) async-start(bf16[16,120,256]{2,1,0:T(8,128)(2,1)} %broadcast_in_dim.10), calls=%async_computation.3 | async-start | bytes 1966080 | tf_op jit(solution)/shard_map/all_to_all | solution.py:20
  117.7 1.5 copy-done.1
  119.4 0.5 convolution_bitcast_fusion
  120.0 1.9 %collective-permute-start.3 = (f32[2,16,240]{2,1,0:T(8,128)S(1)}, f32[2,16,240]{2,1,0:T(8,128)S(1)}, u32[]{:S(2)}, u32[]{:S(2)}) collective-permute-start(f32[2,16,240]{2,1,0:T(8,128)S(1)} %pad_maximum_fusion.3), channel_id=1, source_target_pairs={{0,4},{4,0},{1,5},{5,1},{2,6},{6,2},{3,7},{7,3},{8,12},{12,8},{9,1... | collective-permute-start | bytes 92168 | tf_op jit(solution)/shard_map/ppermute | solution.py:24
  121.9 8.4 %all-to-all-done.3.x1 = bf16[16,120,256]{2,1,0:T(8,128)(2,1)S(1)} async-done(((bf16[16,120,256]{2,1,0:T(8,128)(2,1)}), bf16[16,120,256]{2,1,0:T(8,128)(2,1)S(1)}, u32[]{:S(2)}, u32[]{:S(2)}) %all-to-all-start.3) | async-done | bytes 983072 | tf_op jit(solution)/shard_map/all_to_all | solution.py:20
  130.3 3.5 %second_layer.1 = f32[16,4,240]{2,1,0:T(4,128)} custom-call(s32[5]{0:T(128)S(1)} %pad_add_fusion.scalars, bf16[16,120,256]{2,1,0:T(8,128)(2,1)S(1)} %all-to-all-done.3.x1, bf16[16,3,120,120]{3,2,1,0:T(8,128)(2,1)S(1)} %stage.1.weights, f32[16,120]{1,0:T(8,128)S(1)} %squeeze.39.gain, f32[2,120]{1,0:T(2,128)S(1)} %subtract_bitcast_fusion.rest), custom_call_target="tpu_custom_call" | custom-call | flops 1000000000 | bytes 6000000 | tf_op jit(solution)/shard_map/second_layer/pallas_call | solution.py:215
  133.8 7.0 %all-to-all-start.4 = ((f32[16,4,240]{2,1,0:T(4,128)}), f32[16,4,240]{2,1,0:T(4,128)S(1)}, u32[]{:S(2)}, u32[]{:S(2)}) async-start(f32[16,4,240]{2,1,0:T(4,128)} %second_layer.1), calls=%async_computation.4 | async-start | bytes 131072 | tf_op jit(solution)/shard_map/all_to_all | solution.py:302
  140.9 12.8 %all-to-all-done.4 = f32[16,4,240]{2,1,0:T(4,128)S(1)} async-done(((f32[16,4,240]{2,1,0:T(4,128)}), f32[16,4,240]{2,1,0:T(4,128)S(1)}, u32[]{:S(2)}, u32[]{:S(2)}) %all-to-all-start.4) | async-done | bytes 61472 | tf_op jit(solution)/shard_map/all_to_all | solution.py:302
  154.1 11.7 %all_to_all.30 = f32[32,1,1024]{2,1,0:T(1,128)S(1)} all-to-all(f32[32,1,1024]{2,1,0:T(1,128)S(1)} %reshape.93), channel_id=1, replica_groups=mesh['z'=16,'y'=4,'c'=2,'x'=4] {'y','c','x'}, dimensions={0} | all-to-all | bytes 262144 | tf_op jit(solution)/shard_map/all_to_all | solution.py:305
  165.8 0.5 broadcast.23
  166.3 0.9 reduce.4
  167.4 0.6 reduce_sum.29
  (58 shorter events, 2.9 us)
Async XLA Ops:
  6.5 9.1 %copy-start = (bf16[512,480]{0,1:T(8,128)(2,1)S(1)}, bf16[512,480]{0,1:T(8,128)(2,1)}, u32[]{:S(2)}) copy-start(bf16[512,480]{0,1:T(8,128)(2,1)} %param.10) | copy-start | bytes 1474564
  9.0 12.0 %all-to-all-start = ((bf16[8,4,32,120]{3,2,1,0:T(8,128)(2,1)}), bf16[8,4,32,120]{3,2,1,0:T(8,128)(2,1)S(1)}, u32[]{:S(2)}, u32[]{:S(2)}) async-start(bf16[8,4,32,120]{3,2,1,0:T(8,128)(2,1)} %regroup.1), calls=%async_computation | async-start | bytes 524288 | tf_op jit(solution)/shard_map/all_to_all | solution.py:242
  29.0 53.4 %all-to-all-start.1 = ((bf16[16,4,120,128]{3,2,1,0:T(8,128)(2,1)}), bf16[16,4,120,128]{3,2,1,0:T(8,128)(2,1)S(1)}, u32[]{:S(2)}, u32[]{:S(2)}) async-start(bf16[16,4,120,128]{3,2,1,0:T(8,128)(2,1)} %broadcast_in_dim.9), calls=%async_computation.1 | async-start | bytes 3932160 | tf_op jit(solution)/shard_map/all_to_all | solution.py:260
  37.3 80.4 %all-gather.5.cloned.1.call-start = ((), (), s32[]{:S(2)}) async-start(), calls=%async_computation.6 | async-start | bytes 2088960 | tf_op jit(solution)/shard_map/all_gather | solution.py:256
  80.3 4.6 %collective-permute-start = (bf16[16,2,120,120]{3,2,1,0:T(8,128)(2,1)S(1)}, bf16[16,2,120,120]{3,2,1,0:T(8,128)(2,1)}, u32[]{:S(2)}, u32[]{:S(2)}) collective-permute-start(bf16[16,2,120,120]{3,2,1,0:T(8,128)(2,1)S(1)} %bitcast.58), channel_id=1, source_target_pairs={{0,4},{4,0},{1,5},{5,1},{2,6},{6,2},{3,7},{7,3},{8,12},{12,8},{9,1... | collective-permute-start | bytes 2764808 | tf_op jit(solution)/shard_map/ppermute | solution.py:24
  87.8 1.0 copy-start.2
  88.7 6.6 %copy-start.3 = (f32[1920,16]{0,1:T(8,128)S(1)}, f32[1920,16]{0,1:T(8,128)}, u32[]{:S(2)}) copy-start(f32[1920,16]{0,1:T(8,128)} %param.15) | copy-start | bytes 368644
  88.7 6.8 %copy-start.4 = (f32[1920]{0:T(1024)S(1)}, f32[1920]{0:T(1024)}, u32[]{:S(2)}) copy-start(f32[1920]{0:T(1024)} %param.14) | copy-start | bytes 23044
  88.8 22.1 %all-to-all-start.2 = ((bf16[16,120,256]{2,1,0:T(8,128)(2,1)}), bf16[16,120,256]{2,1,0:T(8,128)(2,1)S(1)}, u32[]{:S(2)}, u32[]{:S(2)}) async-start(bf16[16,120,256]{2,1,0:T(8,128)(2,1)} %copy-done.2), calls=%async_computation.2 | async-start | bytes 1966080 | tf_op jit(solution)/shard_map/all_to_all | solution.py:273
  95.8 21.5 %collective-permute-start.1 = (f32[16,16,120]{2,1,0:T(8,128)S(1)}, f32[16,16,120]{2,1,0:T(8,128)S(1)}, u32[]{:S(2)}, u32[]{:S(2)}) collective-permute-start(f32[16,16,120]{2,1,0:T(8,128)S(1)} %bitcast.66), channel_id=1, source_target_pairs={{8,0},{20,4},{16,8},{28,12},{24,16},{4,20},{0,24},{12,28},{9,1},{2... | collective-permute-start | bytes 368648 | tf_op jit(solution)/shard_map/ppermute | solution.py:270
  100.4 16.9 %collective-permute-start.2 = (f32[16,16,120]{2,1,0:T(8,128)S(1)}, f32[16,16,120]{2,1,0:T(8,128)S(1)}, u32[]{:S(2)}, u32[]{:S(2)}) collective-permute-start(f32[16,16,120]{2,1,0:T(8,128)S(1)} %bitcast.67), channel_id=1, source_target_pairs={{28,4},{4,12},{12,20},{20,28},{29,5},{5,13},{13,21},{21,29},{30,6}... | collective-permute-start | bytes 368648 | tf_op jit(solution)/shard_map/ppermute | solution.py:271
  112.0 18.2 %all-to-all-start.3 = ((bf16[16,120,256]{2,1,0:T(8,128)(2,1)}), bf16[16,120,256]{2,1,0:T(8,128)(2,1)S(1)}, u32[]{:S(2)}, u32[]{:S(2)}) async-start(bf16[16,120,256]{2,1,0:T(8,128)(2,1)} %broadcast_in_dim.10), calls=%async_computation.3 | async-start | bytes 1966080 | tf_op jit(solution)/shard_map/all_to_all | solution.py:20
  117.7 1.6 copy-start.1
  120.0 20.8 %collective-permute-start.3 = (f32[2,16,240]{2,1,0:T(8,128)S(1)}, f32[2,16,240]{2,1,0:T(8,128)S(1)}, u32[]{:S(2)}, u32[]{:S(2)}) collective-permute-start(f32[2,16,240]{2,1,0:T(8,128)S(1)} %pad_maximum_fusion.3), channel_id=1, source_target_pairs={{0,4},{4,0},{1,5},{5,1},{2,6},{6,2},{3,7},{7,3},{8,12},{12,8},{9,1... | collective-permute-start | bytes 92168 | tf_op jit(solution)/shard_map/ppermute | solution.py:24
  133.8 19.9 %all-to-all-start.4 = ((f32[16,4,240]{2,1,0:T(4,128)}), f32[16,4,240]{2,1,0:T(4,128)S(1)}, u32[]{:S(2)}, u32[]{:S(2)}) async-start(f32[16,4,240]{2,1,0:T(4,128)} %second_layer.1), calls=%async_computation.4 | async-start | bytes 131072 | tf_op jit(solution)/shard_map/all_to_all | solution.py:302
Sparse Core Ops, SparseCore 0:
  40.2 74.5 all-gather.4

commit v7 on v6

--- a/solution.py
+++ b/solution.py
@@ -62,7 +62,7 @@
 
 
 def regroup_kernel(lengths, qkv, out, mats):
-    tail = jnp.full((2, HD), lengths[0].astype(F32)).astype(BF)
+    tail = jnp.broadcast_to(lengths[...].astype(F32), (2, HD)).astype(BF)
     for y in range(NY):
         for m in range(4):
             start = (m * NY + y) * HD if m < 3 else y * HD
@@ -71,6 +71,16 @@
             for c in range(2):
                 mats[2 * y + c, m, 0:30, :] = block
                 mats[2 * y + c, m, 30:32, :] = tail
+
+
+def input_kernel(weights, frames, spread):
+    projected = lax.dot_general(
+        weights[...], frames[...], (((1,), (1,)), ((), ())), preferred_element_type=F32
+    )
+    for y in range(NY):
+        block = projected[y * HD : y * HD + HD, :].astype(BF)
+        for target in range(16):
+            spread[target, y] = block
 
 
 def norm_kernel(scalars, raw, own, gain, normed, mine):
@@ -157,11 +167,23 @@
     return pl.pallas_call(
         regroup_kernel,
         out_shape=jax.ShapeDtypeStruct((2 * NY, 4, 32, HD), BF),
-        in_specs=[SMEM, VMEM, VMEM],
+        in_specs=[VMEM, VMEM, VMEM],
         out_specs=VMEM,
         cost_estimate=cost(0, 400_000),
         name="regroup",
     )(lengths, qkv, out)
+
+
+def run_input(weights, frames):
+    return pl.pallas_call(
+        input_kernel,
+        out_shape=jax.ShapeDtypeStruct((16, NY, HD, 128), BF),
+        in_specs=[VMEM, VMEM],
+        out_specs=VMEM,
+        compiler_params=pltpu.CompilerParams(vmem_limit_bytes=20 << 20),
+        cost_estimate=cost(100_000_000, 3_000_000),
+        name="layer_input",
+    )(weights, frames)
 
 
 def run_norm(scalars, raw, own, gain):
@@ -232,17 +254,13 @@
     xi, yi = lax.axis_index("x"), lax.axis_index("y")
     chunk = xi * NY + yi
 
-    projected = lax.dot_general(
-        feature_proj, frames[0], (((0,), (1,)), ((), ())), preferred_element_type=F32
-    )
-    projected = projected.astype(BF).reshape(1, NY, HD, 128)
-    projected = jnp.broadcast_to(projected, (16, NY, HD, 128))
-
-    mats = run_regroup(lengths, qkv_weight[0], out_weight[0].T)
+    projected = run_input(feature_proj.T, frames[0])
+
+    mats = run_regroup(lengths.reshape(1, 1), qkv_weight[0], out_weight[0].T)
     regrouped = lax.all_to_all(mats, ("y", "c"), 0, 0).reshape(NY, 2, 4, 32, HD)
     gains = lax.all_gather(norm_gain[0], "c", axis=0)
     regrouped, gains, projected = lax.optimization_barrier((regrouped, gains, projected))
-    plane_lengths = regrouped[:, 0, 0, 30, 0].astype(jnp.int32)
+    plane_lengths = jnp.max(regrouped[:, 0, 0, 30].astype(F32), axis=1).astype(jnp.int32)
     my_lengths = lax.dynamic_slice_in_dim(plane_lengths, 2 * core, 2, 0)
 
     def shard(layer):
@@ -301,9 +319,10 @@
 
     packed = lax.all_to_all(packed, "z", 0, 0).reshape(64, 2 * HD)
     part = jnp.einsum("tk,nk->nt", packed, mixed, precision=lax.Precision.HIGHEST)
-    part = jnp.broadcast_to(part.reshape(NY, 1, 16, 64), (NY, 8, 16, 64)).reshape(32, 16, 64)
+    part = jnp.pad(part, ((0, 0), (0, 64))).reshape(NY, 1, 16, 128)
+    part = jnp.broadcast_to(part, (NY, 8, 16, 128)).reshape(32, 16, 128)
     part = lax.all_to_all(part, ("y", "c", "x"), 0, 0)
-    return jnp.sum(part, axis=0).T
+    return jnp.sum(part, axis=0)[:, :64].T
 
 
 def solution(mesh):

time: 178 us -> 171 us (0.961)
  local copies, waits for them, and re-layouts: 14 us -> 9.36 us
  waiting for transfers between devices: 35.3 us -> 32.9 us
  other arithmetic: 3.03 us -> 0.96 us
    optimization_barrier x1 -> x0, local copies, waits for them, and re-layouts: 5.96 us -> none  [body(): lax.optimization_barrier((regrouped, gains, projected))]
    unnamed x13 -> x15, local copies, waits for them, and re-layouts: 2.82 us -> 5.72 us
    all_to_all x1, waiting for transfers between devices: 4.13 us -> 1.84 us  [body(): regrouped = lax.all_to_all(mats, ('y', 'c'), 0, 0).reshape(NY, 2, 4, 32, HD)]
where the time goes in v7:
time: 171 us; the launch traced here: 168 us
  blocking collectives  56.1 us (33%)
  starting transfers between devices  42.4 us (25%)
  waiting for transfers between devices  32.9 us (19%)
  between operations  14.4 us (8%)
  Pallas kernels  10.7 us (6%)
  local copies, waits for them, and re-layouts  9.36 us (5%)
    all_gather x1, blocking collectives, body(): own = lax.all_gather(first_shard, 'z', axis=0)  40.9 us
    all_to_all x1, blocking collectives, body(): part = lax.all_to_all(part, ('y', 'c', 'x'), 0, 0)  13 us
    all_to_all x1, waiting for transfers between devices, body(): packed = lax.all_to_all(packed, 'z', 0, 0).reshape(64, 2 * HD)  12.7 us
    all_to_all x1, waiting for transfers between devices, body(): partial = lax.all_to_all(partial, ('x', 'y'), 0, 0)  9.76 us
    all_to_all x1, waiting for transfers between devices, plane_gather(): return lax.all_to_all(spread, ('x', 'y'), 0, 0)  8.35 us
    all_to_all x1, starting transfers between devices, body(): lax.all_to_all(projected, ('x', 'y'), 0, 0).reshape(4, NY, NY, HD, 128)  8.31 us
    all_to_all x1, starting transfers between devices, body(): packed = lax.all_to_all(packed, 'z', 0, 0).reshape(64, 2 * HD)  7.91 us
    all_to_all x1, starting transfers between devices, body(): partial = lax.all_to_all(partial, ('x', 'y'), 0, 0)  7.36 us
  transfers between devices with their start and end apart: 10, of which 5 were waited for; matrix products, arithmetic and copies ran while one was open for 3% of the time, Pallas kernels for 5%

profile of v7, /device:TPU:6, one launch (start us, length us, event | category | flops | bytes accessed | tf_op | source)
XLA Modules:
  0.0 167.6 jit_solution(8118587749905232678)
XLA Ops:
  7.2 1.7 %regroup.1 = bf16[8,4,32,120]{3,2,1,0:T(8,128)(2,1)} custom-call(s32[1,1]{1,0:T(1,128)} %bitcast.56.lengths, bf16[30,1440]{1,0:T(8,128)(2,1)} %bitcast.77, bf16[30,480]{1,0:T(8,128)(2,1)} %bitcast.79), custom_call_target="tpu_custom_call" | custom-call | bytes 400000 | tf_op jit(solution)/shard_map/regroup/pallas_call | solution.py:167
  8.9 4.5 %all-to-all-start = ((bf16[8,4,32,120]{3,2,1,0:T(8,128)(2,1)}), bf16[8,4,32,120]{3,2,1,0:T(8,128)(2,1)S(1)}, u32[]{:S(2)}, u32[]{:S(2)}) async-start(bf16[8,4,32,120]{3,2,1,0:T(8,128)(2,1)} %regroup.1), calls=%async_computation | async-start | bytes 524288 | tf_op jit(solution)/shard_map/all_to_all | solution.py:260
  13.4 2.2 %all-gather.2 = f32[2,1,1920]{2,1,0:T(1,128)S(1)} all-gather(f32[1,1,1920]{2,1,0:T(1,128)} %bitcast.80), channel_id=1, replica_groups=mesh['z'=16,'y'=4,'c'=2,'x'=4] {'c'}, dimensions={0}, use_global_device_ids=true | all-gather | bytes 23040 | tf_op jit(solution)/shard_map/all_gather | solution.py:261
  15.6 1.0 copy-done.3
  16.6 0.9 copy-done.4
  17.5 0.3 layer_input.1
  17.8 1.2 copy-done
  19.1 1.8 %all-to-all-done = bf16[8,4,32,120]{3,2,1,0:T(8,128)(2,1)S(1)} async-done(((bf16[8,4,32,120]{3,2,1,0:T(8,128)(2,1)}), bf16[8,4,32,120]{3,2,1,0:T(8,128)(2,1)S(1)}, u32[]{:S(2)}, u32[]{:S(2)}) %all-to-all-start) | async-done | bytes 245792 | tf_op jit(solution)/shard_map/all_to_all | solution.py:260
  21.0 8.3 %all-to-all-start.1 = ((bf16[16,4,120,128]{3,2,1,0:T(8,128)(2,1)}), bf16[16,4,120,128]{3,2,1,0:T(8,128)(2,1)S(1)}, u32[]{:S(2)}, u32[]{:S(2)}) async-start(bf16[16,4,120,128]{3,2,1,0:T(8,128)(2,1)} %copy-done), calls=%async_computation.1 | async-start | bytes 3932160 | tf_op jit(solution)/shard_map/all_to_all | solution.py:278
  30.0 0.8 copy.32
  30.9 40.9 %all-gather = bf16[32,120,120]{2,1,0:T(8,128)(2,1)S(1)} all-gather(bf16[2,120,120]{2,1,0:T(8,128)(2,1)S(1)} %copy.30), channel_id=2, replica_groups=mesh['z'=16,'y'=4,'c'=2,'x'=4] {'z'}, dimensions={0}, use_global_device_ids=true | all-gather | bytes 979200 | tf_op jit(solution)/shard_map/all_gather | solution.py:275
  71.8 1.9 %collective-permute-start = (bf16[16,2,120,120]{3,2,1,0:T(8,128)(2,1)S(1)}, bf16[16,2,120,120]{3,2,1,0:T(8,128)(2,1)}, u32[]{:S(2)}, u32[]{:S(2)}) collective-permute-start(bf16[16,2,120,120]{3,2,1,0:T(8,128)(2,1)S(1)} %bitcast.59), channel_id=1, source_target_pairs={{0,4},{4,0},{1,5},{5,1},{2,6},{6,2},{3,7},{7,3},{8,12},{12,8},{9,1... | collective-permute-start | bytes 2764808 | tf_op jit(solution)/shard_map/ppermute | solution.py:24
  74.0 2.2 %first_norm.1 = (bf16[16,120,256]{2,1,0:T(8,128)(2,1)S(1)}, bf16[2,120,256]{2,1,0:T(8,128)(2,1)S(1)}) custom-call(s32[5]{0:T(128)S(1)} %pad_add_fusion.scalars, bf16[4,4,4,120,128]{4,3,2,1,0:T(8,128)(2,1)S(1)} %bitcast.57, bf16[16,2,120,120]{3,2,1,0:T(8,128)(2,1)S(1)} %bitcast.60, f32[16,120]{1,0:T(8,128)S(1)} %squeeze.36.gain), custom_call_target="tpu_custom_call" | custom-call | flops 400000000 | bytes 4000000 | tf_op jit(solution)/shard_map/first_norm/pallas_call | solution.py:190
  76.2 0.2 collective-permute-done.other
  76.4 2.9 %first_attend.1 = (bf16[16,120,256]{2,1,0:T(8,128)(2,1)S(1)}, bf16[120,256]{1,0:T(8,128)(2,1)S(1)}) custom-call(s32[5]{0:T(128)S(1)} %pad_add_fusion.scalars, bf16[4,4,4,120,128]{4,3,2,1,0:T(8,128)(2,1)S(1)} %bitcast.58, bf16[16,120,256]{2,1,0:T(8,128)(2,1)S(1)} %get-tuple-element.22.normed, bf16[2,120,256]{2,1,0:T(8,128)(2,1)S(1)} %get-tuple-element.23.mine, ...), custom_call_target="tpu_custom_call" | custom-call | flops 600000000 | bytes 5000000 | tf_op jit(solution)/shard_map/first_attend/pallas_call | solution.py:205
  79.3 1.0 copy-done.2
  80.3 7.4 %all-to-all-start.2 = ((bf16[16,120,256]{2,1,0:T(8,128)(2,1)}), bf16[16,120,256]{2,1,0:T(8,128)(2,1)S(1)}, u32[]{:S(2)}, u32[]{:S(2)}) async-start(bf16[16,120,256]{2,1,0:T(8,128)(2,1)} %copy-done.2), calls=%async_computation.2 | async-start | bytes 1966080 | tf_op jit(solution)/shard_map/all_to_all | solution.py:291
  88.2 4.6 %collective-permute-start.1 = (f32[16,16,120]{2,1,0:T(8,128)S(1)}, f32[16,16,120]{2,1,0:T(8,128)S(1)}, u32[]{:S(2)}, u32[]{:S(2)}) collective-permute-start(f32[16,16,120]{2,1,0:T(8,128)S(1)} %bitcast.69), channel_id=1, source_target_pairs={{8,0},{20,4},{16,8},{28,12},{24,16},{4,20},{0,24},{12,28},{9,1},{2... | collective-permute-start | bytes 368648 | tf_op jit(solution)/shard_map/ppermute | solution.py:288
  92.7 0.7 collective-permute-start.2
  93.4 9.8 %all-to-all-done.2 = bf16[16,120,256]{2,1,0:T(8,128)(2,1)S(1)} async-done(((bf16[16,120,256]{2,1,0:T(8,128)(2,1)}), bf16[16,120,256]{2,1,0:T(8,128)(2,1)S(1)}, u32[]{:S(2)}, u32[]{:S(2)}) %all-to-all-start.2) | async-done | bytes 983072 | tf_op jit(solution)/shard_map/all_to_all | solution.py:291
  103.3 1.0 broadcast_in_dim.6
  104.4 5.3 %all-to-all-start.3 = ((bf16[16,120,256]{2,1,0:T(8,128)(2,1)}), bf16[16,120,256]{2,1,0:T(8,128)(2,1)S(1)}, u32[]{:S(2)}, u32[]{:S(2)}) async-start(bf16[16,120,256]{2,1,0:T(8,128)(2,1)} %broadcast_in_dim.6), calls=%async_computation.3 | async-start | bytes 1966080 | tf_op jit(solution)/shard_map/all_to_all | solution.py:20
  110.1 1.5 copy-done.1
  111.8 0.5 convolution_bitcast_fusion
  112.3 1.9 %collective-permute-start.3 = (f32[2,16,240]{2,1,0:T(8,128)S(1)}, f32[2,16,240]{2,1,0:T(8,128)S(1)}, u32[]{:S(2)}, u32[]{:S(2)}) collective-permute-start(f32[2,16,240]{2,1,0:T(8,128)S(1)} %pad_maximum_fusion.3), channel_id=1, source_target_pairs={{0,4},{4,0},{1,5},{5,1},{2,6},{6,2},{3,7},{7,3},{8,12},{12,8},{9,1... | collective-permute-start | bytes 92168 | tf_op jit(solution)/shard_map/ppermute | solution.py:24
  114.3 8.4 %all-to-all-done.3.x1 = bf16[16,120,256]{2,1,0:T(8,128)(2,1)S(1)} async-done(((bf16[16,120,256]{2,1,0:T(8,128)(2,1)}), bf16[16,120,256]{2,1,0:T(8,128)(2,1)S(1)}, u32[]{:S(2)}, u32[]{:S(2)}) %all-to-all-start.3) | async-done | bytes 983072 | tf_op jit(solution)/shard_map/all_to_all | solution.py:20
  122.6 3.5 %second_layer.1 = f32[16,4,240]{2,1,0:T(4,128)} custom-call(s32[5]{0:T(128)S(1)} %pad_add_fusion.scalars, bf16[16,120,256]{2,1,0:T(8,128)(2,1)S(1)} %all-to-all-done.3.x1, bf16[16,3,120,120]{3,2,1,0:T(8,128)(2,1)S(1)} %stage.1.weights, f32[16,120]{1,0:T(8,128)S(1)} %squeeze.39.gain, f32[2,120]{1,0:T(2,128)S(1)} %subtract_bitcast_fusion.rest), custom_call_target="tpu_custom_call" | custom-call | flops 1000000000 | bytes 6000000 | tf_op jit(solution)/shard_map/second_layer/pallas_call | solution.py:237
  126.1 7.9 %all-to-all-start.4 = ((f32[16,4,240]{2,1,0:T(4,128)}), f32[16,4,240]{2,1,0:T(4,128)S(1)}, u32[]{:S(2)}, u32[]{:S(2)}) async-start(f32[16,4,240]{2,1,0:T(4,128)} %second_layer.1), calls=%async_computation.4 | async-start | bytes 131072 | tf_op jit(solution)/shard_map/all_to_all | solution.py:320
  134.2 12.7 %all-to-all-done.4 = f32[16,4,240]{2,1,0:T(4,128)S(1)} async-done(((f32[16,4,240]{2,1,0:T(4,128)}), f32[16,4,240]{2,1,0:T(4,128)S(1)}, u32[]{:S(2)}, u32[]{:S(2)}) %all-to-all-start.4) | async-done | bytes 61472 | tf_op jit(solution)/shard_map/all_to_all | solution.py:320
  146.9 0.2 fusion.9
  147.2 13.0 %all_to_all.30 = f32[32,16,128]{2,1,0:T(8,128)S(1)} all-to-all(f32[32,16,128]{2,1,0:T(8,128)S(1)} %bitcast.68), channel_id=1, replica_groups=mesh['z'=16,'y'=4,'c'=2,'x'=4] {'y','c','x'}, dimensions={0} | all-to-all | bytes 524288 | tf_op jit(solution)/shard_map/all_to_all | solution.py:324
  160.2 0.6 slice_bitcast_fusion.4
  (60 shorter events, 2.4 us)
Async XLA Ops:
  8.9 12.0 %all-to-all-start = ((bf16[8,4,32,120]{3,2,1,0:T(8,128)(2,1)}), bf16[8,4,32,120]{3,2,1,0:T(8,128)(2,1)S(1)}, u32[]{:S(2)}, u32[]{:S(2)}) async-start(bf16[8,4,32,120]{3,2,1,0:T(8,128)(2,1)} %regroup.1), calls=%async_computation | async-start | bytes 524288 | tf_op jit(solution)/shard_map/all_to_all | solution.py:260
  15.6 1.0 copy-start.3
  16.6 0.9 copy-start.4
  17.8 1.3 copy-start
  21.0 53.0 %all-to-all-start.1 = ((bf16[16,4,120,128]{3,2,1,0:T(8,128)(2,1)}), bf16[16,4,120,128]{3,2,1,0:T(8,128)(2,1)S(1)}, u32[]{:S(2)}, u32[]{:S(2)}) async-start(bf16[16,4,120,128]{3,2,1,0:T(8,128)(2,1)} %copy-done), calls=%async_computation.1 | async-start | bytes 3932160 | tf_op jit(solution)/shard_map/all_to_all | solution.py:278
  29.3 80.8 %all-gather.5.cloned.1.call-start = ((), (), s32[]{:S(2)}) async-start(), calls=%async_computation.6 | async-start | bytes 2088960 | tf_op jit(solution)/shard_map/all_gather | solution.py:274
  71.8 4.6 %collective-permute-start = (bf16[16,2,120,120]{3,2,1,0:T(8,128)(2,1)S(1)}, bf16[16,2,120,120]{3,2,1,0:T(8,128)(2,1)}, u32[]{:S(2)}, u32[]{:S(2)}) collective-permute-start(bf16[16,2,120,120]{3,2,1,0:T(8,128)(2,1)S(1)} %bitcast.59), channel_id=1, source_target_pairs={{0,4},{4,0},{1,5},{5,1},{2,6},{6,2},{3,7},{7,3},{8,12},{12,8},{9,1... | collective-permute-start | bytes 2764808 | tf_op jit(solution)/shard_map/ppermute | solution.py:24
  79.3 1.0 copy-start.2
  80.3 7.4 %copy-start.5 = (f32[1920,16]{0,1:T(8,128)S(1)}, f32[1920,16]{0,1:T(8,128)}, u32[]{:S(2)}) copy-start(f32[1920,16]{0,1:T(8,128)} %param.15) | copy-start | bytes 368644
  80.3 7.6 %copy-start.6 = (f32[1920]{0:T(1024)S(1)}, f32[1920]{0:T(1024)}, u32[]{:S(2)}) copy-start(f32[1920]{0:T(1024)} %param.14) | copy-start | bytes 23044
  80.3 22.9 %all-to-all-start.2 = ((bf16[16,120,256]{2,1,0:T(8,128)(2,1)}), bf16[16,120,256]{2,1,0:T(8,128)(2,1)S(1)}, u32[]{:S(2)}, u32[]{:S(2)}) async-start(bf16[16,120,256]{2,1,0:T(8,128)(2,1)} %copy-done.2), calls=%async_computation.2 | async-start | bytes 1966080 | tf_op jit(solution)/shard_map/all_to_all | solution.py:291
  88.2 21.5 %collective-permute-start.1 = (f32[16,16,120]{2,1,0:T(8,128)S(1)}, f32[16,16,120]{2,1,0:T(8,128)S(1)}, u32[]{:S(2)}, u32[]{:S(2)}) collective-permute-start(f32[16,16,120]{2,1,0:T(8,128)S(1)} %bitcast.69), channel_id=1, source_target_pairs={{8,0},{20,4},{16,8},{28,12},{24,16},{4,20},{0,24},{12,28},{9,1},{2... | collective-permute-start | bytes 368648 | tf_op jit(solution)/shard_map/ppermute | solution.py:288
  92.7 16.9 %collective-permute-start.2 = (f32[16,16,120]{2,1,0:T(8,128)S(1)}, f32[16,16,120]{2,1,0:T(8,128)S(1)}, u32[]{:S(2)}, u32[]{:S(2)}) collective-permute-start(f32[16,16,120]{2,1,0:T(8,128)S(1)} %bitcast.70), channel_id=1, source_target_pairs={{28,4},{4,12},{12,20},{20,28},{29,5},{5,13},{13,21},{21,29},{30,6}... | collective-permute-start | bytes 368648 | tf_op jit(solution)/shard_map/ppermute | solution.py:289
  104.4 18.2 %all-to-all-start.3 = ((bf16[16,120,256]{2,1,0:T(8,128)(2,1)}), bf16[16,120,256]{2,1,0:T(8,128)(2,1)S(1)}, u32[]{:S(2)}, u32[]{:S(2)}) async-start(bf16[16,120,256]{2,1,0:T(8,128)(2,1)} %broadcast_in_dim.6), calls=%async_computation.3 | async-start | bytes 1966080 | tf_op jit(solution)/shard_map/all_to_all | solution.py:20
  110.1 1.6 copy-start.1
  112.3 21.7 %collective-permute-start.3 = (f32[2,16,240]{2,1,0:T(8,128)S(1)}, f32[2,16,240]{2,1,0:T(8,128)S(1)}, u32[]{:S(2)}, u32[]{:S(2)}) collective-permute-start(f32[2,16,240]{2,1,0:T(8,128)S(1)} %pad_maximum_fusion.3), channel_id=1, source_target_pairs={{0,4},{4,0},{1,5},{5,1},{2,6},{6,2},{3,7},{7,3},{8,12},{12,8},{9,1... | collective-permute-start | bytes 92168 | tf_op jit(solution)/shard_map/ppermute | solution.py:24
  126.1 20.8 %all-to-all-start.4 = ((f32[16,4,240]{2,1,0:T(4,128)}), f32[16,4,240]{2,1,0:T(4,128)S(1)}, u32[]{:S(2)}, u32[]{:S(2)}) async-start(f32[16,4,240]{2,1,0:T(4,128)} %second_layer.1), calls=%async_computation.4 | async-start | bytes 131072 | tf_op jit(solution)/shard_map/all_to_all | solution.py:320
Sparse Core Ops, SparseCore 0:
  32.2 75.2 all-gather.4

commit v8 on v7

--- a/solution.py
+++ b/solution.py
@@ -18,6 +18,16 @@
     count = lax.axis_size("x") * lax.axis_size("y")
     spread = jnp.broadcast_to(block[None], (count,) + block.shape)
     return lax.all_to_all(spread, ("x", "y"), 0, 0)
+
+
+def pass_along(value, distance):
+    count = lax.axis_size("z")
+    pairs = []
+    for z in range(count):
+        for c in range(2):
+            target = (z + (distance if c == 0 else -distance)) % count
+            pairs.append((2 * z + c, 2 * target + c))
+    return lax.ppermute(value, ("z", "c"), pairs)
 
 
 def swap_cores(value):
@@ -44,6 +54,16 @@
     for b in range(CHUNKS):
         total += matmul(weight_ref[b, index], normed_ref[b])
     out_ref[slot] = total.astype(BF)
+
+
+def held(pieces, steps):
+    return [(pieces[step % 3].at[step // 3], step) for step in steps]
+
+
+OWN_STEPS = tuple(range(0, 8))
+OTHER_STEPS = tuple(range(1, 9))
+OWN_AT = 5
+OTHER_AT = 14
 
 
 def attend(query, keys, values, length):
@@ -83,50 +103,43 @@
             spread[target, y] = block
 
 
-def norm_kernel(scalars, raw, own, gain, normed, mine):
+def norm_kernel(scalars, raw, own0, own1, own2, gain, normed, sums):
     core = scalars[0]
     gain_rows = gain[...].T
     for u in range(2):
         picks = [raw[x, 2 * core + u] for x in range(4)]
         values = jnp.concatenate(picks, axis=0)
         normalize(values, gain_rows, normed, utterance(u))
-    project(normed, own, 0, mine, 0)
-    pl.when(core == 0)(lambda: project(normed, own, 1, mine, 1))
+    for index in range(3):
+        total = jnp.zeros((HD, 256), F32)
+        for piece, step in held((own0, own1, own2), OWN_STEPS):
+            total += matmul(piece[index], normed[scalars[OWN_AT + step]])
+        sums[index] = total
 
 
 def attend_kernel(
-    scalars, raw, normed, mine, own, other, partial, kept, rest, context
+    scalars, raw, normed, sums, own0, own1, own2, other0, other1, other2, partial, kept, qkv, context
 ):
     core = scalars[0]
     xi, yi = scalars[1], scalars[2]
+    own = held((own0, own1, own2), OWN_STEPS)
+    other = held((other0, other1, other2), OTHER_STEPS)
     for u in range(2):
         kept[:, utterance(u)] = raw[xi, 2 * core + u, yi]
-
-    def attend_all(query, keys, values):
-        for u in range(2):
-            columns = utterance(u)
-            context[:, columns] = attend(
-                query[:, columns], keys[:, columns], values[:, columns], scalars[3 + u]
-            )
-
-    def out_from(high):
-        for group in range(4):
-            for b in range(4 * group, 4 * group + 4):
-                partial[b] = matmul(high[b, 1], context[...]).astype(BF)
-
-    def on_first():
-        project(normed, other, 0, rest, 0)
-        attend_all(mine.at[0], mine.at[1], rest.at[0])
-        out_from(other)
-
-    def on_second():
-        project(normed, other, 0, rest, 0)
-        project(normed, other, 1, rest, 1)
-        attend_all(rest.at[0], rest.at[1], mine.at[0])
-        out_from(own)
-
-    pl.when(core == 0)(on_first)
-    pl.when(core == 1)(on_second)
+    for index in range(3):
+        total = sums[index]
+        for piece, step in other:
+            total += matmul(piece[index], normed[scalars[OTHER_AT + step]])
+        qkv[index] = total.astype(BF)
+    for u in range(2):
+        columns = utterance(u)
+        context[:, columns] = attend(
+            qkv[0, :, columns], qkv[1, :, columns], qkv[2, :, columns], scalars[3 + u]
+        )
+    for piece, step in own:
+        partial[scalars[OWN_AT + step]] = matmul(piece[3], context[...]).astype(BF)
+    for piece, step in other:
+        partial[scalars[OTHER_AT + step]] = matmul(piece[3], context[...]).astype(BF)
 
 
 def stage_kernel(weights_hbm, staged, arrived):
@@ -191,33 +204,33 @@
         norm_kernel,
         out_shape=(
             jax.ShapeDtypeStruct((CHUNKS, HD, 256), BF),
-            jax.ShapeDtypeStruct((2, HD, 256), BF),
+            jax.ShapeDtypeStruct((3, HD, 256), F32),
         ),
-        in_specs=[SMEM] + [VMEM] * 3,
+        in_specs=[SMEM] + [VMEM] * 5,
         out_specs=(VMEM, VMEM),
         compiler_params=pltpu.CompilerParams(vmem_limit_bytes=20 << 20),
         cost_estimate=cost(400_000_000, 4_000_000),
         name="first_norm",
-    )(scalars, raw, own, gain)
-
-
-def run_attend(scalars, raw, normed, mine, own, other):
+    )(scalars, raw, *own, gain)
+
+
+def run_attend(scalars, raw, normed, sums, own, other):
     return pl.pallas_call(
         attend_kernel,
         out_shape=(
             jax.ShapeDtypeStruct((CHUNKS, HD, 256), BF),
             jax.ShapeDtypeStruct((HD, 256), BF),
         ),
-        in_specs=[SMEM] + [VMEM] * 5,
+        in_specs=[SMEM] + [VMEM] * 9,
         out_specs=(VMEM, VMEM),
         scratch_shapes=[
-            pltpu.VMEM((2, HD, 256), BF),
+            pltpu.VMEM((3, HD, 256), BF),
             pltpu.VMEM((HD, 256), BF),
         ],
         compiler_params=pltpu.CompilerParams(vmem_limit_bytes=20 << 20),
         cost_estimate=cost(600_000_000, 5_000_000),
         name="first_attend",
-    )(scalars, raw, normed, mine, own, other)
+    )(scalars, raw, normed, sums, *own, *other)
 
 
 def run_stage(weights):
@@ -267,20 +280,29 @@
         rows = regrouped[:, layer, :, :30].transpose(1, 0, 2, 3).reshape(4, HD, HD)
         return jnp.concatenate([rows[:3].transpose(0, 2, 1), rows[3:]], axis=0)
 
-    first_shard = lax.dynamic_slice_in_dim(shard(0), 2 * core, 2, 0)
     first_shard, second_shard, my_lengths = lax.optimization_barrier(
-        (first_shard, shard(1), my_lengths)
+        (shard(0), shard(1), my_lengths)
     )
     second_weights = lax.all_gather(second_shard, "z", axis=0)
-    own = lax.all_gather(first_shard, "z", axis=0)
-    other = swap_cores(own)
+    by_three = jnp.stack(
+        [first_shard, pass_along(first_shard, 3), pass_along(first_shard, 6)]
+    )
+    own = (by_three, pass_along(by_three, 1), pass_along(by_three, 2))
+    other = tuple(swap_cores(piece) for piece in own)
+    sign = 2 * core - 1
+    steps = jnp.arange(9, dtype=jnp.int32)
+    zi = lax.axis_index("z")
+    own_at = (zi + sign * steps) % CHUNKS
+    other_at = (zi - sign * steps) % CHUNKS
 
     raw = lax.all_to_all(projected, ("x", "y"), 0, 0).reshape(4, NY, NY, HD, 128)
 
-    scalars = jnp.concatenate([jnp.stack([core, xi, yi]).astype(jnp.int32), my_lengths])
+    scalars = jnp.concatenate(
+        [jnp.stack([core, xi, yi]).astype(jnp.int32), my_lengths, own_at, other_at]
+    )
     gains = gains.reshape(2, CHUNKS, HD)
-    normed, mine = run_norm(scalars, raw, own, gains[0])
-    partial, x0_own = run_attend(scalars, raw, normed, mine, own, other)
+    normed, sums = run_norm(scalars, raw, own, gains[0])
+    partial, x0_own = run_attend(scalars, raw, normed, sums, own, other)
     white = whitening.T.reshape(16, CHUNKS, HD).transpose(1, 0, 2)
     x0_own, white = lax.optimization_barrier((x0_own, white))
     near = [(((y + 1 + c) % NY) * 2 + c, y * 2 + c) for y in range(NY) for c in range(2)]

time: 171 us -> 184 us (1.076)
  blocking collectives: 56.1 us -> 15.3 us
  starting transfers between devices: 42.4 us -> 77.5 us
  waiting for transfers between devices: 32.9 us -> 51.9 us
    all_gather x1 -> x0, blocking collectives: 40.9 us -> none  [body(): own = lax.all_gather(first_shard, 'z', axis=0)]
    ppermute x0 -> x4, starting transfers between devices: none -> 21.5 us  [pass_along(): return lax.ppermute(value, ('z', 'c'), pairs)]
    ppermute x0 -> x4, waiting for transfers between devices: none -> 19.4 us  [pass_along(): return lax.ppermute(value, ('z', 'c'), pairs)]
    all_to_all x1, starting transfers between devices: 7.91 us -> 15.1 us  [body(): packed = lax.all_to_all(packed, 'z', 0, 0).reshape(64, 2 * HD)]
    ppermute x2 -> x4, starting transfers between devices: 3.82 us -> 10.2 us  [swap_cores(): return lax.ppermute(value, 'c', [(0, 1), (1, 0)])]
  transfers between devices with their start and end apart: 10 -> 16, of which waited for: 5 -> 7; matrix products, arithmetic and copies ran while one was open for 3% -> 2% of each run, Pallas kernels for 5% -> 5%
where the time goes in v8:
time: 184 us; the launch traced here: 181 us
  starting transfers between devices  77.5 us (42%)
  waiting for transfers between devices  51.9 us (28%)
  blocking collectives  15.3 us (8%)
  between operations  14.5 us (8%)
  Pallas kernels  10.3 us (6%)
  local copies, waits for them, and re-layouts  9.34 us (5%)
    ppermute x4, starting transfers between devices, pass_along(): return lax.ppermute(value, ('z', 'c'), pairs)  21.5 us
    ppermute x4, waiting for transfers between devices, pass_along(): return lax.ppermute(value, ('z', 'c'), pairs)  19.4 us
    all_to_all x1, starting transfers between devices, body(): packed = lax.all_to_all(packed, 'z', 0, 0).reshape(64, 2 * HD)  15.1 us
    all_to_all x1, blocking collectives, body(): part = lax.all_to_all(part, ('y', 'c', 'x'), 0, 0)  13.1 us
    all_to_all x1, waiting for transfers between devices, body(): packed = lax.all_to_all(packed, 'z', 0, 0).reshape(64, 2 * HD)  12.6 us
    ppermute x4, starting transfers between devices, swap_cores(): return lax.ppermute(value, 'c', [(0, 1), (1, 0)])  10.2 us
    all_to_all x1, waiting for transfers between devices, body(): partial = lax.all_to_all(partial, ('x', 'y'), 0, 0)  9.74 us
    all_to_all x1, waiting for transfers between devices, plane_gather(): return lax.all_to_all(spread, ('x', 'y'), 0, 0)  8.31 us
  transfers between devices with their start and end apart: 16, of which 7 were waited for; matrix products, arithmetic and copies ran while one was open for 2% of the time, Pallas kernels for 5%

profile of v8, /device:TPU:6, one launch (start us, length us, event | category | flops | bytes accessed | tf_op | source)
XLA Modules:
  0.0 180.6 jit_solution(3349904669858865944)
XLA Ops:
  7.2 1.7 regroup.1
  8.9 4.5 %all-to-all-start = ((bf16[8,4,32,120]{3,2,1,0:T(8,128)(2,1)}), bf16[8,4,32,120]{3,2,1,0:T(8,128)(2,1)S(1)}, u32[]{:S(2)}, u32[]{:S(2)}) async-start(bf16[8,4,32,120]{3,2,1,0:T(8,128)(2,1)} %regroup.1), calls=%async_computation | async-start | bytes 524288 | tf_op jit(solution)/shard_map/all_to_all | solution.py:273
  13.4 2.2 %all-gather.1 = f32[2,1,1920]{2,1,0:T(1,128)S(1)} all-gather(f32[1,1,1920]{2,1,0:T(1,128)} %bitcast.82), channel_id=1, replica_groups=mesh['z'=16,'y'=4,'c'=2,'x'=4] {'c'}, dimensions={0}, use_global_device_ids=true | all-gather | bytes 23040 | tf_op jit(solution)/shard_map/all_gather | solution.py:274
  15.6 1.0 copy-done.3
  17.8 1.3 copy-done
  19.1 1.8 %all-to-all-done = bf16[8,4,32,120]{3,2,1,0:T(8,128)(2,1)S(1)} async-done(((bf16[8,4,32,120]{3,2,1,0:T(8,128)(2,1)}), bf16[8,4,32,120]{3,2,1,0:T(8,128)(2,1)S(1)}, u32[]{:S(2)}, u32[]{:S(2)}) %all-to-all-start) | async-done | bytes 245792 | tf_op jit(solution)/shard_map/all_to_all | solution.py:273
  20.9 8.3 %all-to-all-start.1 = ((bf16[16,4,120,128]{3,2,1,0:T(8,128)(2,1)}), bf16[16,4,120,128]{3,2,1,0:T(8,128)(2,1)S(1)}, u32[]{:S(2)}, u32[]{:S(2)}) async-start(bf16[16,4,120,128]{3,2,1,0:T(8,128)(2,1)} %copy-done), calls=%async_computation.1 | async-start | bytes 3932160 | tf_op jit(solution)/shard_map/all_to_all | solution.py:298
  30.8 4.0 %collective-permute-start = (bf16[4,120,120]{2,1,0:T(8,128)(2,1)S(1)}, bf16[4,120,120]{2,1,0:T(8,128)(2,1)S(1)}, u32[]{:S(2)}, u32[]{:S(2)}) collective-permute-start(bf16[4,120,120]{2,1,0:T(8,128)(2,1)S(1)} %pad_maximum_fusion.3), channel_id=1, source_target_pairs={{0,96},{4,420},{32,128},{36,452},{64,160},{68,484},{96,192},{100,4... | collective-permute-start | bytes 345608 | tf_op jit(solution)/shard_map/ppermute | solution.py:30
  34.8 12.1 %collective-permute-start.1 = (bf16[4,120,120]{2,1,0:T(8,128)(2,1)S(1)}, bf16[4,120,120]{2,1,0:T(8,128)(2,1)S(1)}, u32[]{:S(2)}, u32[]{:S(2)}) collective-permute-start(bf16[4,120,120]{2,1,0:T(8,128)(2,1)S(1)} %pad_maximum_fusion.3), channel_id=1, source_target_pairs={{0,192},{4,324},{32,224},{36,356},{64,256},{68,388},{96,288},{100,... | collective-permute-start | bytes 345608 | tf_op jit(solution)/shard_map/ppermute | solution.py:30
  46.9 10.6 %collective-permute-done.1 = bf16[4,120,120]{2,1,0:T(8,128)(2,1)S(1)} collective-permute-done((bf16[4,120,120]{2,1,0:T(8,128)(2,1)S(1)}, bf16[4,120,120]{2,1,0:T(8,128)(2,1)S(1)}, u32[]{:S(2)}, u32[]{:S(2)}) %collective-permute-start.1) | collective-permute-done | bytes 115232 | tf_op jit(solution)/shard_map/ppermute | solution.py:30
  57.6 3.4 %collective-permute-start.2 = (bf16[3,4,120,120]{3,2,1,0:T(8,128)(2,1)S(1)}, bf16[3,4,120,120]{3,2,1,0:T(8,128)(2,1)S(1)}, u32[]{:S(2)}, u32[]{:S(2)}) collective-permute-start(bf16[3,4,120,120]{3,2,1,0:T(8,128)(2,1)S(1)} %pad_maximum_fusion.own0), channel_id=1, source_target_pairs={{0,32},{4,484},{32,64},{36,4},{64,96},{68,36},{96,128},{100,68},{1... | collective-permute-start | bytes 1036808 | tf_op jit(solution)/shard_map/ppermute | solution.py:30
  61.1 1.9 %collective-permute-start.3 = (bf16[3,4,120,120]{3,2,1,0:T(8,128)(2,1)S(1)}, bf16[3,4,120,120]{3,2,1,0:T(8,128)(2,1)S(1)}, u32[]{:S(2)}, u32[]{:S(2)}) collective-permute-start(bf16[3,4,120,120]{3,2,1,0:T(8,128)(2,1)S(1)} %pad_maximum_fusion.own0), channel_id=1, source_target_pairs={{0,64},{4,452},{32,96},{36,484},{64,128},{68,4},{96,160},{100,36},... | collective-permute-start | bytes 1036808 | tf_op jit(solution)/shard_map/ppermute | solution.py:30
  63.0 3.9 %collective-permute-start.4 = (bf16[3,4,120,120]{3,2,1,0:T(8,128)(2,1)S(1)}, bf16[3,4,120,120]{3,2,1,0:T(8,128)(2,1)S(1)}, u32[]{:S(2)}, u32[]{:S(2)}) collective-permute-start(bf16[3,4,120,120]{3,2,1,0:T(8,128)(2,1)S(1)} %pad_maximum_fusion.own0), channel_id=1, source_target_pairs={{0,4},{4,0},{1,5},{5,1},{2,6},{6,2},{3,7},{7,3},{8,12},{12,8},{9,1... | collective-permute-start | bytes 1036808 | tf_op jit(solution)/shard_map/ppermute | solution.py:34
  66.9 5.6 %collective-permute-done.2.own1 = bf16[3,4,120,120]{3,2,1,0:T(8,128)(2,1)S(1)} collective-permute-done((bf16[3,4,120,120]{3,2,1,0:T(8,128)(2,1)S(1)}, bf16[3,4,120,120]{3,2,1,0:T(8,128)(2,1)S(1)}, u32[]{:S(2)}, u32[]{:S(2)}) %collective-permute-start.2) | collective-permute-done | bytes 345632 | tf_op jit(solution)/shard_map/ppermute | solution.py:30
  72.5 1.9 %collective-permute-start.5 = (bf16[3,4,120,120]{3,2,1,0:T(8,128)(2,1)S(1)}, bf16[3,4,120,120]{3,2,1,0:T(8,128)(2,1)}, u32[]{:S(2)}, u32[]{:S(2)}) collective-permute-start(bf16[3,4,120,120]{3,2,1,0:T(8,128)(2,1)S(1)} %collective-permute-done.2.own1), channel_id=1, source_target_pairs={{0,4},{4,0},{1,5},{5,1},{2,6},{6,2},{3,7},{7,3},{8,12},{12,8},{9,1... | collective-permute-start | bytes 1036808 | tf_op jit(solution)/shard_map/ppermute | solution.py:34
  74.4 3.3 %collective-permute-done.3.own2 = bf16[3,4,120,120]{3,2,1,0:T(8,128)(2,1)S(1)} collective-permute-done((bf16[3,4,120,120]{3,2,1,0:T(8,128)(2,1)S(1)}, bf16[3,4,120,120]{3,2,1,0:T(8,128)(2,1)S(1)}, u32[]{:S(2)}, u32[]{:S(2)}) %collective-permute-start.3) | collective-permute-done | bytes 345632 | tf_op jit(solution)/shard_map/ppermute | solution.py:30
  77.6 2.5 %collective-permute-start.6 = (bf16[3,4,120,120]{3,2,1,0:T(8,128)(2,1)S(1)}, bf16[3,4,120,120]{3,2,1,0:T(8,128)(2,1)}, u32[]{:S(2)}, u32[]{:S(2)}) collective-permute-start(bf16[3,4,120,120]{3,2,1,0:T(8,128)(2,1)S(1)} %collective-permute-done.3.own2), channel_id=1, source_target_pairs={{0,4},{4,0},{1,5},{5,1},{2,6},{6,2},{3,7},{7,3},{8,12},{12,8},{9,1... | collective-permute-start | bytes 1036808 | tf_op jit(solution)/shard_map/ppermute | solution.py:34
  80.4 2.0 %first_norm.1 = (bf16[16,120,256]{2,1,0:T(8,128)(2,1)S(1)}, f32[3,120,256]{2,1,0:T(8,128)S(1)}) custom-call(s32[23]{0:T(128)S(1)} %concatenate.17.scalars, bf16[4,4,4,120,128]{4,3,2,1,0:T(8,128)(2,1)S(1)} %bitcast.59, bf16[3,4,120,120]{3,2,1,0:T(8,128)(2,1)S(1)} %pad_maximum_fusion.own0, bf16[3,4,120,120]{3,2,1,0:T(8,128)(2,1)S(1)} %collective-permute-done.2.own1, ...), custom_call_target="tpu_custom_call" | custom-call | flops 400000000 | bytes 4000000 | tf_op jit(solution)/shard_map/first_norm/pallas_call | solution.py:203
  82.5 2.7 %first_attend.1 = (bf16[16,120,256]{2,1,0:T(8,128)(2,1)S(1)}, bf16[120,256]{1,0:T(8,128)(2,1)S(1)}) custom-call(s32[23]{0:T(128)S(1)} %concatenate.17.scalars, bf16[4,4,4,120,128]{4,3,2,1,0:T(8,128)(2,1)S(1)} %bitcast.60, bf16[16,120,256]{2,1,0:T(8,128)(2,1)S(1)} %get-tuple-element.22.normed, f32[3,120,256]{2,1,0:T(8,128)S(1)} %get-tuple-element.23.sums, ...), custom_call_target="tpu_custom_call" | custom-call | flops 600000000 | bytes 5000000 | tf_op jit(solution)/shard_map/first_attend/pallas_call | solution.py:218
  85.2 1.0 copy-done.2
  86.2 7.4 %all-to-all-start.2 = ((bf16[16,120,256]{2,1,0:T(8,128)(2,1)}), bf16[16,120,256]{2,1,0:T(8,128)(2,1)S(1)}, u32[]{:S(2)}, u32[]{:S(2)}) async-start(bf16[16,120,256]{2,1,0:T(8,128)(2,1)} %copy-done.2), calls=%async_computation.2 | async-start | bytes 1966080 | tf_op jit(solution)/shard_map/all_to_all | solution.py:313
  94.0 4.6 %collective-permute-start.7 = (f32[16,16,120]{2,1,0:T(8,128)S(1)}, f32[16,16,120]{2,1,0:T(8,128)S(1)}, u32[]{:S(2)}, u32[]{:S(2)}) collective-permute-start(f32[16,16,120]{2,1,0:T(8,128)S(1)} %bitcast.68), channel_id=1, source_target_pairs={{8,0},{20,4},{16,8},{28,12},{24,16},{4,20},{0,24},{12,28},{9,1},{2... | collective-permute-start | bytes 368648 | tf_op jit(solution)/shard_map/ppermute | solution.py:310
  99.3 9.7 %all-to-all-done.2 = bf16[16,120,256]{2,1,0:T(8,128)(2,1)S(1)} async-done(((bf16[16,120,256]{2,1,0:T(8,128)(2,1)}), bf16[16,120,256]{2,1,0:T(8,128)(2,1)S(1)}, u32[]{:S(2)}, u32[]{:S(2)}) %all-to-all-start.2) | async-done | bytes 983072 | tf_op jit(solution)/shard_map/all_to_all | solution.py:313
  109.2 1.0 broadcast_in_dim.6
  110.2 5.3 %all-to-all-start.3 = ((bf16[16,120,256]{2,1,0:T(8,128)(2,1)}), bf16[16,120,256]{2,1,0:T(8,128)(2,1)S(1)}, u32[]{:S(2)}, u32[]{:S(2)}) async-start(bf16[16,120,256]{2,1,0:T(8,128)(2,1)} %broadcast_in_dim.6), calls=%async_computation.3 | async-start | bytes 1966080 | tf_op jit(solution)/shard_map/all_to_all | solution.py:20
  115.9 1.5 copy-done.1
  118.2 1.9 %collective-permute-start.9 = (f32[2,16,240]{2,1,0:T(8,128)S(1)}, f32[2,16,240]{2,1,0:T(8,128)S(1)}, u32[]{:S(2)}, u32[]{:S(2)}) collective-permute-start(f32[2,16,240]{2,1,0:T(8,128)S(1)} %pad_maximum_fusion.5), channel_id=1, source_target_pairs={{0,4},{4,0},{1,5},{5,1},{2,6},{6,2},{3,7},{7,3},{8,12},{12,8},{9,1... | collective-permute-start | bytes 92168 | tf_op jit(solution)/shard_map/ppermute | solution.py:34
  120.1 8.3 %all-to-all-done.3.x1 = bf16[16,120,256]{2,1,0:T(8,128)(2,1)S(1)} async-done(((bf16[16,120,256]{2,1,0:T(8,128)(2,1)}), bf16[16,120,256]{2,1,0:T(8,128)(2,1)S(1)}, u32[]{:S(2)}, u32[]{:S(2)}) %all-to-all-start.3) | async-done | bytes 983072 | tf_op jit(solution)/shard_map/all_to_all | solution.py:20
  128.4 3.5 %second_layer.1 = f32[16,4,240]{2,1,0:T(4,128)} custom-call(s32[23]{0:T(128)S(1)} %concatenate.17.scalars, bf16[16,120,256]{2,1,0:T(8,128)(2,1)S(1)} %all-to-all-done.3.x1, bf16[16,3,120,120]{3,2,1,0:T(8,128)(2,1)S(1)} %stage.1.weights, f32[16,120]{1,0:T(8,128)S(1)} %squeeze.39.gain, f32[2,120]{1,0:T(2,128)S(1)} %subtract_bitcast_fusion.rest), custom_call_target="tpu_custom_call" | custom-call | flops 1000000000 | bytes 6000000 | tf_op jit(solution)/shard_map/second_layer/pallas_call | solution.py:250
  131.9 15.1 %all-to-all-start.4 = ((f32[16,4,240]{2,1,0:T(4,128)}), f32[16,4,240]{2,1,0:T(4,128)S(1)}, u32[]{:S(2)}, u32[]{:S(2)}) async-start(f32[16,4,240]{2,1,0:T(4,128)} %second_layer.1), calls=%async_computation.4 | async-start | bytes 131072 | tf_op jit(solution)/shard_map/all_to_all | solution.py:342
  147.2 12.6 %all-to-all-done.4 = f32[16,4,240]{2,1,0:T(4,128)S(1)} async-done(((f32[16,4,240]{2,1,0:T(4,128)}), f32[16,4,240]{2,1,0:T(4,128)S(1)}, u32[]{:S(2)}, u32[]{:S(2)}) %all-to-all-start.4) | async-done | bytes 61472 | tf_op jit(solution)/shard_map/all_to_all | solution.py:342
  160.1 13.1 %all_to_all.30 = f32[32,16,128]{2,1,0:T(8,128)S(1)} all-to-all(f32[32,16,128]{2,1,0:T(8,128)S(1)} %bitcast.67), channel_id=1, replica_groups=mesh['z'=16,'y'=4,'c'=2,'x'=4] {'y','c','x'}, dimensions={0} | all-to-all | bytes 524288 | tf_op jit(solution)/shard_map/all_to_all | solution.py:346
  (72 shorter events, 6.4 us)
Async XLA Ops:
  8.9 12.0 %all-to-all-start = ((bf16[8,4,32,120]{3,2,1,0:T(8,128)(2,1)}), bf16[8,4,32,120]{3,2,1,0:T(8,128)(2,1)S(1)}, u32[]{:S(2)}, u32[]{:S(2)}) async-start(bf16[8,4,32,120]{3,2,1,0:T(8,128)(2,1)} %regroup.1), calls=%async_computation | async-start | bytes 524288 | tf_op jit(solution)/shard_map/all_to_all | solution.py:273
  15.6 1.0 copy-start.3
  16.6 0.9 copy-start.4
  17.8 1.3 copy-start
  20.9 59.5 %all-to-all-start.1 = ((bf16[16,4,120,128]{3,2,1,0:T(8,128)(2,1)}), bf16[16,4,120,128]{3,2,1,0:T(8,128)(2,1)S(1)}, u32[]{:S(2)}, u32[]{:S(2)}) async-start(bf16[16,4,120,128]{3,2,1,0:T(8,128)(2,1)} %copy-done), calls=%async_computation.1 | async-start | bytes 3932160 | tf_op jit(solution)/shard_map/all_to_all | solution.py:298
  29.2 86.7 %all-gather.4.cloned.1.call-start = ((), (), s32[]{:S(2)}) async-start(), calls=%async_computation.6 | async-start | bytes 2088960 | tf_op jit(solution)/shard_map/all_gather | solution.py:286
  30.8 16.1 %collective-permute-start = (bf16[4,120,120]{2,1,0:T(8,128)(2,1)S(1)}, bf16[4,120,120]{2,1,0:T(8,128)(2,1)S(1)}, u32[]{:S(2)}, u32[]{:S(2)}) collective-permute-start(bf16[4,120,120]{2,1,0:T(8,128)(2,1)S(1)} %pad_maximum_fusion.3), channel_id=1, source_target_pairs={{0,96},{4,420},{32,128},{36,452},{64,160},{68,484},{96,192},{100,4... | collective-permute-start | bytes 345608 | tf_op jit(solution)/shard_map/ppermute | solution.py:30
  34.8 22.7 %collective-permute-start.1 = (bf16[4,120,120]{2,1,0:T(8,128)(2,1)S(1)}, bf16[4,120,120]{2,1,0:T(8,128)(2,1)S(1)}, u32[]{:S(2)}, u32[]{:S(2)}) collective-permute-start(bf16[4,120,120]{2,1,0:T(8,128)(2,1)S(1)} %pad_maximum_fusion.3), channel_id=1, source_target_pairs={{0,192},{4,324},{32,224},{36,356},{64,256},{68,388},{96,288},{100,... | collective-permute-start | bytes 345608 | tf_op jit(solution)/shard_map/ppermute | solution.py:30
  57.6 14.8 %collective-permute-start.2 = (bf16[3,4,120,120]{3,2,1,0:T(8,128)(2,1)S(1)}, bf16[3,4,120,120]{3,2,1,0:T(8,128)(2,1)S(1)}, u32[]{:S(2)}, u32[]{:S(2)}) collective-permute-start(bf16[3,4,120,120]{3,2,1,0:T(8,128)(2,1)S(1)} %pad_maximum_fusion.own0), channel_id=1, source_target_pairs={{0,32},{4,484},{32,64},{36,4},{64,96},{68,36},{96,128},{100,68},{1... | collective-permute-start | bytes 1036808 | tf_op jit(solution)/shard_map/ppermute | solution.py:30
  61.1 16.6 %collective-permute-start.3 = (bf16[3,4,120,120]{3,2,1,0:T(8,128)(2,1)S(1)}, bf16[3,4,120,120]{3,2,1,0:T(8,128)(2,1)S(1)}, u32[]{:S(2)}, u32[]{:S(2)}) collective-permute-start(bf16[3,4,120,120]{3,2,1,0:T(8,128)(2,1)S(1)} %pad_maximum_fusion.own0), channel_id=1, source_target_pairs={{0,64},{4,452},{32,96},{36,484},{64,128},{68,4},{96,160},{100,36},... | collective-permute-start | bytes 1036808 | tf_op jit(solution)/shard_map/ppermute | solution.py:30
  63.0 19.5 %collective-permute-start.4 = (bf16[3,4,120,120]{3,2,1,0:T(8,128)(2,1)S(1)}, bf16[3,4,120,120]{3,2,1,0:T(8,128)(2,1)S(1)}, u32[]{:S(2)}, u32[]{:S(2)}) collective-permute-start(bf16[3,4,120,120]{3,2,1,0:T(8,128)(2,1)S(1)} %pad_maximum_fusion.own0), channel_id=1, source_target_pairs={{0,4},{4,0},{1,5},{5,1},{2,6},{6,2},{3,7},{7,3},{8,12},{12,8},{9,1... | collective-permute-start | bytes 1036808 | tf_op jit(solution)/shard_map/ppermute | solution.py:34
  72.5 10.0 %collective-permute-start.5 = (bf16[3,4,120,120]{3,2,1,0:T(8,128)(2,1)S(1)}, bf16[3,4,120,120]{3,2,1,0:T(8,128)(2,1)}, u32[]{:S(2)}, u32[]{:S(2)}) collective-permute-start(bf16[3,4,120,120]{3,2,1,0:T(8,128)(2,1)S(1)} %collective-permute-done.2.own1), channel_id=1, source_target_pairs={{0,4},{4,0},{1,5},{5,1},{2,6},{6,2},{3,7},{7,3},{8,12},{12,8},{9,1... | collective-permute-start | bytes 1036808 | tf_op jit(solution)/shard_map/ppermute | solution.py:34
  77.6 4.8 %collective-permute-start.6 = (bf16[3,4,120,120]{3,2,1,0:T(8,128)(2,1)S(1)}, bf16[3,4,120,120]{3,2,1,0:T(8,128)(2,1)}, u32[]{:S(2)}, u32[]{:S(2)}) collective-permute-start(bf16[3,4,120,120]{3,2,1,0:T(8,128)(2,1)S(1)} %collective-permute-done.3.own2), channel_id=1, source_target_pairs={{0,4},{4,0},{1,5},{5,1},{2,6},{6,2},{3,7},{7,3},{8,12},{12,8},{9,1... | collective-permute-start | bytes 1036808 | tf_op jit(solution)/shard_map/ppermute | solution.py:34
  85.2 1.0 copy-start.2
  86.2 7.4 %copy-start.5 = (f32[1920,16]{0,1:T(8,128)S(1)}, f32[1920,16]{0,1:T(8,128)}, u32[]{:S(2)}) copy-start(f32[1920,16]{0,1:T(8,128)} %param.15) | copy-start | bytes 368644
  86.2 7.6 %copy-start.6 = (f32[1920]{0:T(1024)S(1)}, f32[1920]{0:T(1024)}, u32[]{:S(2)}) copy-start(f32[1920]{0:T(1024)} %param.14) | copy-start | bytes 23044
  86.2 22.9 %all-to-all-start.2 = ((bf16[16,120,256]{2,1,0:T(8,128)(2,1)}), bf16[16,120,256]{2,1,0:T(8,128)(2,1)S(1)}, u32[]{:S(2)}, u32[]{:S(2)}) async-start(bf16[16,120,256]{2,1,0:T(8,128)(2,1)} %copy-done.2), calls=%async_computation.2 | async-start | bytes 1966080 | tf_op jit(solution)/shard_map/all_to_all | solution.py:313
  94.0 21.4 %collective-permute-start.7 = (f32[16,16,120]{2,1,0:T(8,128)S(1)}, f32[16,16,120]{2,1,0:T(8,128)S(1)}, u32[]{:S(2)}, u32[]{:S(2)}) collective-permute-start(f32[16,16,120]{2,1,0:T(8,128)S(1)} %bitcast.68), channel_id=1, source_target_pairs={{8,0},{20,4},{16,8},{28,12},{24,16},{4,20},{0,24},{12,28},{9,1},{2... | collective-permute-start | bytes 368648 | tf_op jit(solution)/shard_map/ppermute | solution.py:310
  98.6 16.9 %collective-permute-start.8 = (f32[16,16,120]{2,1,0:T(8,128)S(1)}, f32[16,16,120]{2,1,0:T(8,128)S(1)}, u32[]{:S(2)}, u32[]{:S(2)}) collective-permute-start(f32[16,16,120]{2,1,0:T(8,128)S(1)} %bitcast.69), channel_id=1, source_target_pairs={{28,4},{4,12},{12,20},{20,28},{29,5},{5,13},{13,21},{21,29},{30,6}... | collective-permute-start | bytes 368648 | tf_op jit(solution)/shard_map/ppermute | solution.py:311
  110.2 18.2 %all-to-all-start.3 = ((bf16[16,120,256]{2,1,0:T(8,128)(2,1)}), bf16[16,120,256]{2,1,0:T(8,128)(2,1)S(1)}, u32[]{:S(2)}, u32[]{:S(2)}) async-start(bf16[16,120,256]{2,1,0:T(8,128)(2,1)} %broadcast_in_dim.6), calls=%async_computation.3 | async-start | bytes 1966080 | tf_op jit(solution)/shard_map/all_to_all | solution.py:20
  115.9 1.6 copy-start.1
  118.2 28.9 %collective-permute-start.9 = (f32[2,16,240]{2,1,0:T(8,128)S(1)}, f32[2,16,240]{2,1,0:T(8,128)S(1)}, u32[]{:S(2)}, u32[]{:S(2)}) collective-permute-start(f32[2,16,240]{2,1,0:T(8,128)S(1)} %pad_maximum_fusion.5), channel_id=1, source_target_pairs={{0,4},{4,0},{1,5},{5,1},{2,6},{6,2},{3,7},{7,3},{8,12},{12,8},{9,1... | collective-permute-start | bytes 92168 | tf_op jit(solution)/shard_map/ppermute | solution.py:34
  131.9 27.9 %all-to-all-start.4 = ((f32[16,4,240]{2,1,0:T(4,128)}), f32[16,4,240]{2,1,0:T(4,128)S(1)}, u32[]{:S(2)}, u32[]{:S(2)}) async-start(f32[16,4,240]{2,1,0:T(4,128)} %second_layer.1), calls=%async_computation.4 | async-start | bytes 131072 | tf_op jit(solution)/shard_map/all_to_all | solution.py:342
Sparse Core Ops, SparseCore 0:
  32.2 79.4 all-gather.3

commit v9 on v7

--- a/solution.py
+++ b/solution.py
@@ -12,12 +12,6 @@
 F32 = jnp.float32
 VMEM = pl.BlockSpec(memory_space=pltpu.VMEM)
 SMEM = pl.BlockSpec(memory_space=pltpu.SMEM)
-
-
-def plane_gather(block):
-    count = lax.axis_size("x") * lax.axis_size("y")
-    spread = jnp.broadcast_to(block[None], (count,) + block.shape)
-    return lax.all_to_all(spread, ("x", "y"), 0, 0)
 
 
 def swap_cores(value):
@@ -95,7 +89,7 @@
 
 
 def attend_kernel(
-    scalars, raw, normed, mine, own, other, partial, kept, rest, context
+    scalars, raw, normed, mine, own, other, partial_hbm, kept, rest, context, partial, sent
 ):
     core = scalars[0]
     xi, yi = scalars[1], scalars[2]
@@ -110,9 +104,17 @@
             )
 
     def out_from(high):
+        copies = []
         for group in range(4):
+            chunks = pl.ds(4 * group, 4)
             for b in range(4 * group, 4 * group + 4):
                 partial[b] = matmul(high[b, 1], context[...]).astype(BF)
+            copies.append(
+                pltpu.make_async_copy(partial.at[chunks], partial_hbm.at[chunks], sent.at[group])
+            )
+            copies[-1].start()
+        for copy in copies:
+            copy.wait()
 
     def on_first():
         project(normed, other, 0, rest, 0)
@@ -127,6 +129,21 @@
 
     pl.when(core == 0)(on_first)
     pl.when(core == 1)(on_second)
+
+
+def combine_kernel(partial, kept, spread, result, sent):
+    total = partial[0].astype(F32)
+    for head in range(1, CHUNKS):
+        total += partial[head].astype(F32)
+    result[...] = (kept[...].astype(F32) + total).astype(BF)
+    copies = [
+        pltpu.make_async_copy(result, spread.at[target], sent.at[target])
+        for target in range(CHUNKS)
+    ]
+    for copy in copies:
+        copy.start()
+    for copy in copies:
+        copy.wait()
 
 
 def stage_kernel(weights_hbm, staged, arrived):
@@ -205,19 +222,37 @@
     return pl.pallas_call(
         attend_kernel,
         out_shape=(
-            jax.ShapeDtypeStruct((CHUNKS, HD, 256), BF),
+            pltpu.HBM((CHUNKS, HD, 256), BF),
             jax.ShapeDtypeStruct((HD, 256), BF),
         ),
         in_specs=[SMEM] + [VMEM] * 5,
-        out_specs=(VMEM, VMEM),
+        out_specs=(pl.BlockSpec(memory_space=pltpu.HBM), VMEM),
         scratch_shapes=[
             pltpu.VMEM((2, HD, 256), BF),
             pltpu.VMEM((HD, 256), BF),
+            pltpu.VMEM((CHUNKS, HD, 256), BF),
+            pltpu.SemaphoreType.DMA((4,)),
         ],
         compiler_params=pltpu.CompilerParams(vmem_limit_bytes=20 << 20),
         cost_estimate=cost(600_000_000, 5_000_000),
         name="first_attend",
     )(scalars, raw, normed, mine, own, other)
+
+
+def run_combine(partial, kept):
+    return pl.pallas_call(
+        combine_kernel,
+        out_shape=(
+            pltpu.HBM((CHUNKS, HD, 256), BF),
+            jax.ShapeDtypeStruct((HD, 256), BF),
+        ),
+        in_specs=[VMEM, VMEM],
+        out_specs=(pl.BlockSpec(memory_space=pltpu.HBM), VMEM),
+        scratch_shapes=[pltpu.SemaphoreType.DMA((CHUNKS,))],
+        compiler_params=pltpu.CompilerParams(vmem_limit_bytes=20 << 20),
+        cost_estimate=cost(1_000_000, 2_000_000),
+        name="combine",
+    )(partial, kept)
 
 
 def run_stage(weights):
@@ -289,9 +324,8 @@
     white_far = lax.ppermute(white, ("y", "c"), far)
 
     partial = lax.all_to_all(partial, ("x", "y"), 0, 0)
-    attended = jnp.sum(partial.astype(F32), axis=0)
-    x1_own = (x0_own.astype(F32) + attended).astype(BF)
-    x1 = plane_gather(x1_own)
+    spread, x1_own = run_combine(partial, x0_own)
+    x1 = lax.all_to_all(spread, ("x", "y"), 0, 0)
 
     valid = jnp.arange(128)[None, :] < my_lengths[:, None]
     share = valid.astype(F32) / my_lengths.astype(F32)[:, None]
@@ -319,10 +353,12 @@
 
     packed = lax.all_to_all(packed, "z", 0, 0).reshape(64, 2 * HD)
     part = jnp.einsum("tk,nk->nt", packed, mixed, precision=lax.Precision.HIGHEST)
-    part = jnp.pad(part, ((0, 0), (0, 64))).reshape(NY, 1, 16, 128)
-    part = jnp.broadcast_to(part, (NY, 8, 16, 128)).reshape(32, 16, 128)
+    part = part.reshape(NY, 1, 2, 8, 64)
+    part = jnp.concatenate([part[:, :, 0], part[:, :, 1]], axis=3)
+    part = jnp.broadcast_to(part, (NY, 8, 8, 128)).reshape(32, 8, 128)
     part = lax.all_to_all(part, ("y", "c", "x"), 0, 0)
-    return jnp.sum(part, axis=0)[:, :64].T
+    total = jnp.sum(part, axis=0)
+    return jnp.concatenate([total[:, :64], total[:, 64:]], axis=0).T
 
 
 def solution(mesh):

time: 171 us -> 169 us (0.988)
  local copies, waits for them, and re-layouts: 9.36 us -> 6.85 us
  Pallas kernels: 10.7 us -> 12.7 us
    pallas_call x1 -> x2, Pallas kernels: 2.88 us -> 4.86 us  [the longest x1 3.61 us: run_attend(): pl.pallas_call(attend_kernel, out_shape=(pltpu.HBM((CHUNKS, HD, 256), BF)...]
    unnamed x15 -> x13, local copies, waits for them, and re-layouts: 5.72 us -> 4.77 us
  transfers between devices with their start and end apart: 10 -> 10, of which waited for: 5 -> 5; matrix products, arithmetic and copies ran while one was open for 3% -> 2% of each run, Pallas kernels for 5% -> 7%
where the time goes in v9:
time: 169 us; the launch traced here: 166 us
  blocking collectives  54.4 us (32%)
  starting transfers between devices  42.1 us (25%)
  waiting for transfers between devices  33.1 us (20%)
  between operations  14.4 us (9%)
  Pallas kernels  12.7 us (8%)
  local copies, waits for them, and re-layouts  6.85 us (4%)
    all_gather x1, blocking collectives, body(): own = lax.all_gather(first_shard, 'z', axis=0)  40.5 us
    all_to_all x1, waiting for transfers between devices, body(): packed = lax.all_to_all(packed, 'z', 0, 0).reshape(64, 2 * HD)  12.8 us
    all_to_all x1, blocking collectives, body(): part = lax.all_to_all(part, ('y', 'c', 'x'), 0, 0)  11.6 us
    all_to_all x1, waiting for transfers between devices, body(): partial = lax.all_to_all(partial, ('x', 'y'), 0, 0)  9.81 us
    all_to_all x1, waiting for transfers between devices, body(): x1 = lax.all_to_all(spread, ('x', 'y'), 0, 0)  8.47 us
    all_to_all x1, starting transfers between devices, body(): lax.all_to_all(projected, ('x', 'y'), 0, 0).reshape(4, NY, NY, HD, 128)  8.31 us
    all_to_all x1, starting transfers between devices, body(): packed = lax.all_to_all(packed, 'z', 0, 0).reshape(64, 2 * HD)  7.96 us
    all_to_all x1, starting transfers between devices, body(): partial = lax.all_to_all(partial, ('x', 'y'), 0, 0)  6.93 us
  transfers between devices with their start and end apart: 10, of which 5 were waited for; matrix products, arithmetic and copies ran while one was open for 2% of the time, Pallas kernels for 7%

profile of v9, /device:TPU:6, one launch (start us, length us, event | category | flops | bytes accessed | tf_op | source)
XLA Modules:
  0.0 165.8 jit_solution(1903454498169642057)
XLA Ops:
  7.2 1.7 %regroup.1 = bf16[8,4,32,120]{3,2,1,0:T(8,128)(2,1)} custom-call(s32[1,1]{1,0:T(1,128)} %bitcast.68.lengths, bf16[30,1440]{1,0:T(8,128)(2,1)} %bitcast.87, bf16[30,480]{1,0:T(8,128)(2,1)} %bitcast.89), custom_call_target="tpu_custom_call" | custom-call | bytes 400000 | tf_op jit(solution)/shard_map/regroup/pallas_call | solution.py:184
  8.9 4.5 %all-to-all-start = ((bf16[8,4,32,120]{3,2,1,0:T(8,128)(2,1)}), bf16[8,4,32,120]{3,2,1,0:T(8,128)(2,1)S(1)}, u32[]{:S(2)}, u32[]{:S(2)}) async-start(bf16[8,4,32,120]{3,2,1,0:T(8,128)(2,1)} %regroup.1), calls=%async_computation | async-start | bytes 524288 | tf_op jit(solution)/shard_map/all_to_all | solution.py:295
  13.4 2.2 %all-gather.2 = f32[2,1,1920]{2,1,0:T(1,128)S(1)} all-gather(f32[1,1,1920]{2,1,0:T(1,128)} %bitcast.90), channel_id=1, replica_groups=mesh['z'=16,'y'=4,'c'=2,'x'=4] {'c'}, dimensions={0}, use_global_device_ids=true | all-gather | bytes 23040 | tf_op jit(solution)/shard_map/all_gather | solution.py:296
  15.6 1.0 copy-done.2
  16.6 0.9 copy-done.3
  17.5 0.3 layer_input.1
  17.8 1.3 copy-done
  19.1 1.8 %all-to-all-done = bf16[8,4,32,120]{3,2,1,0:T(8,128)(2,1)S(1)} async-done(((bf16[8,4,32,120]{3,2,1,0:T(8,128)(2,1)}), bf16[8,4,32,120]{3,2,1,0:T(8,128)(2,1)S(1)}, u32[]{:S(2)}, u32[]{:S(2)}) %all-to-all-start) | async-done | bytes 245792 | tf_op jit(solution)/shard_map/all_to_all | solution.py:295
  21.5 8.3 %all-to-all-start.1 = ((bf16[16,4,120,128]{3,2,1,0:T(8,128)(2,1)}), bf16[16,4,120,128]{3,2,1,0:T(8,128)(2,1)S(1)}, u32[]{:S(2)}, u32[]{:S(2)}) async-start(bf16[16,4,120,128]{3,2,1,0:T(8,128)(2,1)} %copy-done), calls=%async_computation.1 | async-start | bytes 3932160 | tf_op jit(solution)/shard_map/all_to_all | solution.py:313
  30.0 0.8 copy.35
  30.9 40.5 %all-gather = bf16[32,120,120]{2,1,0:T(8,128)(2,1)S(1)} all-gather(bf16[2,120,120]{2,1,0:T(8,128)(2,1)S(1)} %copy.33), channel_id=2, replica_groups=mesh['z'=16,'y'=4,'c'=2,'x'=4] {'z'}, dimensions={0}, use_global_device_ids=true | all-gather | bytes 979200 | tf_op jit(solution)/shard_map/all_gather | solution.py:310
  71.5 1.9 %collective-permute-start = (bf16[16,2,120,120]{3,2,1,0:T(8,128)(2,1)S(1)}, bf16[16,2,120,120]{3,2,1,0:T(8,128)(2,1)}, u32[]{:S(2)}, u32[]{:S(2)}) collective-permute-start(bf16[16,2,120,120]{3,2,1,0:T(8,128)(2,1)S(1)} %bitcast.71), channel_id=1, source_target_pairs={{0,4},{4,0},{1,5},{5,1},{2,6},{6,2},{3,7},{7,3},{8,12},{12,8},{9,1... | collective-permute-start | bytes 2764808 | tf_op jit(solution)/shard_map/ppermute | solution.py:18
  73.6 2.2 %first_norm.1 = (bf16[16,120,256]{2,1,0:T(8,128)(2,1)S(1)}, bf16[2,120,256]{2,1,0:T(8,128)(2,1)S(1)}) custom-call(s32[5]{0:T(128)S(1)} %pad_add_fusion.scalars, bf16[4,4,4,120,128]{4,3,2,1,0:T(8,128)(2,1)S(1)} %bitcast.69, bf16[16,2,120,120]{3,2,1,0:T(8,128)(2,1)S(1)} %bitcast.72, f32[16,120]{1,0:T(8,128)S(1)} %squeeze.42.gain), custom_call_target="tpu_custom_call" | custom-call | flops 400000000 | bytes 4000000 | tf_op jit(solution)/shard_map/first_norm/pallas_call | solution.py:207
  75.8 0.2 collective-permute-done.other
  76.0 3.6 %first_attend.1 = (bf16[16,120,256]{2,1,0:T(8,128)(2,1)}, bf16[120,256]{1,0:T(8,128)(2,1)S(1)}) custom-call(s32[5]{0:T(128)S(1)} %pad_add_fusion.scalars, bf16[4,4,4,120,128]{4,3,2,1,0:T(8,128)(2,1)S(1)} %bitcast.70, bf16[16,120,256]{2,1,0:T(8,128)(2,1)S(1)} %get-tuple-element.24.normed, bf16[2,120,256]{2,1,0:T(8,128)(2,1)S(1)} %get-tuple-element.25.mine, ...), custom_call_target="tpu_custom_call" | custom-call | flops 600000000 | bytes 5000000 | tf_op jit(solution)/shard_map/first_attend/pallas_call | solution.py:222
  79.7 6.9 %all-to-all-start.2 = ((bf16[16,120,256]{2,1,0:T(8,128)(2,1)}), bf16[16,120,256]{2,1,0:T(8,128)(2,1)S(1)}, u32[]{:S(2)}, u32[]{:S(2)}) async-start(bf16[16,120,256]{2,1,0:T(8,128)(2,1)} %get-tuple-element.29), calls=%async_computation.2 | async-start | bytes 1966080 | tf_op jit(solution)/shard_map/all_to_all | solution.py:326
  87.1 4.6 %collective-permute-start.1 = (f32[16,16,120]{2,1,0:T(8,128)S(1)}, f32[16,16,120]{2,1,0:T(8,128)S(1)}, u32[]{:S(2)}, u32[]{:S(2)}) collective-permute-start(f32[16,16,120]{2,1,0:T(8,128)S(1)} %bitcast.81), channel_id=1, source_target_pairs={{8,0},{20,4},{16,8},{28,12},{24,16},{4,20},{0,24},{12,28},{9,1},{2... | collective-permute-start | bytes 368648 | tf_op jit(solution)/shard_map/ppermute | solution.py:323
  91.6 0.7 collective-permute-start.2
  92.4 9.8 %all-to-all-done.2.partial = bf16[16,120,256]{2,1,0:T(8,128)(2,1)S(1)} async-done(((bf16[16,120,256]{2,1,0:T(8,128)(2,1)}), bf16[16,120,256]{2,1,0:T(8,128)(2,1)S(1)}, u32[]{:S(2)}, u32[]{:S(2)}) %all-to-all-start.2) | async-done | bytes 983072 | tf_op jit(solution)/shard_map/all_to_all | solution.py:326
  102.2 1.2 combine.1
  103.5 5.3 %all-to-all-start.3 = ((bf16[16,120,256]{2,1,0:T(8,128)(2,1)}), bf16[16,120,256]{2,1,0:T(8,128)(2,1)S(1)}, u32[]{:S(2)}, u32[]{:S(2)}) async-start(bf16[16,120,256]{2,1,0:T(8,128)(2,1)} %get-tuple-element.31), calls=%async_computation.3 | async-start | bytes 1966080 | tf_op jit(solution)/shard_map/all_to_all | solution.py:328
  108.9 0.2 multiply_reduce_fusion
  109.2 1.5 copy-done.1
  110.9 0.5 convolution_bitcast_fusion.1
  111.4 1.9 %collective-permute-start.3 = (f32[2,16,240]{2,1,0:T(8,128)S(1)}, f32[2,16,240]{2,1,0:T(8,128)S(1)}, u32[]{:S(2)}, u32[]{:S(2)}) collective-permute-start(f32[2,16,240]{2,1,0:T(8,128)S(1)} %pad_maximum_fusion.3), channel_id=1, source_target_pairs={{0,4},{4,0},{1,5},{5,1},{2,6},{6,2},{3,7},{7,3},{8,12},{12,8},{9,1... | collective-permute-start | bytes 92168 | tf_op jit(solution)/shard_map/ppermute | solution.py:18
  113.4 8.5 %all-to-all-done.3.x1 = bf16[16,120,256]{2,1,0:T(8,128)(2,1)S(1)} async-done(((bf16[16,120,256]{2,1,0:T(8,128)(2,1)}), bf16[16,120,256]{2,1,0:T(8,128)(2,1)S(1)}, u32[]{:S(2)}, u32[]{:S(2)}) %all-to-all-start.3) | async-done | bytes 983072 | tf_op jit(solution)/shard_map/all_to_all | solution.py:328
  121.8 3.5 %second_layer.1 = f32[16,4,240]{2,1,0:T(4,128)} custom-call(s32[5]{0:T(128)S(1)} %pad_add_fusion.scalars, bf16[16,120,256]{2,1,0:T(8,128)(2,1)S(1)} %all-to-all-done.3.x1, bf16[16,3,120,120]{3,2,1,0:T(8,128)(2,1)S(1)} %stage.1.weights, f32[16,120]{1,0:T(8,128)S(1)} %squeeze.45.gain, f32[2,120]{1,0:T(2,128)S(1)} %subtract_bitcast_fusion.rest), custom_call_target="tpu_custom_call" | custom-call | flops 1000000000 | bytes 6000000 | tf_op jit(solution)/shard_map/second_layer/pallas_call | solution.py:272
  125.3 8.0 %all-to-all-start.4 = ((f32[16,4,240]{2,1,0:T(4,128)}), f32[16,4,240]{2,1,0:T(4,128)S(1)}, u32[]{:S(2)}, u32[]{:S(2)}) async-start(f32[16,4,240]{2,1,0:T(4,128)} %second_layer.1), calls=%async_computation.4 | async-start | bytes 131072 | tf_op jit(solution)/shard_map/all_to_all | solution.py:354
  133.4 12.8 %all-to-all-done.4 = f32[16,4,240]{2,1,0:T(4,128)S(1)} async-done(((f32[16,4,240]{2,1,0:T(4,128)}), f32[16,4,240]{2,1,0:T(4,128)S(1)}, u32[]{:S(2)}, u32[]{:S(2)}) %all-to-all-start.4) | async-done | bytes 61472 | tf_op jit(solution)/shard_map/all_to_all | solution.py:354
  146.2 0.2 convolution_bitcast_fusion
  146.6 11.6 %all_to_all.30 = f32[32,8,128]{2,1,0:T(8,128)S(1)} all-to-all(f32[32,8,128]{2,1,0:T(8,128)S(1)} %bitcast.80), channel_id=1, replica_groups=mesh['z'=16,'y'=4,'c'=2,'x'=4] {'y','c','x'}, dimensions={0} | all-to-all | bytes 262144 | tf_op jit(solution)/shard_map/all_to_all | solution.py:359
  158.3 0.6 maximum_bitcast_fusion.1
  (57 shorter events, 2.2 us)
Async XLA Ops:
  8.9 12.0 %all-to-all-start = ((bf16[8,4,32,120]{3,2,1,0:T(8,128)(2,1)}), bf16[8,4,32,120]{3,2,1,0:T(8,128)(2,1)S(1)}, u32[]{:S(2)}, u32[]{:S(2)}) async-start(bf16[8,4,32,120]{3,2,1,0:T(8,128)(2,1)} %regroup.1), calls=%async_computation | async-start | bytes 524288 | tf_op jit(solution)/shard_map/all_to_all | solution.py:295
  15.6 1.0 copy-start.2
  16.6 0.9 copy-start.3
  17.8 1.3 copy-start
  21.5 52.1 %all-to-all-start.1 = ((bf16[16,4,120,128]{3,2,1,0:T(8,128)(2,1)}), bf16[16,4,120,128]{3,2,1,0:T(8,128)(2,1)S(1)}, u32[]{:S(2)}, u32[]{:S(2)}) async-start(bf16[16,4,120,128]{3,2,1,0:T(8,128)(2,1)} %copy-done), calls=%async_computation.1 | async-start | bytes 3932160 | tf_op jit(solution)/shard_map/all_to_all | solution.py:313
  29.8 79.4 %all-gather.5.cloned.1.call-start = ((), (), s32[]{:S(2)}) async-start(), calls=%async_computation.6 | async-start | bytes 2088960 | tf_op jit(solution)/shard_map/all_gather | solution.py:309
  71.5 4.6 %collective-permute-start = (bf16[16,2,120,120]{3,2,1,0:T(8,128)(2,1)S(1)}, bf16[16,2,120,120]{3,2,1,0:T(8,128)(2,1)}, u32[]{:S(2)}, u32[]{:S(2)}) collective-permute-start(bf16[16,2,120,120]{3,2,1,0:T(8,128)(2,1)S(1)} %bitcast.71), channel_id=1, source_target_pairs={{0,4},{4,0},{1,5},{5,1},{2,6},{6,2},{3,7},{7,3},{8,12},{12,8},{9,1... | collective-permute-start | bytes 2764808 | tf_op jit(solution)/shard_map/ppermute | solution.py:18
  79.7 7.0 %copy-start.4 = (f32[1920,16]{0,1:T(8,128)S(1)}, f32[1920,16]{0,1:T(8,128)}, u32[]{:S(2)}) copy-start(f32[1920,16]{0,1:T(8,128)} %param.15) | copy-start | bytes 368644
  79.7 7.2 %copy-start.5 = (f32[1920]{0:T(1024)S(1)}, f32[1920]{0:T(1024)}, u32[]{:S(2)}) copy-start(f32[1920]{0:T(1024)} %param.14) | copy-start | bytes 23044
  79.7 22.5 %all-to-all-start.2 = ((bf16[16,120,256]{2,1,0:T(8,128)(2,1)}), bf16[16,120,256]{2,1,0:T(8,128)(2,1)S(1)}, u32[]{:S(2)}, u32[]{:S(2)}) async-start(bf16[16,120,256]{2,1,0:T(8,128)(2,1)} %get-tuple-element.29), calls=%async_computation.2 | async-start | bytes 1966080 | tf_op jit(solution)/shard_map/all_to_all | solution.py:326
  87.1 21.7 %collective-permute-start.1 = (f32[16,16,120]{2,1,0:T(8,128)S(1)}, f32[16,16,120]{2,1,0:T(8,128)S(1)}, u32[]{:S(2)}, u32[]{:S(2)}) collective-permute-start(f32[16,16,120]{2,1,0:T(8,128)S(1)} %bitcast.81), channel_id=1, source_target_pairs={{8,0},{20,4},{16,8},{28,12},{24,16},{4,20},{0,24},{12,28},{9,1},{2... | collective-permute-start | bytes 368648 | tf_op jit(solution)/shard_map/ppermute | solution.py:323
  91.6 17.1 %collective-permute-start.2 = (f32[16,16,120]{2,1,0:T(8,128)S(1)}, f32[16,16,120]{2,1,0:T(8,128)S(1)}, u32[]{:S(2)}, u32[]{:S(2)}) collective-permute-start(f32[16,16,120]{2,1,0:T(8,128)S(1)} %bitcast.82), channel_id=1, source_target_pairs={{28,4},{4,12},{12,20},{20,28},{29,5},{5,13},{13,21},{21,29},{30,6}... | collective-permute-start | bytes 368648 | tf_op jit(solution)/shard_map/ppermute | solution.py:324
  103.5 18.4 %all-to-all-start.3 = ((bf16[16,120,256]{2,1,0:T(8,128)(2,1)}), bf16[16,120,256]{2,1,0:T(8,128)(2,1)S(1)}, u32[]{:S(2)}, u32[]{:S(2)}) async-start(bf16[16,120,256]{2,1,0:T(8,128)(2,1)} %get-tuple-element.31), calls=%async_computation.3 | async-start | bytes 1966080 | tf_op jit(solution)/shard_map/all_to_all | solution.py:328
  109.2 1.6 copy-start.1
  111.4 21.9 %collective-permute-start.3 = (f32[2,16,240]{2,1,0:T(8,128)S(1)}, f32[2,16,240]{2,1,0:T(8,128)S(1)}, u32[]{:S(2)}, u32[]{:S(2)}) collective-permute-start(f32[2,16,240]{2,1,0:T(8,128)S(1)} %pad_maximum_fusion.3), channel_id=1, source_target_pairs={{0,4},{4,0},{1,5},{5,1},{2,6},{6,2},{3,7},{7,3},{8,12},{12,8},{9,1... | collective-permute-start | bytes 92168 | tf_op jit(solution)/shard_map/ppermute | solution.py:18
  125.3 20.9 %all-to-all-start.4 = ((f32[16,4,240]{2,1,0:T(4,128)}), f32[16,4,240]{2,1,0:T(4,128)S(1)}, u32[]{:S(2)}, u32[]{:S(2)}) async-start(f32[16,4,240]{2,1,0:T(4,128)} %second_layer.1), calls=%async_computation.4 | async-start | bytes 131072 | tf_op jit(solution)/shard_map/all_to_all | solution.py:354
Sparse Core Ops, SparseCore 0:
  32.7 74.8 all-gather.4

commit v10 on v9

--- a/solution.py
+++ b/solution.py
@@ -55,26 +55,46 @@
     return slice(u * 128, u * 128 + 128)
 
 
-def regroup_kernel(lengths, qkv, out, mats):
+def regroup_kernel(lengths, qkv, out, mats_hbm, mats, sent):
     tail = jnp.broadcast_to(lengths[...].astype(F32), (2, HD)).astype(BF)
+    copies = []
     for y in range(NY):
         for m in range(4):
             start = (m * NY + y) * HD if m < 3 else y * HD
             source = qkv if m < 3 else out
-            block = source[:, start : start + HD]
-            for c in range(2):
-                mats[2 * y + c, m, 0:30, :] = block
-                mats[2 * y + c, m, 30:32, :] = tail
-
-
-def input_kernel(weights, frames, spread):
+            mats[y, m, 0:30, :] = source[:, start : start + HD]
+            mats[y, m, 30:32, :] = tail
+        for c in range(2):
+            target = 2 * y + c
+            copies.append(
+                pltpu.make_async_copy(mats.at[y], mats_hbm.at[target], sent.at[target])
+            )
+            copies[-1].start()
+    for copy in copies:
+        copy.wait()
+
+
+def input_kernel(weights_hbm, frames_hbm, spread, weights, frames, blocks, arrived, sent):
+    fetches = [
+        pltpu.make_async_copy(weights_hbm, weights, arrived.at[0]),
+        pltpu.make_async_copy(frames_hbm, frames, arrived.at[1]),
+    ]
+    for fetch in fetches:
+        fetch.start()
+    for fetch in fetches:
+        fetch.wait()
     projected = lax.dot_general(
         weights[...], frames[...], (((1,), (1,)), ((), ())), preferred_element_type=F32
     )
     for y in range(NY):
-        block = projected[y * HD : y * HD + HD, :].astype(BF)
-        for target in range(16):
-            spread[target, y] = block
+        blocks[y] = projected[y * HD : y * HD + HD, :].astype(BF)
+    copies = [
+        pltpu.make_async_copy(blocks, spread.at[target], sent.at[target]) for target in range(16)
+    ]
+    for copy in copies:
+        copy.start()
+    for copy in copies:
+        copy.wait()
 
 
 def norm_kernel(scalars, raw, own, gain, normed, mine):
@@ -183,24 +203,39 @@
 def run_regroup(lengths, qkv, out):
     return pl.pallas_call(
         regroup_kernel,
-        out_shape=jax.ShapeDtypeStruct((2 * NY, 4, 32, HD), BF),
+        out_shape=pltpu.HBM((2 * NY, 4, 32, HD), BF),
         in_specs=[VMEM, VMEM, VMEM],
-        out_specs=VMEM,
+        out_specs=pl.BlockSpec(memory_space=pltpu.HBM),
+        scratch_shapes=[
+            pltpu.VMEM((NY, 4, 32, HD), BF),
+            pltpu.SemaphoreType.DMA((2 * NY,)),
+        ],
         cost_estimate=cost(0, 400_000),
         name="regroup",
     )(lengths, qkv, out)
 
 
 def run_input(weights, frames):
+    hbm = pl.BlockSpec(memory_space=pltpu.HBM)
     return pl.pallas_call(
         input_kernel,
-        out_shape=jax.ShapeDtypeStruct((16, NY, HD, 128), BF),
-        in_specs=[VMEM, VMEM],
-        out_specs=VMEM,
+        out_shape=pltpu.HBM((16, NY, HD, 128), BF),
+        in_specs=[hbm, hbm],
+        out_specs=hbm,
+        scratch_shapes=[
+            pltpu.VMEM(weights.shape, BF),
+            pltpu.VMEM(frames.shape, BF),
+            pltpu.VMEM((NY, HD, 128), BF),
+            pltpu.SemaphoreType.DMA((2,)),
+            pltpu.SemaphoreType.DMA((16,)),
+        ],
         compiler_params=pltpu.CompilerParams(vmem_limit_bytes=20 << 20),
         cost_estimate=cost(100_000_000, 3_000_000),
         name="layer_input",
-    )(weights, frames)
+    )(
+        pltpu.with_memory_space_constraint(weights, pltpu.HBM),
+        pltpu.with_memory_space_constraint(frames, pltpu.HBM),
+    )
 
 
 def run_norm(scalars, raw, own, gain):

time: 169 us -> 168 us (level)
  local copies, waits for them, and re-layouts: 6.85 us -> 3.64 us
  Pallas kernels: 12.7 us -> 15.2 us
    unnamed x13 -> x7, local copies, waits for them, and re-layouts: 4.77 us -> 1.58 us
    pallas_call x2, Pallas kernels: 2.01 us -> 4.52 us  [the longest x1 2.77 us: run_input(): pl.pallas_call(input_kernel, out_shape=pltpu.HBM((16, NY, HD, 128), BF),...]
  transfers between devices with their start and end apart: 10 -> 10, of which waited for: 5 -> 5; matrix products, arithmetic and copies ran while one was open for 2% -> 2% of each run, Pallas kernels for 7% -> 8%
where the time goes in v10:
time: 168 us; the launch traced here: 165 us
  blocking collectives  54 us (32%)
  starting transfers between devices  41.8 us (25%)
  waiting for transfers between devices  33.9 us (20%)
  Pallas kernels  15.2 us (9%)
  between operations  14.4 us (9%)
  local copies, waits for them, and re-layouts  3.64 us (2%)
    all_gather x1, blocking collectives, body(): own = lax.all_gather(first_shard, 'z', axis=0)  40.1 us
    all_to_all x1, waiting for transfers between devices, body(): packed = lax.all_to_all(packed, 'z', 0, 0).reshape(64, 2 * HD)  12.8 us
    all_to_all x1, blocking collectives, body(): part = lax.all_to_all(part, ('y', 'c', 'x'), 0, 0)  11.7 us
    all_to_all x1, waiting for transfers between devices, body(): partial = lax.all_to_all(partial, ('x', 'y'), 0, 0)  9.82 us
    all_to_all x1, waiting for transfers between devices, body(): x1 = lax.all_to_all(spread, ('x', 'y'), 0, 0)  8.51 us
    all_to_all x1, starting transfers between devices, body(): lax.all_to_all(projected, ('x', 'y'), 0, 0).reshape(4, NY, NY, HD, 128)  8.31 us
    all_to_all x1, starting transfers between devices, body(): packed = lax.all_to_all(packed, 'z', 0, 0).reshape(64, 2 * HD)  7.75 us
    all_to_all x1, starting transfers between devices, body(): partial = lax.all_to_all(partial, ('x', 'y'), 0, 0)  6.89 us
  transfers between devices with their start and end apart: 10, of which 5 were waited for; matrix products, arithmetic and copies ran while one was open for 2% of the time, Pallas kernels for 8%

profile of v10, /device:TPU:6, one launch (start us, length us, event | category | flops | bytes accessed | tf_op | source)
XLA Modules:
  0.0 165.2 jit_solution(1003556845478381826)
XLA Ops:
  7.2 1.8 %regroup.1 = bf16[8,4,32,120]{3,2,1,0:T(8,128)(2,1)} custom-call(s32[1,1]{1,0:T(1,128)} %bitcast.68.lengths, bf16[30,1440]{1,0:T(8,128)(2,1)} %bitcast.87, bf16[30,480]{1,0:T(8,128)(2,1)} %bitcast.89), custom_call_target="tpu_custom_call" | custom-call | bytes 400000 | tf_op jit(solution)/shard_map/regroup/pallas_call | solution.py:204
  8.9 4.5 %all-to-all-start = ((bf16[8,4,32,120]{3,2,1,0:T(8,128)(2,1)}), bf16[8,4,32,120]{3,2,1,0:T(8,128)(2,1)S(1)}, u32[]{:S(2)}, u32[]{:S(2)}) async-start(bf16[8,4,32,120]{3,2,1,0:T(8,128)(2,1)} %regroup.1), calls=%async_computation | async-start | bytes 524288 | tf_op jit(solution)/shard_map/all_to_all | solution.py:330
  13.4 2.2 %all-gather.2 = f32[2,1,1920]{2,1,0:T(1,128)S(1)} all-gather(f32[1,1,1920]{2,1,0:T(1,128)} %bitcast.90), channel_id=1, replica_groups=mesh['z'=16,'y'=4,'c'=2,'x'=4] {'c'}, dimensions={0}, use_global_device_ids=true | all-gather | bytes 23040 | tf_op jit(solution)/shard_map/all_gather | solution.py:331
  15.6 2.8 %layer_input.1 = bf16[16,4,120,128]{3,2,1,0:T(8,128)(2,1)} custom-call(bf16[480,512]{1,0:T(8,128)(2,1)} %bitcast.82, bf16[128,512]{1,0:T(8,128)(2,1)} %bitcast.85), custom_call_target="tpu_custom_call" | custom-call | flops 100000000 | bytes 3000000 | tf_op jit(solution)/shard_map/layer_input/pallas_call | solution.py:220
  18.4 2.6 %all-to-all-done = bf16[8,4,32,120]{3,2,1,0:T(8,128)(2,1)S(1)} async-done(((bf16[8,4,32,120]{3,2,1,0:T(8,128)(2,1)}), bf16[8,4,32,120]{3,2,1,0:T(8,128)(2,1)S(1)}, u32[]{:S(2)}, u32[]{:S(2)}) %all-to-all-start) | async-done | bytes 245792 | tf_op jit(solution)/shard_map/all_to_all | solution.py:330
  21.0 0.1 slice_reduce_fusion.2
  21.5 8.3 %all-to-all-start.1 = ((bf16[16,4,120,128]{3,2,1,0:T(8,128)(2,1)}), bf16[16,4,120,128]{3,2,1,0:T(8,128)(2,1)S(1)}, u32[]{:S(2)}, u32[]{:S(2)}) async-start(bf16[16,4,120,128]{3,2,1,0:T(8,128)(2,1)} %layer_input.1), calls=%async_computation.1 | async-start | bytes 3932160 | tf_op jit(solution)/shard_map/all_to_all | solution.py:348
  30.0 0.8 copy.35
  30.8 0.1 copy.33
  30.9 40.1 %all-gather = bf16[32,120,120]{2,1,0:T(8,128)(2,1)S(1)} all-gather(bf16[2,120,120]{2,1,0:T(8,128)(2,1)S(1)} %copy.33), channel_id=2, replica_groups=mesh['z'=16,'y'=4,'c'=2,'x'=4] {'z'}, dimensions={0}, use_global_device_ids=true | all-gather | bytes 979200 | tf_op jit(solution)/shard_map/all_gather | solution.py:345
  71.0 1.9 %collective-permute-start = (bf16[16,2,120,120]{3,2,1,0:T(8,128)(2,1)S(1)}, bf16[16,2,120,120]{3,2,1,0:T(8,128)(2,1)}, u32[]{:S(2)}, u32[]{:S(2)}) collective-permute-start(bf16[16,2,120,120]{3,2,1,0:T(8,128)(2,1)S(1)} %bitcast.71), channel_id=1, source_target_pairs={{0,4},{4,0},{1,5},{5,1},{2,6},{6,2},{3,7},{7,3},{8,12},{12,8},{9,1... | collective-permute-start | bytes 2764808 | tf_op jit(solution)/shard_map/ppermute | solution.py:18
  73.2 2.2 %first_norm.1 = (bf16[16,120,256]{2,1,0:T(8,128)(2,1)S(1)}, bf16[2,120,256]{2,1,0:T(8,128)(2,1)S(1)}) custom-call(s32[5]{0:T(128)S(1)} %pad_add_fusion.scalars, bf16[4,4,4,120,128]{4,3,2,1,0:T(8,128)(2,1)S(1)} %bitcast.69, bf16[16,2,120,120]{3,2,1,0:T(8,128)(2,1)S(1)} %bitcast.72, f32[16,120]{1,0:T(8,128)S(1)} %squeeze.42.gain), custom_call_target="tpu_custom_call" | custom-call | flops 400000000 | bytes 4000000 | tf_op jit(solution)/shard_map/first_norm/pallas_call | solution.py:242
  75.4 0.2 collective-permute-done.other
  75.6 3.6 %first_attend.1 = (bf16[16,120,256]{2,1,0:T(8,128)(2,1)}, bf16[120,256]{1,0:T(8,128)(2,1)S(1)}) custom-call(s32[5]{0:T(128)S(1)} %pad_add_fusion.scalars, bf16[4,4,4,120,128]{4,3,2,1,0:T(8,128)(2,1)S(1)} %bitcast.70, bf16[16,120,256]{2,1,0:T(8,128)(2,1)S(1)} %get-tuple-element.24.normed, bf16[2,120,256]{2,1,0:T(8,128)(2,1)S(1)} %get-tuple-element.25.mine, ...), custom_call_target="tpu_custom_call" | custom-call | flops 600000000 | bytes 5000000 | tf_op jit(solution)/shard_map/first_attend/pallas_call | solution.py:257
  79.2 6.9 %all-to-all-start.2 = ((bf16[16,120,256]{2,1,0:T(8,128)(2,1)}), bf16[16,120,256]{2,1,0:T(8,128)(2,1)S(1)}, u32[]{:S(2)}, u32[]{:S(2)}) async-start(bf16[16,120,256]{2,1,0:T(8,128)(2,1)} %get-tuple-element.29), calls=%async_computation.2 | async-start | bytes 1966080 | tf_op jit(solution)/shard_map/all_to_all | solution.py:361
  86.1 0.2 reshape.78
  86.6 4.6 %collective-permute-start.1 = (f32[16,16,120]{2,1,0:T(8,128)S(1)}, f32[16,16,120]{2,1,0:T(8,128)S(1)}, u32[]{:S(2)}, u32[]{:S(2)}) collective-permute-start(f32[16,16,120]{2,1,0:T(8,128)S(1)} %bitcast.79), channel_id=1, source_target_pairs={{8,0},{20,4},{16,8},{28,12},{24,16},{4,20},{0,24},{12,28},{9,1},{2... | collective-permute-start | bytes 368648 | tf_op jit(solution)/shard_map/ppermute | solution.py:358
  91.2 0.7 collective-permute-start.2
  91.9 9.8 %all-to-all-done.2.partial = bf16[16,120,256]{2,1,0:T(8,128)(2,1)S(1)} async-done(((bf16[16,120,256]{2,1,0:T(8,128)(2,1)}), bf16[16,120,256]{2,1,0:T(8,128)(2,1)S(1)}, u32[]{:S(2)}, u32[]{:S(2)}) %all-to-all-start.2) | async-done | bytes 983072 | tf_op jit(solution)/shard_map/all_to_all | solution.py:361
  101.7 1.3 combine.1
  103.0 5.3 %all-to-all-start.3 = ((bf16[16,120,256]{2,1,0:T(8,128)(2,1)}), bf16[16,120,256]{2,1,0:T(8,128)(2,1)S(1)}, u32[]{:S(2)}, u32[]{:S(2)}) async-start(bf16[16,120,256]{2,1,0:T(8,128)(2,1)} %get-tuple-element.31), calls=%async_computation.3 | async-start | bytes 1966080 | tf_op jit(solution)/shard_map/all_to_all | solution.py:363
  108.5 0.2 multiply_reduce_fusion
  108.8 1.5 copy-done
  110.4 0.5 convolution_bitcast_fusion.1
  111.0 1.9 %collective-permute-start.3 = (f32[2,16,240]{2,1,0:T(8,128)S(1)}, f32[2,16,240]{2,1,0:T(8,128)S(1)}, u32[]{:S(2)}, u32[]{:S(2)}) collective-permute-start(f32[2,16,240]{2,1,0:T(8,128)S(1)} %pad_maximum_fusion.3), channel_id=1, source_target_pairs={{0,4},{4,0},{1,5},{5,1},{2,6},{6,2},{3,7},{7,3},{8,12},{12,8},{9,1... | collective-permute-start | bytes 92168 | tf_op jit(solution)/shard_map/ppermute | solution.py:18
  112.9 8.5 %all-to-all-done.3.x1 = bf16[16,120,256]{2,1,0:T(8,128)(2,1)S(1)} async-done(((bf16[16,120,256]{2,1,0:T(8,128)(2,1)}), bf16[16,120,256]{2,1,0:T(8,128)(2,1)S(1)}, u32[]{:S(2)}, u32[]{:S(2)}) %all-to-all-start.3) | async-done | bytes 983072 | tf_op jit(solution)/shard_map/all_to_all | solution.py:363
  121.4 3.5 %second_layer.1 = f32[16,4,240]{2,1,0:T(4,128)} custom-call(s32[5]{0:T(128)S(1)} %pad_add_fusion.scalars, bf16[16,120,256]{2,1,0:T(8,128)(2,1)S(1)} %all-to-all-done.3.x1, bf16[16,3,120,120]{3,2,1,0:T(8,128)(2,1)S(1)} %stage.1.weights, f32[16,120]{1,0:T(8,128)S(1)} %squeeze.45.gain, f32[2,120]{1,0:T(2,128)S(1)} %subtract_bitcast_fusion.rest), custom_call_target="tpu_custom_call" | custom-call | flops 1000000000 | bytes 6000000 | tf_op jit(solution)/shard_map/second_layer/pallas_call | solution.py:307
  124.9 7.7 %all-to-all-start.4 = ((f32[16,4,240]{2,1,0:T(4,128)}), f32[16,4,240]{2,1,0:T(4,128)S(1)}, u32[]{:S(2)}, u32[]{:S(2)}) async-start(f32[16,4,240]{2,1,0:T(4,128)} %second_layer.1), calls=%async_computation.4 | async-start | bytes 131072 | tf_op jit(solution)/shard_map/all_to_all | solution.py:389
  132.8 12.8 %all-to-all-done.4 = f32[16,4,240]{2,1,0:T(4,128)S(1)} async-done(((f32[16,4,240]{2,1,0:T(4,128)}), f32[16,4,240]{2,1,0:T(4,128)S(1)}, u32[]{:S(2)}, u32[]{:S(2)}) %all-to-all-start.4) | async-done | bytes 61472 | tf_op jit(solution)/shard_map/all_to_all | solution.py:389
  145.6 0.2 convolution_bitcast_fusion
  145.9 11.7 %all_to_all.30 = f32[32,8,128]{2,1,0:T(8,128)S(1)} all-to-all(f32[32,8,128]{2,1,0:T(8,128)S(1)} %bitcast.78), channel_id=1, replica_groups=mesh['z'=16,'y'=4,'c'=2,'x'=4] {'y','c','x'}, dimensions={0} | all-to-all | bytes 262144 | tf_op jit(solution)/shard_map/all_to_all | solution.py:394
  157.7 0.6 maximum_bitcast_fusion.1
  (51 shorter events, 1.8 us)
Async XLA Ops:
  8.9 12.0 %all-to-all-start = ((bf16[8,4,32,120]{3,2,1,0:T(8,128)(2,1)}), bf16[8,4,32,120]{3,2,1,0:T(8,128)(2,1)S(1)}, u32[]{:S(2)}, u32[]{:S(2)}) async-start(bf16[8,4,32,120]{3,2,1,0:T(8,128)(2,1)} %regroup.1), calls=%async_computation | async-start | bytes 524288 | tf_op jit(solution)/shard_map/all_to_all | solution.py:330
  21.5 51.6 %all-to-all-start.1 = ((bf16[16,4,120,128]{3,2,1,0:T(8,128)(2,1)}), bf16[16,4,120,128]{3,2,1,0:T(8,128)(2,1)S(1)}, u32[]{:S(2)}, u32[]{:S(2)}) async-start(bf16[16,4,120,128]{3,2,1,0:T(8,128)(2,1)} %layer_input.1), calls=%async_computation.1 | async-start | bytes 3932160 | tf_op jit(solution)/shard_map/all_to_all | solution.py:348
  29.8 78.9 %all-gather.5.cloned.1.call-start = ((), (), s32[]{:S(2)}) async-start(), calls=%async_computation.6 | async-start | bytes 2088960 | tf_op jit(solution)/shard_map/all_gather | solution.py:344
  71.0 4.6 %collective-permute-start = (bf16[16,2,120,120]{3,2,1,0:T(8,128)(2,1)S(1)}, bf16[16,2,120,120]{3,2,1,0:T(8,128)(2,1)}, u32[]{:S(2)}, u32[]{:S(2)}) collective-permute-start(bf16[16,2,120,120]{3,2,1,0:T(8,128)(2,1)S(1)} %bitcast.71), channel_id=1, source_target_pairs={{0,4},{4,0},{1,5},{5,1},{2,6},{6,2},{3,7},{7,3},{8,12},{12,8},{9,1... | collective-permute-start | bytes 2764808 | tf_op jit(solution)/shard_map/ppermute | solution.py:18
  79.2 6.9 %copy-start.1 = (f32[1920,16]{0,1:T(8,128)S(1)}, f32[1920,16]{0,1:T(8,128)}, u32[]{:S(2)}) copy-start(f32[1920,16]{0,1:T(8,128)} %param.15) | copy-start | bytes 368644
  79.2 7.1 %copy-start.2 = (f32[1920]{0:T(1024)S(1)}, f32[1920]{0:T(1024)}, u32[]{:S(2)}) copy-start(f32[1920]{0:T(1024)} %param.14) | copy-start | bytes 23044
  79.2 22.5 %all-to-all-start.2 = ((bf16[16,120,256]{2,1,0:T(8,128)(2,1)}), bf16[16,120,256]{2,1,0:T(8,128)(2,1)S(1)}, u32[]{:S(2)}, u32[]{:S(2)}) async-start(bf16[16,120,256]{2,1,0:T(8,128)(2,1)} %get-tuple-element.29), calls=%async_computation.2 | async-start | bytes 1966080 | tf_op jit(solution)/shard_map/all_to_all | solution.py:361
  86.6 21.7 %collective-permute-start.1 = (f32[16,16,120]{2,1,0:T(8,128)S(1)}, f32[16,16,120]{2,1,0:T(8,128)S(1)}, u32[]{:S(2)}, u32[]{:S(2)}) collective-permute-start(f32[16,16,120]{2,1,0:T(8,128)S(1)} %bitcast.79), channel_id=1, source_target_pairs={{8,0},{20,4},{16,8},{28,12},{24,16},{4,20},{0,24},{12,28},{9,1},{2... | collective-permute-start | bytes 368648 | tf_op jit(solution)/shard_map/ppermute | solution.py:358
  91.2 17.2 %collective-permute-start.2 = (f32[16,16,120]{2,1,0:T(8,128)S(1)}, f32[16,16,120]{2,1,0:T(8,128)S(1)}, u32[]{:S(2)}, u32[]{:S(2)}) collective-permute-start(f32[16,16,120]{2,1,0:T(8,128)S(1)} %bitcast.80), channel_id=1, source_target_pairs={{28,4},{4,12},{12,20},{20,28},{29,5},{5,13},{13,21},{21,29},{30,6}... | collective-permute-start | bytes 368648 | tf_op jit(solution)/shard_map/ppermute | solution.py:359
  103.0 18.4 %all-to-all-start.3 = ((bf16[16,120,256]{2,1,0:T(8,128)(2,1)}), bf16[16,120,256]{2,1,0:T(8,128)(2,1)S(1)}, u32[]{:S(2)}, u32[]{:S(2)}) async-start(bf16[16,120,256]{2,1,0:T(8,128)(2,1)} %get-tuple-element.31), calls=%async_computation.3 | async-start | bytes 1966080 | tf_op jit(solution)/shard_map/all_to_all | solution.py:363
  108.7 1.6 copy-start
  111.0 21.7 %collective-permute-start.3 = (f32[2,16,240]{2,1,0:T(8,128)S(1)}, f32[2,16,240]{2,1,0:T(8,128)S(1)}, u32[]{:S(2)}, u32[]{:S(2)}) collective-permute-start(f32[2,16,240]{2,1,0:T(8,128)S(1)} %pad_maximum_fusion.3), channel_id=1, source_target_pairs={{0,4},{4,0},{1,5},{5,1},{2,6},{6,2},{3,7},{7,3},{8,12},{12,8},{9,1... | collective-permute-start | bytes 92168 | tf_op jit(solution)/shard_map/ppermute | solution.py:18
  124.9 20.6 %all-to-all-start.4 = ((f32[16,4,240]{2,1,0:T(4,128)}), f32[16,4,240]{2,1,0:T(4,128)S(1)}, u32[]{:S(2)}, u32[]{:S(2)}) async-start(f32[16,4,240]{2,1,0:T(4,128)} %second_layer.1), calls=%async_computation.4 | async-start | bytes 131072 | tf_op jit(solution)/shard_map/all_to_all | solution.py:389
Sparse Core Ops, SparseCore 0:
  32.7 74.8 all-gather.4

commit v11 on v10

--- a/solution.py
+++ b/solution.py
@@ -173,7 +173,6 @@
 
 
 def second_kernel(scalars, x1, weights, gain, rest, packed, normed, qkv):
-    core = scalars[0]
     rows = []
     gain_rows = gain[...].T
     for u in range(2):
@@ -189,11 +188,8 @@
         pooled = jnp.sum(total, axis=0, keepdims=True) / length.astype(F32)
         rows.append(jnp.concatenate([pooled, rest[u : u + 1, :]], axis=1))
     mine = jnp.concatenate(rows, axis=0)
-    first = jnp.where(core == 0, mine, F32(0.0))
-    second = jnp.where(core == 1, mine, F32(0.0))
-    block = jnp.concatenate([first, second], axis=0)
-    for z in range(16):
-        packed[z] = block
+    for target in range(32):
+        packed[target] = mine
 
 
 def cost(flops, moved):
@@ -306,7 +302,7 @@
 def run_second(scalars, x1, weights, gain, rest):
     return pl.pallas_call(
         second_kernel,
-        out_shape=jax.ShapeDtypeStruct((16, 4, 2 * HD), F32),
+        out_shape=jax.ShapeDtypeStruct((32, 2, 2 * HD), F32),
         in_specs=[SMEM] + [VMEM] * 4,
         out_specs=VMEM,
         scratch_shapes=[
@@ -386,12 +382,12 @@
     mixed = jnp.concatenate([low, high, low, high], axis=0)
     mixed = lax.dynamic_slice_in_dim(mixed, (NY - yi) % NY, NY, 0).reshape(64, 2 * HD)
 
-    packed = lax.all_to_all(packed, "z", 0, 0).reshape(64, 2 * HD)
+    packed = lax.all_to_all(packed, ("z", "c"), 0, 0).reshape(64, 2 * HD)
     part = jnp.einsum("tk,nk->nt", packed, mixed, precision=lax.Precision.HIGHEST)
     part = part.reshape(NY, 1, 2, 8, 64)
     part = jnp.concatenate([part[:, :, 0], part[:, :, 1]], axis=3)
-    part = jnp.broadcast_to(part, (NY, 8, 8, 128)).reshape(32, 8, 128)
-    part = lax.all_to_all(part, ("y", "c", "x"), 0, 0)
+    part = jnp.broadcast_to(part, (NY, 4, 8, 128)).reshape(16, 8, 128)
+    part = lax.all_to_all(part, ("y", "x"), 0, 0)
     total = jnp.sum(part, axis=0)
     return jnp.concatenate([total[:, :64], total[:, 64:]], axis=0).T
 

time: 168 us -> 168 us (level)
  no operation moved by 1% of the time
where the time goes in v11:
time: 168 us; the launch traced here: 166 us
  blocking collectives  53.3 us (32%)
  starting transfers between devices  42.1 us (25%)
  waiting for transfers between devices  35.4 us (21%)
  Pallas kernels  15.2 us (9%)
  between operations  14.4 us (9%)
  local copies, waits for them, and re-layouts  3.66 us (2%)
    all_gather x1, blocking collectives, body(): own = lax.all_gather(first_shard, 'z', axis=0)  40.1 us
    all_to_all x1, waiting for transfers between devices, body(): packed = lax.all_to_all(packed, ('z', 'c'), 0, 0).reshape(64, 2 * HD)  14.3 us
    all_to_all x1, blocking collectives, body(): part = lax.all_to_all(part, ('y', 'x'), 0, 0)  11 us
    all_to_all x1, waiting for transfers between devices, body(): partial = lax.all_to_all(partial, ('x', 'y'), 0, 0)  9.82 us
    all_to_all x1, waiting for transfers between devices, body(): x1 = lax.all_to_all(spread, ('x', 'y'), 0, 0)  8.51 us
    all_to_all x1, starting transfers between devices, body(): lax.all_to_all(projected, ('x', 'y'), 0, 0).reshape(4, NY, NY, HD, 128)  8.31 us
    all_to_all x1, starting transfers between devices, body(): packed = lax.all_to_all(packed, ('z', 'c'), 0, 0).reshape(64, 2 * HD)  8.03 us
    all_to_all x1, starting transfers between devices, body(): partial = lax.all_to_all(partial, ('x', 'y'), 0, 0)  6.89 us
  transfers between devices with their start and end apart: 10, of which 5 were waited for; matrix products, arithmetic and copies ran while one was open for 2% of the time, Pallas kernels for 8%

profile of v11, /device:TPU:6, one launch (start us, length us, event | category | flops | bytes accessed | tf_op | source)
XLA Modules:
  0.0 166.3 jit_solution(1425697694692198627)
XLA Ops:
  7.2 1.8 %regroup.1 = bf16[8,4,32,120]{3,2,1,0:T(8,128)(2,1)} custom-call(s32[1,1]{1,0:T(1,128)} %bitcast.68.lengths, bf16[30,1440]{1,0:T(8,128)(2,1)} %bitcast.87, bf16[30,480]{1,0:T(8,128)(2,1)} %bitcast.89), custom_call_target="tpu_custom_call" | custom-call | bytes 400000 | tf_op jit(solution)/shard_map/regroup/pallas_call | solution.py:200
  8.9 4.5 %all-to-all-start = ((bf16[8,4,32,120]{3,2,1,0:T(8,128)(2,1)}), bf16[8,4,32,120]{3,2,1,0:T(8,128)(2,1)S(1)}, u32[]{:S(2)}, u32[]{:S(2)}) async-start(bf16[8,4,32,120]{3,2,1,0:T(8,128)(2,1)} %regroup.1), calls=%async_computation | async-start | bytes 524288 | tf_op jit(solution)/shard_map/all_to_all | solution.py:326
  13.4 2.2 %all-gather.2 = f32[2,1,1920]{2,1,0:T(1,128)S(1)} all-gather(f32[1,1,1920]{2,1,0:T(1,128)} %bitcast.90), channel_id=1, replica_groups=mesh['z'=16,'y'=4,'c'=2,'x'=4] {'c'}, dimensions={0}, use_global_device_ids=true | all-gather | bytes 23040 | tf_op jit(solution)/shard_map/all_gather | solution.py:327
  15.6 2.8 %layer_input.1 = bf16[16,4,120,128]{3,2,1,0:T(8,128)(2,1)} custom-call(bf16[480,512]{1,0:T(8,128)(2,1)} %bitcast.81, bf16[128,512]{1,0:T(8,128)(2,1)} %bitcast.85), custom_call_target="tpu_custom_call" | custom-call | flops 100000000 | bytes 3000000 | tf_op jit(solution)/shard_map/layer_input/pallas_call | solution.py:216
  18.4 2.6 %all-to-all-done = bf16[8,4,32,120]{3,2,1,0:T(8,128)(2,1)S(1)} async-done(((bf16[8,4,32,120]{3,2,1,0:T(8,128)(2,1)}), bf16[8,4,32,120]{3,2,1,0:T(8,128)(2,1)S(1)}, u32[]{:S(2)}, u32[]{:S(2)}) %all-to-all-start) | async-done | bytes 245792 | tf_op jit(solution)/shard_map/all_to_all | solution.py:326
  21.0 0.1 slice_reduce_fusion.2
  21.5 8.3 %all-to-all-start.1 = ((bf16[16,4,120,128]{3,2,1,0:T(8,128)(2,1)}), bf16[16,4,120,128]{3,2,1,0:T(8,128)(2,1)S(1)}, u32[]{:S(2)}, u32[]{:S(2)}) async-start(bf16[16,4,120,128]{3,2,1,0:T(8,128)(2,1)} %layer_input.1), calls=%async_computation.1 | async-start | bytes 3932160 | tf_op jit(solution)/shard_map/all_to_all | solution.py:344
  30.0 0.8 copy.35
  30.8 0.1 copy.33
  30.9 40.1 %all-gather = bf16[32,120,120]{2,1,0:T(8,128)(2,1)S(1)} all-gather(bf16[2,120,120]{2,1,0:T(8,128)(2,1)S(1)} %copy.33), channel_id=2, replica_groups=mesh['z'=16,'y'=4,'c'=2,'x'=4] {'z'}, dimensions={0}, use_global_device_ids=true | all-gather | bytes 979200 | tf_op jit(solution)/shard_map/all_gather | solution.py:341
  71.0 1.9 %collective-permute-start = (bf16[16,2,120,120]{3,2,1,0:T(8,128)(2,1)S(1)}, bf16[16,2,120,120]{3,2,1,0:T(8,128)(2,1)}, u32[]{:S(2)}, u32[]{:S(2)}) collective-permute-start(bf16[16,2,120,120]{3,2,1,0:T(8,128)(2,1)S(1)} %bitcast.71), channel_id=1, source_target_pairs={{0,4},{4,0},{1,5},{5,1},{2,6},{6,2},{3,7},{7,3},{8,12},{12,8},{9,1... | collective-permute-start | bytes 2764808 | tf_op jit(solution)/shard_map/ppermute | solution.py:18
  73.2 2.2 %first_norm.1 = (bf16[16,120,256]{2,1,0:T(8,128)(2,1)S(1)}, bf16[2,120,256]{2,1,0:T(8,128)(2,1)S(1)}) custom-call(s32[5]{0:T(128)S(1)} %pad_add_fusion.scalars, bf16[4,4,4,120,128]{4,3,2,1,0:T(8,128)(2,1)S(1)} %bitcast.69, bf16[16,2,120,120]{3,2,1,0:T(8,128)(2,1)S(1)} %bitcast.72, f32[16,120]{1,0:T(8,128)S(1)} %squeeze.42.gain), custom_call_target="tpu_custom_call" | custom-call | flops 400000000 | bytes 4000000 | tf_op jit(solution)/shard_map/first_norm/pallas_call | solution.py:238
  75.4 0.2 collective-permute-done.other
  75.6 3.6 %first_attend.1 = (bf16[16,120,256]{2,1,0:T(8,128)(2,1)}, bf16[120,256]{1,0:T(8,128)(2,1)S(1)}) custom-call(s32[5]{0:T(128)S(1)} %pad_add_fusion.scalars, bf16[4,4,4,120,128]{4,3,2,1,0:T(8,128)(2,1)S(1)} %bitcast.70, bf16[16,120,256]{2,1,0:T(8,128)(2,1)S(1)} %get-tuple-element.24.normed, bf16[2,120,256]{2,1,0:T(8,128)(2,1)S(1)} %get-tuple-element.25.mine, ...), custom_call_target="tpu_custom_call" | custom-call | flops 600000000 | bytes 5000000 | tf_op jit(solution)/shard_map/first_attend/pallas_call | solution.py:253
  79.2 6.9 %all-to-all-start.2 = ((bf16[16,120,256]{2,1,0:T(8,128)(2,1)}), bf16[16,120,256]{2,1,0:T(8,128)(2,1)S(1)}, u32[]{:S(2)}, u32[]{:S(2)}) async-start(bf16[16,120,256]{2,1,0:T(8,128)(2,1)} %get-tuple-element.29), calls=%async_computation.2 | async-start | bytes 1966080 | tf_op jit(solution)/shard_map/all_to_all | solution.py:357
  86.1 0.2 reshape.78
  86.6 4.6 %collective-permute-start.1 = (f32[16,16,120]{2,1,0:T(8,128)S(1)}, f32[16,16,120]{2,1,0:T(8,128)S(1)}, u32[]{:S(2)}, u32[]{:S(2)}) collective-permute-start(f32[16,16,120]{2,1,0:T(8,128)S(1)} %bitcast.78), channel_id=1, source_target_pairs={{8,0},{20,4},{16,8},{28,12},{24,16},{4,20},{0,24},{12,28},{9,1},{2... | collective-permute-start | bytes 368648 | tf_op jit(solution)/shard_map/ppermute | solution.py:354
  91.2 0.7 collective-permute-start.2
  91.9 9.8 %all-to-all-done.2.partial = bf16[16,120,256]{2,1,0:T(8,128)(2,1)S(1)} async-done(((bf16[16,120,256]{2,1,0:T(8,128)(2,1)}), bf16[16,120,256]{2,1,0:T(8,128)(2,1)S(1)}, u32[]{:S(2)}, u32[]{:S(2)}) %all-to-all-start.2) | async-done | bytes 983072 | tf_op jit(solution)/shard_map/all_to_all | solution.py:357
  101.7 1.3 combine.1
  103.0 5.3 %all-to-all-start.3 = ((bf16[16,120,256]{2,1,0:T(8,128)(2,1)}), bf16[16,120,256]{2,1,0:T(8,128)(2,1)S(1)}, u32[]{:S(2)}, u32[]{:S(2)}) async-start(bf16[16,120,256]{2,1,0:T(8,128)(2,1)} %get-tuple-element.31), calls=%async_computation.3 | async-start | bytes 1966080 | tf_op jit(solution)/shard_map/all_to_all | solution.py:359
  108.5 0.2 multiply_reduce_fusion
  108.8 1.5 copy-done
  110.4 0.5 convolution_bitcast_fusion.1
  111.0 1.9 %collective-permute-start.3 = (f32[2,16,240]{2,1,0:T(8,128)S(1)}, f32[2,16,240]{2,1,0:T(8,128)S(1)}, u32[]{:S(2)}, u32[]{:S(2)}) collective-permute-start(f32[2,16,240]{2,1,0:T(8,128)S(1)} %pad_maximum_fusion.3), channel_id=1, source_target_pairs={{0,4},{4,0},{1,5},{5,1},{2,6},{6,2},{3,7},{7,3},{8,12},{12,8},{9,1... | collective-permute-start | bytes 92168 | tf_op jit(solution)/shard_map/ppermute | solution.py:18
  112.9 8.5 %all-to-all-done.3.x1 = bf16[16,120,256]{2,1,0:T(8,128)(2,1)S(1)} async-done(((bf16[16,120,256]{2,1,0:T(8,128)(2,1)}), bf16[16,120,256]{2,1,0:T(8,128)(2,1)S(1)}, u32[]{:S(2)}, u32[]{:S(2)}) %all-to-all-start.3) | async-done | bytes 983072 | tf_op jit(solution)/shard_map/all_to_all | solution.py:359
  121.4 3.5 %second_layer.1 = f32[32,2,240]{2,1,0:T(2,128)} custom-call(s32[5]{0:T(128)S(1)} %pad_add_fusion.scalars, bf16[16,120,256]{2,1,0:T(8,128)(2,1)S(1)} %all-to-all-done.3.x1, bf16[16,3,120,120]{3,2,1,0:T(8,128)(2,1)S(1)} %stage.1.weights, f32[16,120]{1,0:T(8,128)S(1)} %squeeze.45.gain, f32[2,120]{1,0:T(2,128)S(1)} %subtract_bitcast_fusion.rest), custom_call_target="tpu_custom_call" | custom-call | flops 1000000000 | bytes 6000000 | tf_op jit(solution)/shard_map/second_layer/pallas_call | solution.py:303
  124.9 8.0 %all-to-all-start.4 = ((f32[32,2,240]{2,1,0:T(2,128)}), f32[32,2,240]{2,1,0:T(2,128)S(1)}, u32[]{:S(2)}, u32[]{:S(2)}) async-start(f32[32,2,240]{2,1,0:T(2,128)} %second_layer.1), calls=%async_computation.4 | async-start | bytes 131072 | tf_op jit(solution)/shard_map/all_to_all | solution.py:385
  133.1 14.3 %all-to-all-done.4 = f32[32,2,240]{2,1,0:T(2,128)S(1)} async-done(((f32[32,2,240]{2,1,0:T(2,128)}), f32[32,2,240]{2,1,0:T(2,128)S(1)}, u32[]{:S(2)}, u32[]{:S(2)}) %all-to-all-start.4) | async-done | bytes 61472 | tf_op jit(solution)/shard_map/all_to_all | solution.py:385
  147.4 0.2 convolution_bitcast_fusion
  147.8 11.0 %all_to_all.30 = f32[16,8,128]{2,1,0:T(8,128)S(1)} all-to-all(f32[16,8,128]{2,1,0:T(8,128)S(1)} %bitcast.84), channel_id=1, replica_groups=mesh['z'=16,'y'=4,'c'=2,'x'=4] {'y','x'}, dimensions={0} | all-to-all | bytes 131072 | tf_op jit(solution)/shard_map/all_to_all | solution.py:390
  158.8 0.6 maximum_bitcast_fusion.1
  (51 shorter events, 1.8 us)
Async XLA Ops:
  8.9 12.0 %all-to-all-start = ((bf16[8,4,32,120]{3,2,1,0:T(8,128)(2,1)}), bf16[8,4,32,120]{3,2,1,0:T(8,128)(2,1)S(1)}, u32[]{:S(2)}, u32[]{:S(2)}) async-start(bf16[8,4,32,120]{3,2,1,0:T(8,128)(2,1)} %regroup.1), calls=%async_computation | async-start | bytes 524288 | tf_op jit(solution)/shard_map/all_to_all | solution.py:326
  21.5 51.6 %all-to-all-start.1 = ((bf16[16,4,120,128]{3,2,1,0:T(8,128)(2,1)}), bf16[16,4,120,128]{3,2,1,0:T(8,128)(2,1)S(1)}, u32[]{:S(2)}, u32[]{:S(2)}) async-start(bf16[16,4,120,128]{3,2,1,0:T(8,128)(2,1)} %layer_input.1), calls=%async_computation.1 | async-start | bytes 3932160 | tf_op jit(solution)/shard_map/all_to_all | solution.py:344
  29.8 78.9 %all-gather.5.cloned.1.call-start = ((), (), s32[]{:S(2)}) async-start(), calls=%async_computation.6 | async-start | bytes 2088960 | tf_op jit(solution)/shard_map/all_gather | solution.py:340
  71.0 4.6 %collective-permute-start = (bf16[16,2,120,120]{3,2,1,0:T(8,128)(2,1)S(1)}, bf16[16,2,120,120]{3,2,1,0:T(8,128)(2,1)}, u32[]{:S(2)}, u32[]{:S(2)}) collective-permute-start(bf16[16,2,120,120]{3,2,1,0:T(8,128)(2,1)S(1)} %bitcast.71), channel_id=1, source_target_pairs={{0,4},{4,0},{1,5},{5,1},{2,6},{6,2},{3,7},{7,3},{8,12},{12,8},{9,1... | collective-permute-start | bytes 2764808 | tf_op jit(solution)/shard_map/ppermute | solution.py:18
  79.2 6.9 %copy-start.1 = (f32[1920,16]{0,1:T(8,128)S(1)}, f32[1920,16]{0,1:T(8,128)}, u32[]{:S(2)}) copy-start(f32[1920,16]{0,1:T(8,128)} %param.15) | copy-start | bytes 368644
  79.2 7.1 %copy-start.2 = (f32[1920]{0:T(1024)S(1)}, f32[1920]{0:T(1024)}, u32[]{:S(2)}) copy-start(f32[1920]{0:T(1024)} %param.14) | copy-start | bytes 23044
  79.2 22.5 %all-to-all-start.2 = ((bf16[16,120,256]{2,1,0:T(8,128)(2,1)}), bf16[16,120,256]{2,1,0:T(8,128)(2,1)S(1)}, u32[]{:S(2)}, u32[]{:S(2)}) async-start(bf16[16,120,256]{2,1,0:T(8,128)(2,1)} %get-tuple-element.29), calls=%async_computation.2 | async-start | bytes 1966080 | tf_op jit(solution)/shard_map/all_to_all | solution.py:357
  86.6 21.7 %collective-permute-start.1 = (f32[16,16,120]{2,1,0:T(8,128)S(1)}, f32[16,16,120]{2,1,0:T(8,128)S(1)}, u32[]{:S(2)}, u32[]{:S(2)}) collective-permute-start(f32[16,16,120]{2,1,0:T(8,128)S(1)} %bitcast.78), channel_id=1, source_target_pairs={{8,0},{20,4},{16,8},{28,12},{24,16},{4,20},{0,24},{12,28},{9,1},{2... | collective-permute-start | bytes 368648 | tf_op jit(solution)/shard_map/ppermute | solution.py:354
  91.2 17.2 %collective-permute-start.2 = (f32[16,16,120]{2,1,0:T(8,128)S(1)}, f32[16,16,120]{2,1,0:T(8,128)S(1)}, u32[]{:S(2)}, u32[]{:S(2)}) collective-permute-start(f32[16,16,120]{2,1,0:T(8,128)S(1)} %bitcast.79), channel_id=1, source_target_pairs={{28,4},{4,12},{12,20},{20,28},{29,5},{5,13},{13,21},{21,29},{30,6}... | collective-permute-start | bytes 368648 | tf_op jit(solution)/shard_map/ppermute | solution.py:355
  103.0 18.4 %all-to-all-start.3 = ((bf16[16,120,256]{2,1,0:T(8,128)(2,1)}), bf16[16,120,256]{2,1,0:T(8,128)(2,1)S(1)}, u32[]{:S(2)}, u32[]{:S(2)}) async-start(bf16[16,120,256]{2,1,0:T(8,128)(2,1)} %get-tuple-element.31), calls=%async_computation.3 | async-start | bytes 1966080 | tf_op jit(solution)/shard_map/all_to_all | solution.py:359
  108.7 1.6 copy-start
  111.0 22.0 %collective-permute-start.3 = (f32[2,16,240]{2,1,0:T(8,128)S(1)}, f32[2,16,240]{2,1,0:T(8,128)S(1)}, u32[]{:S(2)}, u32[]{:S(2)}) collective-permute-start(f32[2,16,240]{2,1,0:T(8,128)S(1)} %pad_maximum_fusion.3), channel_id=1, source_target_pairs={{0,4},{4,0},{1,5},{5,1},{2,6},{6,2},{3,7},{7,3},{8,12},{12,8},{9,1... | collective-permute-start | bytes 92168 | tf_op jit(solution)/shard_map/ppermute | solution.py:18
  124.9 22.5 %all-to-all-start.4 = ((f32[32,2,240]{2,1,0:T(2,128)}), f32[32,2,240]{2,1,0:T(2,128)S(1)}, u32[]{:S(2)}, u32[]{:S(2)}) async-start(f32[32,2,240]{2,1,0:T(2,128)} %second_layer.1), calls=%async_computation.4 | async-start | bytes 131072 | tf_op jit(solution)/shard_map/all_to_all | solution.py:385
Sparse Core Ops, SparseCore 0:
  32.7 74.8 all-gather.4

commit v12 on v11

--- a/solution.py
+++ b/solution.py
@@ -101,7 +101,7 @@
     core = scalars[0]
     gain_rows = gain[...].T
     for u in range(2):
-        picks = [raw[x, 2 * core + u] for x in range(4)]
+        picks = [raw[2 * core + u, x] for x in range(4)]
         values = jnp.concatenate(picks, axis=0)
         normalize(values, gain_rows, normed, utterance(u))
     project(normed, own, 0, mine, 0)
@@ -112,9 +112,9 @@
     scalars, raw, normed, mine, own, other, partial_hbm, kept, rest, context, partial, sent
 ):
     core = scalars[0]
-    xi, yi = scalars[1], scalars[2]
+    major, minor = scalars[1], scalars[2]
     for u in range(2):
-        kept[:, utterance(u)] = raw[xi, 2 * core + u, yi]
+        kept[:, utterance(u)] = raw[2 * core + u, major, minor]
 
     def attend_all(query, keys, values):
         for u in range(2):
@@ -318,7 +318,7 @@
 def body(frames, lengths, feature_proj, norm_gain, qkv_weight, out_weight, center, whitening):
     core = lax.axis_index("c")
     xi, yi = lax.axis_index("x"), lax.axis_index("y")
-    chunk = xi * NY + yi
+    chunk = yi * 4 + xi
 
     projected = run_input(feature_proj.T, frames[0])
 
@@ -341,9 +341,9 @@
     own = lax.all_gather(first_shard, "z", axis=0)
     other = swap_cores(own)
 
-    raw = lax.all_to_all(projected, ("x", "y"), 0, 0).reshape(4, NY, NY, HD, 128)
-
-    scalars = jnp.concatenate([jnp.stack([core, xi, yi]).astype(jnp.int32), my_lengths])
+    raw = lax.all_to_all(projected, ("y", "x"), 0, 0).reshape(NY, 4, NY, HD, 128)
+
+    scalars = jnp.concatenate([jnp.stack([core, yi, xi]).astype(jnp.int32), my_lengths])
     gains = gains.reshape(2, CHUNKS, HD)
     normed, mine = run_norm(scalars, raw, own, gains[0])
     partial, x0_own = run_attend(scalars, raw, normed, mine, own, other)
@@ -354,9 +354,9 @@
     white_near = lax.ppermute(white, ("y", "c"), near)
     white_far = lax.ppermute(white, ("y", "c"), far)
 
-    partial = lax.all_to_all(partial, ("x", "y"), 0, 0)
+    partial = lax.all_to_all(partial, ("y", "x"), 0, 0)
     spread, x1_own = run_combine(partial, x0_own)
-    x1 = lax.all_to_all(spread, ("x", "y"), 0, 0)
+    x1 = lax.all_to_all(spread, ("y", "x"), 0, 0)
 
     valid = jnp.arange(128)[None, :] < my_lengths[:, None]
     share = valid.astype(F32) / my_lengths.astype(F32)[:, None]

time: 168 us -> 168 us (level)
  no operation moved by 1% of the time
where the time goes in v12:
time: 168 us; the launch traced here: 167 us
  blocking collectives  53.5 us (32%)
  starting transfers between devices  42.6 us (25%)
  waiting for transfers between devices  35.1 us (21%)
  Pallas kernels  15.2 us (9%)
  between operations  14.4 us (9%)
  local copies, waits for them, and re-layouts  3.66 us (2%)
    all_gather x1, blocking collectives, body(): own = lax.all_gather(first_shard, 'z', axis=0)  40.1 us
    all_to_all x1, waiting for transfers between devices, body(): packed = lax.all_to_all(packed, ('z', 'c'), 0, 0).reshape(64, 2 * HD)  14.3 us
    all_to_all x1, blocking collectives, body(): part = lax.all_to_all(part, ('y', 'x'), 0, 0)  11.2 us
    all_to_all x1, waiting for transfers between devices, body(): partial = lax.all_to_all(partial, ('y', 'x'), 0, 0)  9.13 us
    all_to_all x1, waiting for transfers between devices, body(): x1 = lax.all_to_all(spread, ('y', 'x'), 0, 0)  8.8 us
    all_to_all x1, starting transfers between devices, body(): lax.all_to_all(projected, ('y', 'x'), 0, 0).reshape(NY, 4, NY, HD, 128)  8.25 us
    all_to_all x1, starting transfers between devices, body(): packed = lax.all_to_all(packed, ('z', 'c'), 0, 0).reshape(64, 2 * HD)  8.16 us
    all_to_all x1, starting transfers between devices, body(): partial = lax.all_to_all(partial, ('y', 'x'), 0, 0)  6.94 us
  transfers between devices with their start and end apart: 10, of which 5 were waited for; matrix products, arithmetic and copies ran while one was open for 2% of the time, Pallas kernels for 8%

profile of v12, /device:TPU:6, one launch (start us, length us, event | category | flops | bytes accessed | tf_op | source)
XLA Modules:
  0.0 166.6 jit_solution(3078597859701411509)
XLA Ops:
  7.2 1.8 %regroup.1 = bf16[8,4,32,120]{3,2,1,0:T(8,128)(2,1)} custom-call(s32[1,1]{1,0:T(1,128)} %bitcast.68.lengths, bf16[30,1440]{1,0:T(8,128)(2,1)} %bitcast.87, bf16[30,480]{1,0:T(8,128)(2,1)} %bitcast.89), custom_call_target="tpu_custom_call" | custom-call | bytes 400000 | tf_op jit(solution)/shard_map/regroup/pallas_call | solution.py:200
  8.9 4.5 %all-to-all-start = ((bf16[8,4,32,120]{3,2,1,0:T(8,128)(2,1)}), bf16[8,4,32,120]{3,2,1,0:T(8,128)(2,1)S(1)}, u32[]{:S(2)}, u32[]{:S(2)}) async-start(bf16[8,4,32,120]{3,2,1,0:T(8,128)(2,1)} %regroup.1), calls=%async_computation | async-start | bytes 524288 | tf_op jit(solution)/shard_map/all_to_all | solution.py:326
  13.4 2.2 %all-gather.2 = f32[2,1,1920]{2,1,0:T(1,128)S(1)} all-gather(f32[1,1,1920]{2,1,0:T(1,128)} %bitcast.90), channel_id=1, replica_groups=mesh['z'=16,'y'=4,'c'=2,'x'=4] {'c'}, dimensions={0}, use_global_device_ids=true | all-gather | bytes 23040 | tf_op jit(solution)/shard_map/all_gather | solution.py:327
  15.6 2.8 %layer_input.1 = bf16[16,4,120,128]{3,2,1,0:T(8,128)(2,1)} custom-call(bf16[480,512]{1,0:T(8,128)(2,1)} %bitcast.81, bf16[128,512]{1,0:T(8,128)(2,1)} %bitcast.85), custom_call_target="tpu_custom_call" | custom-call | flops 100000000 | bytes 3000000 | tf_op jit(solution)/shard_map/layer_input/pallas_call | solution.py:216
  18.4 2.6 %all-to-all-done = bf16[8,4,32,120]{3,2,1,0:T(8,128)(2,1)S(1)} async-done(((bf16[8,4,32,120]{3,2,1,0:T(8,128)(2,1)}), bf16[8,4,32,120]{3,2,1,0:T(8,128)(2,1)S(1)}, u32[]{:S(2)}, u32[]{:S(2)}) %all-to-all-start) | async-done | bytes 245792 | tf_op jit(solution)/shard_map/all_to_all | solution.py:326
  21.0 0.1 slice_reduce_fusion.2
  21.5 8.2 %all-to-all-start.1 = ((bf16[16,4,120,128]{3,2,1,0:T(8,128)(2,1)}), bf16[16,4,120,128]{3,2,1,0:T(8,128)(2,1)S(1)}, u32[]{:S(2)}, u32[]{:S(2)}) async-start(bf16[16,4,120,128]{3,2,1,0:T(8,128)(2,1)} %layer_input.1), calls=%async_computation.1 | async-start | bytes 3932160 | tf_op jit(solution)/shard_map/all_to_all | solution.py:344
  30.0 0.8 copy.35
  30.8 0.1 copy.33
  30.9 40.1 %all-gather = bf16[32,120,120]{2,1,0:T(8,128)(2,1)S(1)} all-gather(bf16[2,120,120]{2,1,0:T(8,128)(2,1)S(1)} %copy.33), channel_id=2, replica_groups=mesh['z'=16,'y'=4,'c'=2,'x'=4] {'z'}, dimensions={0}, use_global_device_ids=true | all-gather | bytes 979200 | tf_op jit(solution)/shard_map/all_gather | solution.py:341
  71.0 1.9 %collective-permute-start = (bf16[16,2,120,120]{3,2,1,0:T(8,128)(2,1)S(1)}, bf16[16,2,120,120]{3,2,1,0:T(8,128)(2,1)}, u32[]{:S(2)}, u32[]{:S(2)}) collective-permute-start(bf16[16,2,120,120]{3,2,1,0:T(8,128)(2,1)S(1)} %bitcast.71), channel_id=1, source_target_pairs={{0,4},{4,0},{1,5},{5,1},{2,6},{6,2},{3,7},{7,3},{8,12},{12,8},{9,1... | collective-permute-start | bytes 2764808 | tf_op jit(solution)/shard_map/ppermute | solution.py:18
  73.1 2.2 %first_norm.1 = (bf16[16,120,256]{2,1,0:T(8,128)(2,1)S(1)}, bf16[2,120,256]{2,1,0:T(8,128)(2,1)S(1)}) custom-call(s32[5]{0:T(128)S(1)} %pad_add_fusion.scalars, bf16[4,4,4,120,128]{4,3,2,1,0:T(8,128)(2,1)S(1)} %bitcast.69, bf16[16,2,120,120]{3,2,1,0:T(8,128)(2,1)S(1)} %bitcast.72, f32[16,120]{1,0:T(8,128)S(1)} %squeeze.42.gain), custom_call_target="tpu_custom_call" | custom-call | flops 400000000 | bytes 4000000 | tf_op jit(solution)/shard_map/first_norm/pallas_call | solution.py:238
  75.4 0.2 collective-permute-done.other
  75.6 3.6 %first_attend.1 = (bf16[16,120,256]{2,1,0:T(8,128)(2,1)}, bf16[120,256]{1,0:T(8,128)(2,1)S(1)}) custom-call(s32[5]{0:T(128)S(1)} %pad_add_fusion.scalars, bf16[4,4,4,120,128]{4,3,2,1,0:T(8,128)(2,1)S(1)} %bitcast.70, bf16[16,120,256]{2,1,0:T(8,128)(2,1)S(1)} %get-tuple-element.24.normed, bf16[2,120,256]{2,1,0:T(8,128)(2,1)S(1)} %get-tuple-element.25.mine, ...), custom_call_target="tpu_custom_call" | custom-call | flops 600000000 | bytes 5000000 | tf_op jit(solution)/shard_map/first_attend/pallas_call | solution.py:253
  79.2 6.9 %all-to-all-start.2 = ((bf16[16,120,256]{2,1,0:T(8,128)(2,1)}), bf16[16,120,256]{2,1,0:T(8,128)(2,1)S(1)}, u32[]{:S(2)}, u32[]{:S(2)}) async-start(bf16[16,120,256]{2,1,0:T(8,128)(2,1)} %get-tuple-element.29), calls=%async_computation.2 | async-start | bytes 1966080 | tf_op jit(solution)/shard_map/all_to_all | solution.py:357
  86.2 0.2 reshape.78
  86.6 4.6 %collective-permute-start.1 = (f32[16,16,120]{2,1,0:T(8,128)S(1)}, f32[16,16,120]{2,1,0:T(8,128)S(1)}, u32[]{:S(2)}, u32[]{:S(2)}) collective-permute-start(f32[16,16,120]{2,1,0:T(8,128)S(1)} %bitcast.78), channel_id=1, source_target_pairs={{8,0},{20,4},{16,8},{28,12},{24,16},{4,20},{0,24},{12,28},{9,1},{2... | collective-permute-start | bytes 368648 | tf_op jit(solution)/shard_map/ppermute | solution.py:354
  91.2 0.7 collective-permute-start.2
  92.0 9.1 %all-to-all-done.2.partial = bf16[16,120,256]{2,1,0:T(8,128)(2,1)S(1)} async-done(((bf16[16,120,256]{2,1,0:T(8,128)(2,1)}), bf16[16,120,256]{2,1,0:T(8,128)(2,1)S(1)}, u32[]{:S(2)}, u32[]{:S(2)}) %all-to-all-start.2) | async-done | bytes 983072 | tf_op jit(solution)/shard_map/all_to_all | solution.py:357
  101.1 1.3 combine.1
  102.4 5.7 %all-to-all-start.3 = ((bf16[16,120,256]{2,1,0:T(8,128)(2,1)}), bf16[16,120,256]{2,1,0:T(8,128)(2,1)S(1)}, u32[]{:S(2)}, u32[]{:S(2)}) async-start(bf16[16,120,256]{2,1,0:T(8,128)(2,1)} %get-tuple-element.31), calls=%async_computation.3 | async-start | bytes 1966080 | tf_op jit(solution)/shard_map/all_to_all | solution.py:359
  108.2 0.2 multiply_reduce_fusion
  108.5 1.5 copy-done
  110.2 0.5 convolution_bitcast_fusion.1
  110.7 1.9 %collective-permute-start.3 = (f32[2,16,240]{2,1,0:T(8,128)S(1)}, f32[2,16,240]{2,1,0:T(8,128)S(1)}, u32[]{:S(2)}, u32[]{:S(2)}) collective-permute-start(f32[2,16,240]{2,1,0:T(8,128)S(1)} %pad_maximum_fusion.3), channel_id=1, source_target_pairs={{0,4},{4,0},{1,5},{5,1},{2,6},{6,2},{3,7},{7,3},{8,12},{12,8},{9,1... | collective-permute-start | bytes 92168 | tf_op jit(solution)/shard_map/ppermute | solution.py:18
  112.7 8.8 %all-to-all-done.3.x1 = bf16[16,120,256]{2,1,0:T(8,128)(2,1)S(1)} async-done(((bf16[16,120,256]{2,1,0:T(8,128)(2,1)}), bf16[16,120,256]{2,1,0:T(8,128)(2,1)S(1)}, u32[]{:S(2)}, u32[]{:S(2)}) %all-to-all-start.3) | async-done | bytes 983072 | tf_op jit(solution)/shard_map/all_to_all | solution.py:359
  121.5 3.5 %second_layer.1 = f32[32,2,240]{2,1,0:T(2,128)} custom-call(s32[5]{0:T(128)S(1)} %pad_add_fusion.scalars, bf16[16,120,256]{2,1,0:T(8,128)(2,1)S(1)} %all-to-all-done.3.x1, bf16[16,3,120,120]{3,2,1,0:T(8,128)(2,1)S(1)} %stage.1.weights, f32[16,120]{1,0:T(8,128)S(1)} %squeeze.45.gain, f32[2,120]{1,0:T(2,128)S(1)} %subtract_bitcast_fusion.rest), custom_call_target="tpu_custom_call" | custom-call | flops 1000000000 | bytes 6000000 | tf_op jit(solution)/shard_map/second_layer/pallas_call | solution.py:303
  125.0 8.2 %all-to-all-start.4 = ((f32[32,2,240]{2,1,0:T(2,128)}), f32[32,2,240]{2,1,0:T(2,128)S(1)}, u32[]{:S(2)}, u32[]{:S(2)}) async-start(f32[32,2,240]{2,1,0:T(2,128)} %second_layer.1), calls=%async_computation.4 | async-start | bytes 131072 | tf_op jit(solution)/shard_map/all_to_all | solution.py:385
  133.2 14.3 %all-to-all-done.4 = f32[32,2,240]{2,1,0:T(2,128)S(1)} async-done(((f32[32,2,240]{2,1,0:T(2,128)}), f32[32,2,240]{2,1,0:T(2,128)S(1)}, u32[]{:S(2)}, u32[]{:S(2)}) %all-to-all-start.4) | async-done | bytes 61472 | tf_op jit(solution)/shard_map/all_to_all | solution.py:385
  147.6 0.2 convolution_bitcast_fusion
  147.9 11.2 %all_to_all.30 = f32[16,8,128]{2,1,0:T(8,128)S(1)} all-to-all(f32[16,8,128]{2,1,0:T(8,128)S(1)} %bitcast.84), channel_id=1, replica_groups=mesh['z'=16,'y'=4,'c'=2,'x'=4] {'y','x'}, dimensions={0} | all-to-all | bytes 131072 | tf_op jit(solution)/shard_map/all_to_all | solution.py:390
  159.2 0.6 maximum_bitcast_fusion.1
  (51 shorter events, 1.8 us)
Async XLA Ops:
  8.9 12.0 %all-to-all-start = ((bf16[8,4,32,120]{3,2,1,0:T(8,128)(2,1)}), bf16[8,4,32,120]{3,2,1,0:T(8,128)(2,1)S(1)}, u32[]{:S(2)}, u32[]{:S(2)}) async-start(bf16[8,4,32,120]{3,2,1,0:T(8,128)(2,1)} %regroup.1), calls=%async_computation | async-start | bytes 524288 | tf_op jit(solution)/shard_map/all_to_all | solution.py:326
  21.5 51.6 %all-to-all-start.1 = ((bf16[16,4,120,128]{3,2,1,0:T(8,128)(2,1)}), bf16[16,4,120,128]{3,2,1,0:T(8,128)(2,1)S(1)}, u32[]{:S(2)}, u32[]{:S(2)}) async-start(bf16[16,4,120,128]{3,2,1,0:T(8,128)(2,1)} %layer_input.1), calls=%async_computation.1 | async-start | bytes 3932160 | tf_op jit(solution)/shard_map/all_to_all | solution.py:344
  29.8 78.7 %all-gather.5.cloned.1.call-start = ((), (), s32[]{:S(2)}) async-start(), calls=%async_computation.6 | async-start | bytes 2088960 | tf_op jit(solution)/shard_map/all_gather | solution.py:340
  71.0 4.6 %collective-permute-start = (bf16[16,2,120,120]{3,2,1,0:T(8,128)(2,1)S(1)}, bf16[16,2,120,120]{3,2,1,0:T(8,128)(2,1)}, u32[]{:S(2)}, u32[]{:S(2)}) collective-permute-start(bf16[16,2,120,120]{3,2,1,0:T(8,128)(2,1)S(1)} %bitcast.71), channel_id=1, source_target_pairs={{0,4},{4,0},{1,5},{5,1},{2,6},{6,2},{3,7},{7,3},{8,12},{12,8},{9,1... | collective-permute-start | bytes 2764808 | tf_op jit(solution)/shard_map/ppermute | solution.py:18
  79.2 7.0 %copy-start.1 = (f32[1920,16]{0,1:T(8,128)S(1)}, f32[1920,16]{0,1:T(8,128)}, u32[]{:S(2)}) copy-start(f32[1920,16]{0,1:T(8,128)} %param.15) | copy-start | bytes 368644
  79.2 7.2 %copy-start.2 = (f32[1920]{0:T(1024)S(1)}, f32[1920]{0:T(1024)}, u32[]{:S(2)}) copy-start(f32[1920]{0:T(1024)} %param.14) | copy-start | bytes 23044
  79.2 21.9 %all-to-all-start.2 = ((bf16[16,120,256]{2,1,0:T(8,128)(2,1)}), bf16[16,120,256]{2,1,0:T(8,128)(2,1)S(1)}, u32[]{:S(2)}, u32[]{:S(2)}) async-start(bf16[16,120,256]{2,1,0:T(8,128)(2,1)} %get-tuple-element.29), calls=%async_computation.2 | async-start | bytes 1966080 | tf_op jit(solution)/shard_map/all_to_all | solution.py:357
  86.6 21.5 %collective-permute-start.1 = (f32[16,16,120]{2,1,0:T(8,128)S(1)}, f32[16,16,120]{2,1,0:T(8,128)S(1)}, u32[]{:S(2)}, u32[]{:S(2)}) collective-permute-start(f32[16,16,120]{2,1,0:T(8,128)S(1)} %bitcast.78), channel_id=1, source_target_pairs={{8,0},{20,4},{16,8},{28,12},{24,16},{4,20},{0,24},{12,28},{9,1},{2... | collective-permute-start | bytes 368648 | tf_op jit(solution)/shard_map/ppermute | solution.py:354
  91.2 16.9 %collective-permute-start.2 = (f32[16,16,120]{2,1,0:T(8,128)S(1)}, f32[16,16,120]{2,1,0:T(8,128)S(1)}, u32[]{:S(2)}, u32[]{:S(2)}) collective-permute-start(f32[16,16,120]{2,1,0:T(8,128)S(1)} %bitcast.79), channel_id=1, source_target_pairs={{28,4},{4,12},{12,20},{20,28},{29,5},{5,13},{13,21},{21,29},{30,6}... | collective-permute-start | bytes 368648 | tf_op jit(solution)/shard_map/ppermute | solution.py:355
  102.4 19.1 %all-to-all-start.3 = ((bf16[16,120,256]{2,1,0:T(8,128)(2,1)}), bf16[16,120,256]{2,1,0:T(8,128)(2,1)S(1)}, u32[]{:S(2)}, u32[]{:S(2)}) async-start(bf16[16,120,256]{2,1,0:T(8,128)(2,1)} %get-tuple-element.31), calls=%async_computation.3 | async-start | bytes 1966080 | tf_op jit(solution)/shard_map/all_to_all | solution.py:359
  108.5 1.6 copy-start
  110.7 22.4 %collective-permute-start.3 = (f32[2,16,240]{2,1,0:T(8,128)S(1)}, f32[2,16,240]{2,1,0:T(8,128)S(1)}, u32[]{:S(2)}, u32[]{:S(2)}) collective-permute-start(f32[2,16,240]{2,1,0:T(8,128)S(1)} %pad_maximum_fusion.3), channel_id=1, source_target_pairs={{0,4},{4,0},{1,5},{5,1},{2,6},{6,2},{3,7},{7,3},{8,12},{12,8},{9,1... | collective-permute-start | bytes 92168 | tf_op jit(solution)/shard_map/ppermute | solution.py:18
  125.0 22.6 %all-to-all-start.4 = ((f32[32,2,240]{2,1,0:T(2,128)}), f32[32,2,240]{2,1,0:T(2,128)S(1)}, u32[]{:S(2)}, u32[]{:S(2)}) async-start(f32[32,2,240]{2,1,0:T(2,128)} %second_layer.1), calls=%async_computation.4 | async-start | bytes 131072 | tf_op jit(solution)/shard_map/all_to_all | solution.py:385
Sparse Core Ops, SparseCore 0:
  32.7 74.8 all-gather.4

commit v13 on v11

--- a/solution.py
+++ b/solution.py
@@ -164,12 +164,6 @@
         copy.start()
     for copy in copies:
         copy.wait()
-
-
-def stage_kernel(weights_hbm, staged, arrived):
-    copy = pltpu.make_async_copy(weights_hbm.at[:, pl.ds(0, 3)], staged, arrived)
-    copy.start()
-    copy.wait()
 
 
 def second_kernel(scalars, x1, weights, gain, rest, packed, normed, qkv):
@@ -286,19 +280,6 @@
     )(partial, kept)
 
 
-def run_stage(weights):
-    return pl.pallas_call(
-        stage_kernel,
-        out_shape=jax.ShapeDtypeStruct((CHUNKS, 3, HD, HD), BF),
-        in_specs=[pl.BlockSpec(memory_space=pltpu.HBM)],
-        out_specs=VMEM,
-        scratch_shapes=[pltpu.SemaphoreType.DMA],
-        compiler_params=pltpu.CompilerParams(vmem_limit_bytes=20 << 20),
-        cost_estimate=cost(0, 3_000_000),
-        name="stage",
-    )(weights)
-
-
 def run_second(scalars, x1, weights, gain, rest):
     return pl.pallas_call(
         second_kernel,
@@ -329,15 +310,13 @@
     plane_lengths = jnp.max(regrouped[:, 0, 0, 30].astype(F32), axis=1).astype(jnp.int32)
     my_lengths = lax.dynamic_slice_in_dim(plane_lengths, 2 * core, 2, 0)
 
-    def shard(layer):
-        rows = regrouped[:, layer, :, :30].transpose(1, 0, 2, 3).reshape(4, HD, HD)
-        return jnp.concatenate([rows[:3].transpose(0, 2, 1), rows[3:]], axis=0)
-
-    first_shard = lax.dynamic_slice_in_dim(shard(0), 2 * core, 2, 0)
-    first_shard, second_shard, my_lengths = lax.optimization_barrier(
-        (first_shard, shard(1), my_lengths)
-    )
-    second_weights = lax.all_gather(second_shard, "z", axis=0)
+    rows = regrouped[:, 0, :, :30].transpose(1, 0, 2, 3).reshape(4, HD, HD)
+    rows = jnp.concatenate([rows[:3].transpose(0, 2, 1), rows[3:]], axis=0)
+    first_shard = lax.dynamic_slice_in_dim(rows, 2 * core, 2, 0)
+    gathered = lax.all_gather(regrouped[:, 1], "z", axis=0)[:, :, :, :30]
+    gathered = gathered.transpose(0, 2, 1, 3, 4).reshape(CHUNKS, 4, HD, HD)
+    second_qkv = gathered[:, :3].transpose(0, 1, 3, 2)
+    second_out = gathered[:, 3]
     own = lax.all_gather(first_shard, "z", axis=0)
     other = swap_cores(own)
 
@@ -362,8 +341,7 @@
     share = valid.astype(F32) / my_lengths.astype(F32)[:, None]
     pooled_x1 = jnp.sum(x1_own.reshape(HD, 2, 128).astype(F32) * share, axis=2).T
     center_own = lax.dynamic_index_in_dim(center.reshape(CHUNKS, HD), chunk, 0, keepdims=False)
-    staged = run_stage(second_weights)
-    packed = run_second(scalars, x1, staged, gains[1], pooled_x1 - center_own)
+    packed = run_second(scalars, x1, second_qkv, gains[1], pooled_x1 - center_own)
 
     white_cols = jnp.stack(
         [jnp.where(core == 0, white, white_near), jnp.where(core == 0, white_near, white_far)]
@@ -371,7 +349,7 @@
     out_white = jnp.einsum(
         "ybnc,bcr->ynr",
         white_cols,
-        second_weights[:, 3].astype(F32),
+        second_out.astype(F32),
         precision=lax.Precision.HIGHEST,
     )
     white_own = lax.dynamic_index_in_dim(white_cols, chunk, 1, keepdims=False)

time: 168 us -> 176 us (1.048)
  local copies, waits for them, and re-layouts: 3.66 us -> 8.56 us
  waiting for transfers between devices: 35.4 us -> 31.1 us
  starting transfers between devices: 42.1 us -> 46 us
  blocking collectives: 53.3 us -> 56.8 us
    all_to_all x1, waiting for transfers between devices: 9.82 us -> 0.12 us  [body(): partial = lax.all_to_all(partial, ('x', 'y'), 0, 0)]
    ppermute x1, waiting for transfers between devices: 0.01 us -> 9.63 us  [body(): white_near = lax.ppermute(white, ('y', 'c'), near)]
    all_to_all x1, waiting for transfers between devices: 8.51 us -> 4.46 us  [body(): x1 = lax.all_to_all(spread, ('x', 'y'), 0, 0)]
    all_gather x1, blocking collectives: 40.1 us -> 43.7 us  [body(): own = lax.all_gather(first_shard, 'z', axis=0)]
    transpose x1 -> x3, local copies, waits for them, and re-layouts: 0.02 us -> 3.38 us  [the longest x2 3.37 us: body(): gathered = gathered.transpose(0, 2, 1, 3, 4).reshape(CHUNKS, 4, HD, HD)]
    all_to_all x1, starting transfers between devices: 5.31 us -> 7.37 us  [body(): x1 = lax.all_to_all(spread, ('x', 'y'), 0, 0)]
    slice x11 -> x10, local copies, waits for them, and re-layouts: 0.4 us -> 2.28 us  [the longest x1 1.37 us: body(): second_qkv = gathered[:, :3].transpose(0, 1, 3, 2)]
  transfers between devices with their start and end apart: 10 -> 10, of which waited for: 5 -> 5; matrix products, arithmetic and copies ran while one was open for 2% -> 5% of each run, Pallas kernels for 8% -> 8%
where the time goes in v13:
time: 176 us; the launch traced here: 174 us
  blocking collectives  56.8 us (32%)
  starting transfers between devices  46 us (26%)
  waiting for transfers between devices  31.1 us (18%)
  Pallas kernels  15.1 us (9%)
  between operations  14.4 us (8%)
  local copies, waits for them, and re-layouts  8.56 us (5%)
    all_gather x1, blocking collectives, body(): own = lax.all_gather(first_shard, 'z', axis=0)  43.7 us
    all_to_all x1, waiting for transfers between devices, body(): packed = lax.all_to_all(packed, ('z', 'c'), 0, 0).reshape(64, 2 * HD)  14.3 us
    all_to_all x1, blocking collectives, body(): part = lax.all_to_all(part, ('y', 'x'), 0, 0)  10.9 us
    ppermute x1, waiting for transfers between devices, body(): white_near = lax.ppermute(white, ('y', 'c'), near)  9.63 us
    all_to_all x1, starting transfers between devices, body(): packed = lax.all_to_all(packed, ('z', 'c'), 0, 0).reshape(64, 2 * HD)  9.36 us
    all_to_all x1, starting transfers between devices, body(): lax.all_to_all(projected, ('x', 'y'), 0, 0).reshape(4, NY, NY, HD, 128)  8.31 us
    all_to_all x1, starting transfers between devices, body(): partial = lax.all_to_all(partial, ('x', 'y'), 0, 0)  7.38 us
    all_to_all x1, starting transfers between devices, body(): x1 = lax.all_to_all(spread, ('x', 'y'), 0, 0)  7.37 us
  transfers between devices with their start and end apart: 10, of which 5 were waited for; matrix products, arithmetic and copies ran while one was open for 5% of the time, Pallas kernels for 8%

profile of v13, /device:TPU:6, one launch (start us, length us, event | category | flops | bytes accessed | tf_op | source)
XLA Modules:
  0.0 174.2 jit_solution(14034412479249238476)
XLA Ops:
  7.2 1.7 %regroup.1 = bf16[8,4,32,120]{3,2,1,0:T(8,128)(2,1)} custom-call(s32[1,1]{1,0:T(1,128)} %bitcast.69.lengths, bf16[30,1440]{1,0:T(8,128)(2,1)} %bitcast.90, bf16[30,480]{1,0:T(8,128)(2,1)} %bitcast.92), custom_call_target="tpu_custom_call" | custom-call | bytes 400000 | tf_op jit(solution)/shard_map/regroup/pallas_call | solution.py:194
  8.9 4.5 %all-to-all-start = ((bf16[8,4,32,120]{3,2,1,0:T(8,128)(2,1)}), bf16[8,4,32,120]{3,2,1,0:T(8,128)(2,1)S(1)}, u32[]{:S(2)}, u32[]{:S(2)}) async-start(bf16[8,4,32,120]{3,2,1,0:T(8,128)(2,1)} %regroup.1), calls=%async_computation | async-start | bytes 524288 | tf_op jit(solution)/shard_map/all_to_all | solution.py:307
  13.5 2.2 %all-gather.2 = f32[2,1,1920]{2,1,0:T(1,128)S(1)} all-gather(f32[1,1,1920]{2,1,0:T(1,128)} %bitcast.93), channel_id=1, replica_groups=mesh['z'=16,'y'=4,'c'=2,'x'=4] {'c'}, dimensions={0}, use_global_device_ids=true | all-gather | bytes 23040 | tf_op jit(solution)/shard_map/all_gather | solution.py:308
  15.6 2.7 %layer_input.1 = bf16[16,4,120,128]{3,2,1,0:T(8,128)(2,1)} custom-call(bf16[480,512]{1,0:T(8,128)(2,1)} %bitcast.85, bf16[128,512]{1,0:T(8,128)(2,1)} %bitcast.88), custom_call_target="tpu_custom_call" | custom-call | flops 100000000 | bytes 3000000 | tf_op jit(solution)/shard_map/layer_input/pallas_call | solution.py:210
  18.4 2.6 %all-to-all-done = bf16[8,4,32,120]{3,2,1,0:T(8,128)(2,1)S(1)} async-done(((bf16[8,4,32,120]{3,2,1,0:T(8,128)(2,1)}), bf16[8,4,32,120]{3,2,1,0:T(8,128)(2,1)S(1)}, u32[]{:S(2)}, u32[]{:S(2)}) %all-to-all-start) | async-done | bytes 245792 | tf_op jit(solution)/shard_map/all_to_all | solution.py:307
  21.0 0.7 slice.57
  21.6 8.3 %all-to-all-start.1 = ((bf16[16,4,120,128]{3,2,1,0:T(8,128)(2,1)}), bf16[16,4,120,128]{3,2,1,0:T(8,128)(2,1)S(1)}, u32[]{:S(2)}, u32[]{:S(2)}) async-start(bf16[16,4,120,128]{3,2,1,0:T(8,128)(2,1)} %layer_input.1), calls=%async_computation.1 | async-start | bytes 3932160 | tf_op jit(solution)/shard_map/all_to_all | solution.py:323
  30.4 43.7 %all-gather = bf16[32,120,120]{2,1,0:T(8,128)(2,1)S(1)} all-gather(bf16[2,120,120]{2,1,0:T(8,128)(2,1)S(1)} %copy.32), channel_id=2, replica_groups=mesh['z'=16,'y'=4,'c'=2,'x'=4] {'z'}, dimensions={0}, use_global_device_ids=true | all-gather | bytes 979200 | tf_op jit(solution)/shard_map/all_gather | solution.py:320
  74.1 1.9 %collective-permute-start = (bf16[16,2,120,120]{3,2,1,0:T(8,128)(2,1)S(1)}, bf16[16,2,120,120]{3,2,1,0:T(8,128)(2,1)}, u32[]{:S(2)}, u32[]{:S(2)}) collective-permute-start(bf16[16,2,120,120]{3,2,1,0:T(8,128)(2,1)S(1)} %bitcast.72), channel_id=1, source_target_pairs={{0,4},{4,0},{1,5},{5,1},{2,6},{6,2},{3,7},{7,3},{8,12},{12,8},{9,1... | collective-permute-start | bytes 2764808 | tf_op jit(solution)/shard_map/ppermute | solution.py:18
  76.4 2.2 %first_norm.1 = (bf16[16,120,256]{2,1,0:T(8,128)(2,1)S(1)}, bf16[2,120,256]{2,1,0:T(8,128)(2,1)S(1)}) custom-call(s32[5]{0:T(128)S(1)} %pad_add_fusion.scalars, bf16[4,4,4,120,128]{4,3,2,1,0:T(8,128)(2,1)S(1)} %bitcast.70, bf16[16,2,120,120]{3,2,1,0:T(8,128)(2,1)S(1)} %bitcast.73, f32[16,120]{1,0:T(8,128)S(1)} %squeeze.38.gain), custom_call_target="tpu_custom_call" | custom-call | flops 400000000 | bytes 4000000 | tf_op jit(solution)/shard_map/first_norm/pallas_call | solution.py:232
  78.6 3.6 %first_attend.1 = (bf16[16,120,256]{2,1,0:T(8,128)(2,1)}, bf16[120,256]{1,0:T(8,128)(2,1)S(1)}) custom-call(s32[5]{0:T(128)S(1)} %pad_add_fusion.scalars, bf16[4,4,4,120,128]{4,3,2,1,0:T(8,128)(2,1)S(1)} %bitcast.71, bf16[16,120,256]{2,1,0:T(8,128)(2,1)S(1)} %get-tuple-element.19.normed, bf16[2,120,256]{2,1,0:T(8,128)(2,1)S(1)} %get-tuple-element.20.mine, ...), custom_call_target="tpu_custom_call" | custom-call | flops 600000000 | bytes 5000000 | tf_op jit(solution)/shard_map/first_attend/pallas_call | solution.py:247
  82.3 7.4 %all-to-all-start.2 = ((bf16[16,120,256]{2,1,0:T(8,128)(2,1)}), bf16[16,120,256]{2,1,0:T(8,128)(2,1)S(1)}, u32[]{:S(2)}, u32[]{:S(2)}) async-start(bf16[16,120,256]{2,1,0:T(8,128)(2,1)} %get-tuple-element.23), calls=%async_computation.2 | async-start | bytes 1966080 | tf_op jit(solution)/shard_map/all_to_all | solution.py:336
  89.7 0.2 reshape.78
  90.1 4.6 %collective-permute-start.1 = (f32[16,16,120]{2,1,0:T(8,128)S(1)}, f32[16,16,120]{2,1,0:T(8,128)S(1)}, u32[]{:S(2)}, u32[]{:S(2)}) collective-permute-start(f32[16,16,120]{2,1,0:T(8,128)S(1)} %bitcast.82), channel_id=1, source_target_pairs={{8,0},{20,4},{16,8},{28,12},{24,16},{4,20},{0,24},{12,28},{9,1},{2... | collective-permute-start | bytes 368648 | tf_op jit(solution)/shard_map/ppermute | solution.py:333
  94.7 0.7 collective-permute-start.2
  95.4 9.6 %collective-permute-done.1 = f32[16,16,120]{2,1,0:T(8,128)S(1)} collective-permute-done((f32[16,16,120]{2,1,0:T(8,128)S(1)}, f32[16,16,120]{2,1,0:T(8,128)S(1)}, u32[]{:S(2)}, u32[]{:S(2)}) %collective-permute-start.1) | collective-permute-done | bytes 122912 | tf_op jit(solution)/shard_map/ppermute | solution.py:333
  105.2 1.2 combine.1
  106.6 7.4 %all-to-all-start.3 = ((bf16[16,120,256]{2,1,0:T(8,128)(2,1)}), bf16[16,120,256]{2,1,0:T(8,128)(2,1)S(1)}, u32[]{:S(2)}, u32[]{:S(2)}) async-start(bf16[16,120,256]{2,1,0:T(8,128)(2,1)} %get-tuple-element.25), calls=%async_computation.3 | async-start | bytes 1966080 | tf_op jit(solution)/shard_map/all_to_all | solution.py:338
  113.9 0.2 multiply_reduce_fusion
  114.2 2.1 %slice_bitcast_fusion = bf16[16,4,4,30,120]{4,3,1,2,0:T(8,128)(2,1)S(1)} fusion(bf16[16,4,4,32,120]{4,3,2,1,0:T(8,128)(2,1)} %bitcast.78), kind=kLoop, calls=%fused_computation | loop fusion | bytes 3686400 | tf_op jit(solution)/shard_map/transpose | solution.py:317
  116.3 1.3 copy.34
  117.6 1.4 slice.70
  119.0 2.0 %copy.43 = bf16[16,3,120,120]{2,3,1,0:T(8,128)(2,1)S(1)} copy(bf16[16,3,120,120]{3,0,2,1:T(8,128)(2,1)} %slice.70) | data formatting | bytes 2764800
  121.0 0.5 convolution_bitcast_fusion.1
  121.6 1.9 %collective-permute-start.3 = (f32[2,16,240]{2,1,0:T(8,128)S(1)}, f32[2,16,240]{2,1,0:T(8,128)S(1)}, u32[]{:S(2)}, u32[]{:S(2)}) collective-permute-start(f32[2,16,240]{2,1,0:T(8,128)S(1)} %pad_maximum_fusion.2), channel_id=1, source_target_pairs={{0,4},{4,0},{1,5},{5,1},{2,6},{6,2},{3,7},{7,3},{8,12},{12,8},{9,1... | collective-permute-start | bytes 92168 | tf_op jit(solution)/shard_map/ppermute | solution.py:18
  123.6 4.5 %all-to-all-done.3.x1 = bf16[16,120,256]{2,1,0:T(8,128)(2,1)S(1)} async-done(((bf16[16,120,256]{2,1,0:T(8,128)(2,1)}), bf16[16,120,256]{2,1,0:T(8,128)(2,1)S(1)}, u32[]{:S(2)}, u32[]{:S(2)}) %all-to-all-start.3) | async-done | bytes 983072 | tf_op jit(solution)/shard_map/all_to_all | solution.py:338
  128.0 3.5 %second_layer.1 = f32[32,2,240]{2,1,0:T(2,128)} custom-call(s32[5]{0:T(128)S(1)} %pad_add_fusion.scalars, bf16[16,120,256]{2,1,0:T(8,128)(2,1)S(1)} %all-to-all-done.3.x1, bf16[16,3,120,120]{3,2,1,0:T(8,128)(2,1)S(1)} %bitcast.75, f32[16,120]{1,0:T(8,128)S(1)} %squeeze.41.gain, f32[2,120]{1,0:T(2,128)S(1)} %subtract_bitcast_fusion.rest), custom_call_target="tpu_custom_call" | custom-call | flops 1000000000 | bytes 6000000 | tf_op jit(solution)/shard_map/second_layer/pallas_call | solution.py:284
  131.5 9.4 %all-to-all-start.4 = ((f32[32,2,240]{2,1,0:T(2,128)}), f32[32,2,240]{2,1,0:T(2,128)S(1)}, u32[]{:S(2)}, u32[]{:S(2)}) async-start(f32[32,2,240]{2,1,0:T(2,128)} %second_layer.1), calls=%async_computation.4 | async-start | bytes 131072 | tf_op jit(solution)/shard_map/all_to_all | solution.py:363
  141.0 14.3 %all-to-all-done.4 = f32[32,2,240]{2,1,0:T(2,128)S(1)} async-done(((f32[32,2,240]{2,1,0:T(2,128)}), f32[32,2,240]{2,1,0:T(2,128)S(1)}, u32[]{:S(2)}, u32[]{:S(2)}) %all-to-all-start.4) | async-done | bytes 61472 | tf_op jit(solution)/shard_map/all_to_all | solution.py:363
  155.4 0.2 convolution_bitcast_fusion
  155.7 10.9 %all_to_all.30 = f32[16,8,128]{2,1,0:T(8,128)S(1)} all-to-all(f32[16,8,128]{2,1,0:T(8,128)S(1)} %bitcast.87), channel_id=1, replica_groups=mesh['z'=16,'y'=4,'c'=2,'x'=4] {'y','x'}, dimensions={0} | all-to-all | bytes 131072 | tf_op jit(solution)/shard_map/all_to_all | solution.py:368
  166.7 0.6 maximum_bitcast_fusion.1
  (47 shorter events, 1.9 us)
Async XLA Ops:
  8.9 12.0 %all-to-all-start = ((bf16[8,4,32,120]{3,2,1,0:T(8,128)(2,1)}), bf16[8,4,32,120]{3,2,1,0:T(8,128)(2,1)S(1)}, u32[]{:S(2)}, u32[]{:S(2)}) async-start(bf16[8,4,32,120]{3,2,1,0:T(8,128)(2,1)} %regroup.1), calls=%async_computation | async-start | bytes 524288 | tf_op jit(solution)/shard_map/all_to_all | solution.py:307
  13.4 100.8 %all-gather.5.cloned.1.call-start = ((), (), s32[]{:S(2)}) async-start(), calls=%async_computation.6 | async-start | bytes 2228224 | tf_op jit(solution)/shard_map/all_gather | solution.py:316
  21.6 54.8 %all-to-all-start.1 = ((bf16[16,4,120,128]{3,2,1,0:T(8,128)(2,1)}), bf16[16,4,120,128]{3,2,1,0:T(8,128)(2,1)S(1)}, u32[]{:S(2)}, u32[]{:S(2)}) async-start(bf16[16,4,120,128]{3,2,1,0:T(8,128)(2,1)} %layer_input.1), calls=%async_computation.1 | async-start | bytes 3932160 | tf_op jit(solution)/shard_map/all_to_all | solution.py:323
  74.1 4.6 %collective-permute-start = (bf16[16,2,120,120]{3,2,1,0:T(8,128)(2,1)S(1)}, bf16[16,2,120,120]{3,2,1,0:T(8,128)(2,1)}, u32[]{:S(2)}, u32[]{:S(2)}) collective-permute-start(bf16[16,2,120,120]{3,2,1,0:T(8,128)(2,1)S(1)} %bitcast.72), channel_id=1, source_target_pairs={{0,4},{4,0},{1,5},{5,1},{2,6},{6,2},{3,7},{7,3},{8,12},{12,8},{9,1... | collective-permute-start | bytes 2764808 | tf_op jit(solution)/shard_map/ppermute | solution.py:18
  82.3 7.4 %copy-start = (f32[1920,16]{0,1:T(8,128)S(1)}, f32[1920,16]{0,1:T(8,128)}, u32[]{:S(2)}) copy-start(f32[1920,16]{0,1:T(8,128)} %param.15) | copy-start | bytes 368644
  82.3 7.6 %copy-start.1 = (f32[1920]{0:T(1024)S(1)}, f32[1920]{0:T(1024)}, u32[]{:S(2)}) copy-start(f32[1920]{0:T(1024)} %param.14) | copy-start | bytes 23044
  82.3 23.0 %all-to-all-start.2 = ((bf16[16,120,256]{2,1,0:T(8,128)(2,1)}), bf16[16,120,256]{2,1,0:T(8,128)(2,1)S(1)}, u32[]{:S(2)}, u32[]{:S(2)}) async-start(bf16[16,120,256]{2,1,0:T(8,128)(2,1)} %get-tuple-element.23), calls=%async_computation.2 | async-start | bytes 1966080 | tf_op jit(solution)/shard_map/all_to_all | solution.py:336
  90.1 15.0 %collective-permute-start.1 = (f32[16,16,120]{2,1,0:T(8,128)S(1)}, f32[16,16,120]{2,1,0:T(8,128)S(1)}, u32[]{:S(2)}, u32[]{:S(2)}) collective-permute-start(f32[16,16,120]{2,1,0:T(8,128)S(1)} %bitcast.82), channel_id=1, source_target_pairs={{8,0},{20,4},{16,8},{28,12},{24,16},{4,20},{0,24},{12,28},{9,1},{2... | collective-permute-start | bytes 368648 | tf_op jit(solution)/shard_map/ppermute | solution.py:333
  94.7 10.4 %collective-permute-start.2 = (f32[16,16,120]{2,1,0:T(8,128)S(1)}, f32[16,16,120]{2,1,0:T(8,128)S(1)}, u32[]{:S(2)}, u32[]{:S(2)}) collective-permute-start(f32[16,16,120]{2,1,0:T(8,128)S(1)} %bitcast.83), channel_id=1, source_target_pairs={{28,4},{4,12},{12,20},{20,28},{29,5},{5,13},{13,21},{21,29},{30,6}... | collective-permute-start | bytes 368648 | tf_op jit(solution)/shard_map/ppermute | solution.py:334
  106.6 21.5 %all-to-all-start.3 = ((bf16[16,120,256]{2,1,0:T(8,128)(2,1)}), bf16[16,120,256]{2,1,0:T(8,128)(2,1)S(1)}, u32[]{:S(2)}, u32[]{:S(2)}) async-start(bf16[16,120,256]{2,1,0:T(8,128)(2,1)} %get-tuple-element.25), calls=%async_computation.3 | async-start | bytes 1966080 | tf_op jit(solution)/shard_map/all_to_all | solution.py:338
  121.6 19.3 %collective-permute-start.3 = (f32[2,16,240]{2,1,0:T(8,128)S(1)}, f32[2,16,240]{2,1,0:T(8,128)S(1)}, u32[]{:S(2)}, u32[]{:S(2)}) collective-permute-start(f32[2,16,240]{2,1,0:T(8,128)S(1)} %pad_maximum_fusion.2), channel_id=1, source_target_pairs={{0,4},{4,0},{1,5},{5,1},{2,6},{6,2},{3,7},{7,3},{8,12},{12,8},{9,1... | collective-permute-start | bytes 92168 | tf_op jit(solution)/shard_map/ppermute | solution.py:18
  131.5 23.8 %all-to-all-start.4 = ((f32[32,2,240]{2,1,0:T(2,128)}), f32[32,2,240]{2,1,0:T(2,128)S(1)}, u32[]{:S(2)}, u32[]{:S(2)}) async-start(f32[32,2,240]{2,1,0:T(2,128)} %second_layer.1), calls=%async_computation.4 | async-start | bytes 131072 | tf_op jit(solution)/shard_map/all_to_all | solution.py:363
Sparse Core Ops, SparseCore 0:
  21.8 76.9 all-gather.4
